TPU v7x, 32 devices: a whole 2x2x4 slice. The times are simulated.
32 devices in a mesh: batch: 4 (over y, x), rows: 8 (over z, core).
Axes of the slice: x: 2, y: 2, z: 4, core: 2. Of those that a mesh axis runs over, the one named last changes fastest.
Arguments:
- features: bfloat16 [256, 8, 16, 2048], P('batch', 'rows'), may hold values from -6 to 6
- w_reduce: bfloat16 [2048, 512], P('rows'), may hold values from -0.125 to 0.125
- w_spatial: bfloat16 [4608, 512], P('rows'), may hold values from -0.09375 to 0.09375
- w_expand: bfloat16 [512, 2048], P('rows'), may hold values from -0.25 to 0.25
- query_weight: bfloat16 [2048, 512], P('rows'), may hold values from -0.125 to 0.125
- w_key: bfloat16 [2048, 512], P('rows'), may hold values from -0.125 to 0.125
- w_value: bfloat16 [2048, 512], P('rows'), may hold values from -0.125 to 0.125
- w_out: bfloat16 [512, 2048], P('rows'), may hold values from -0.5 to 0.5
- w_head: bfloat16 [4096, 80], P('rows'), may hold values from -0.09375 to 0.09375
- gain_a: float32 [512], replicated, may hold values from 0.1 to 1.9
- bias_a: float32 [512], replicated, may hold values from -0.5 to 0.5
- gain_b: float32 [512], replicated, may hold values from 0.1 to 1.9
- bias_b: float32 [512], replicated, may hold values from -0.5 to 0.5
- gain_c: float32 [2048], replicated, may hold values from 0.1 to 1.9
- bias_c: float32 [2048], replicated, may hold values from -0.5 to 0.5
- ln_gain: float32 [512], replicated, may hold values from 0.1 to 1.9
- ln_bias: float32 [512], replicated, may hold values from -0.5 to 0.5
- head_bias: float32 [80], replicated, may hold values from -1 to 1
- bank: bfloat16 [320, 2048], P(('batch', 'rows')), may hold values from -6 to 6
- piece_box: int32 [256, 8], P(('batch', 'rows')), may hold values from 0 to 127
- piece_clip: int32 [256, 8], P(('batch', 'rows')), may hold values from 0 to 63
- send_count: int32 [256], P(('batch', 'rows')), may hold values from 0 to 8, as said below
- sample_pos: int32 [256, 224], P(('batch', 'rows')), may hold values from 0 to 15
- sample_weight: float32 [256, 224], P(('batch', 'rows')), may hold values from 0.01 to 0.06
- win_start: int32 [4096], P(('batch', 'rows')), may hold values from 0 to 60, as said below
- win_len: int32 [4096], P(('batch', 'rows')), may hold values from 20 to 40, as said below
- prob_cotangent: float32 [4096, 80], P(('batch', 'rows')), may hold values from -6 to 6
Outputs:
- probs: float32 [4096, 80], P(('batch', 'rows'))
- features_grad: bfloat16 [256, 8, 16, 2048], P('batch', 'rows')
- w_reduce_grad: float32 [2048, 512], P('rows', 'batch')
- w_spatial_grad: float32 [4608, 512], P('rows', 'batch')
- w_expand_grad: float32 [512, 2048], P('rows', 'batch')
- w_query_grad: float32 [2048, 512], P('rows', 'batch')
- w_key_grad: float32 [2048, 512], P('rows', 'batch')
- w_value_grad: float32 [2048, 512], P('rows', 'batch')
- w_out_grad: float32 [512, 2048], P('rows', 'batch')
- w_head_grad: float32 [4096, 80], P('rows', 'batch')
- gain_a_grad: float32 [512], replicated
- bias_a_grad: float32 [512], replicated
- gain_b_grad: float32 [512], replicated
- bias_b_grad: float32 [512], replicated
- gain_c_grad: float32 [2048], replicated
- bias_c_grad: float32 [2048], replicated
- ln_gain_grad: float32 [512], replicated
- ln_bias_grad: float32 [512], replicated
- classifier_bias_gradient: float32 [80], replicated
Inputs may be any that keep to these rules, and one draw needn't show every extreme that they name: `send_count`: at most 8 live slots from one device to one owner; some device sends exactly 8 to some owner in every draw. `win_len`: every window holds 20 to 40 entries, some box's exactly 40. win_start + win_len <= 80.
All inputs are finite; a program needn't handle non-finite values.
Results may differ from a plain program's by a relative error of at most 0.024.
Values may be sent and summed in bfloat16 or wider, within the bound.
A program may use at most 256 MiB of HBM per device.

v0:
```python
import jax
import jax.numpy as jnp
from jax import lax
from jax.sharding import PartitionSpec as P


def padded(cells, sides, width):
    for axis, dim in sides:
        count = lax.axis_size(axis)
        ends = count - 1
        head = lax.slice_in_dim(cells, 0, width, axis=dim)
        tail = lax.slice_in_dim(cells, cells.shape[dim] - width, cells.shape[dim], axis=dim)
        cells = jnp.concatenate(
            [
                lax.ppermute(tail, axis, [(i, (i + 1) % count) for i in range(ends)]),
                cells,
                lax.ppermute(head, axis, [((i + 1) % count, i) for i in range(ends)]),
            ],
            axis=dim,
        )
    return cells


def split_up(value, dim, peers):
    shape = value.shape
    parts = value.reshape(*shape[:dim], peers, shape[dim] // peers, *shape[dim + 1 :])
    return jnp.moveaxis(parts, dim, 0)


def sum_at_owner(value, axis, dim):
    peers = lax.axis_size(axis)
    parts = lax.all_to_all(split_up(value, dim, peers), axis, 0, 0, tiled=True)
    return jnp.sum(parts.astype(jnp.float32), axis=0)


def side_by_side(arrays, axis, dim, along):
    ends, at = ([], 0)
    for a in arrays[:-1]:
        at += a.shape[along]
        ends.append(at)
    both = jnp.concatenate(arrays, axis=along)
    return tuple(jnp.split(sum_at_owner(both, axis, dim), ends, axis=along))


def tdot(left, right):
    return lax.dot_general(
        left, right, (((0,), (0,)), ((), ())), preferred_element_type=jnp.float32
    )


def ndot(left, right):
    return lax.dot_general(
        left, right, (((1,), (1,)), ((), ())), preferred_element_type=jnp.float32
    )


def silu_slope(value):
    sig = jax.nn.sigmoid(value)
    return sig * (1.0 + value * (1.0 - sig))


def normalize(field, total_count):
    sums, squares = lax.psum((jnp.sum(field, 0), jnp.sum(field * field, 0)), ("batch", "rows"))
    centre_value = sums / total_count
    inverse = lax.rsqrt(squares / total_count - centre_value * centre_value + 1e-05)
    return ((field - centre_value) * inverse, inverse)


def segment_totals(grad, normed):
    return lax.psum((jnp.sum(grad, 0), jnp.sum(grad * normed, 0)), ("batch", "rows"))


def norm_back(grad, normed, inverse, gain, shift_sum, gain_total_grad, total_count):
    return (
        gain * inverse * (grad - shift_sum / total_count - normed * gain_total_grad / total_count)
    )


def on_device(
    features,
    w_reduce,
    w_spatial,
    w_expand,
    query_weight,
    w_key,
    w_value,
    w_out,
    w_head,
    gain_a,
    bias_a,
    gain_b,
    bias_b,
    gain_c,
    bias_c,
    ln_gain,
    ln_bias,
    head_bias,
    bank,
    piece_box,
    piece_clip,
    send_count,
    sample_pos,
    sample_weight,
    win_start,
    win_len,
    prob_cotangent,
):
    owners = lax.axis_size("rows")
    clip_dev, row_dev, col_count, d_in = features.shape
    cell_count = clip_dev * row_dev * col_count
    total_count = cell_count * owners * lax.axis_size("batch")
    w_a, w_b, w_c, w_q, w_k, w_v, w_o, w_h = (
        lax.all_gather(w_reduce, "rows", axis=0, tiled=True),
        lax.all_gather(w_spatial, "rows", axis=0, tiled=True),
        lax.all_gather(w_expand, "rows", axis=0, tiled=True),
        lax.all_gather(query_weight, "rows", axis=0, tiled=True),
        lax.all_gather(w_key, "rows", axis=0, tiled=True),
        lax.all_gather(w_value, "rows", axis=0, tiled=True),
        lax.all_gather(w_out, "rows", axis=0, tiled=True),
        lax.all_gather(w_head, "rows", axis=0, tiled=True),
    )
    d_mid = w_a.shape[1]
    flat_x = features.reshape(cell_count, d_in)
    pre_a = jnp.dot(flat_x, w_a, preferred_element_type=jnp.float32)
    hat_a, inverse_a = normalize(pre_a, total_count)
    act_a = gain_a * hat_a + bias_a
    low_a = jax.nn.silu(act_a).astype(jnp.bfloat16)
    halo_a = padded(low_a.reshape(clip_dev, row_dev, col_count, d_mid), (("rows", 1),), 1)
    halo_a = jnp.pad(halo_a, ((0, 0), (0, 0), (1, 1), (0, 0)))
    window_a = jnp.concatenate(
        [
            halo_a[:, row_step : row_step + row_dev, col_step : col_step + col_count]
            for row_step in range(3)
            for col_step in range(3)
        ],
        axis=3,
    ).reshape(cell_count, 9 * d_mid)
    pre_b = jnp.dot(window_a, w_b, preferred_element_type=jnp.float32)
    hat_b, inverse_b = normalize(pre_b, total_count)
    act_b = gain_b * hat_b + bias_b
    low_b = jax.nn.silu(act_b).astype(jnp.bfloat16)
    pre_c = jnp.dot(low_b, w_c, preferred_element_type=jnp.float32)
    hat_c, inverse_c = normalize(pre_c, total_count)
    pre_out = gain_c * hat_c + bias_c + flat_x.astype(jnp.float32)
    fmap = jax.nn.silu(pre_out).astype(jnp.bfloat16)
    capacity = piece_box.shape[1]
    samples = sample_pos.shape[1] // capacity
    slot_count = owners * capacity
    sample_cells = (
        piece_clip[:, :, None] * (row_dev * col_count)
        + sample_pos.reshape(owners, capacity, samples)
    ).reshape(slot_count, samples)
    is_live = (jnp.arange(capacity)[None, :] < send_count[:, None]).reshape(slot_count)
    slot_weights = sample_weight.reshape(slot_count, samples) * is_live[:, None].astype(jnp.float32)
    cell_ids = jnp.arange(cell_count)[None, :]
    interp_sum = jnp.zeros((slot_count, cell_count), jnp.float32)
    for sample_index in range(samples):
        interp_sum = interp_sum + jnp.where(
            sample_cells[:, sample_index, None] == cell_ids,
            slot_weights[:, sample_index, None],
            0.0,
        )
    interpolated_value = interp_sum.astype(jnp.bfloat16)
    region_parts = (
        jnp.dot(interpolated_value, fmap, preferred_element_type=jnp.float32)
        .astype(jnp.bfloat16)
        .reshape(owners, capacity, d_in)
    )
    arrived, arrived_box = (
        lax.all_to_all(region_parts, "rows", split_axis=0, concat_axis=0, tiled=True),
        lax.all_to_all(piece_box, "rows", split_axis=0, concat_axis=0, tiled=True),
    )
    box_dev = win_start.shape[0]
    flat_box = arrived_box.reshape(slot_count)
    owner_hits = (flat_box[None, :] == jnp.arange(box_dev)[:, None]).astype(jnp.bfloat16)
    pooled = jnp.dot(
        owner_hits, arrived.reshape(slot_count, d_in), preferred_element_type=jnp.float32
    )
    pooled_low = pooled.astype(jnp.bfloat16)
    keys_own = jnp.dot(bank, w_k, preferred_element_type=jnp.float32).astype(jnp.bfloat16)
    values_own = jnp.dot(bank, w_v, preferred_element_type=jnp.float32).astype(jnp.bfloat16)
    key_rows, value_rows = (
        lax.all_gather(keys_own, "rows", axis=0, tiled=True),
        lax.all_gather(values_own, "rows", axis=0, tiled=True),
    )
    bank_length = key_rows.shape[0]
    queries = jnp.dot(pooled_low, w_q, preferred_element_type=jnp.float32).astype(jnp.bfloat16)
    score_scale = d_mid ** (-0.5)
    scores = ndot(queries, key_rows) * score_scale
    positions = jnp.arange(bank_length)[None, :]
    window_mask = (positions >= win_start[:, None]) & (positions < (win_start + win_len)[:, None])
    attend = jax.nn.softmax(jnp.where(window_mask, scores, -1e30), axis=-1)
    attend_low = attend.astype(jnp.bfloat16)
    mixture = jnp.dot(attend_low, value_rows, preferred_element_type=jnp.float32)
    centred = mixture - jnp.mean(mixture, axis=-1, keepdims=True)
    inverse_z = lax.rsqrt(jnp.mean(centred * centred, axis=-1, keepdims=True) + 1e-05)
    hat_z = centred * inverse_z
    pre_ln = ln_gain * hat_z + ln_bias
    low_r = jax.nn.silu(pre_ln).astype(jnp.bfloat16)
    branch = jnp.dot(low_r, w_o, preferred_element_type=jnp.float32)
    joined = jnp.concatenate([pooled, pooled + branch], axis=1).astype(jnp.bfloat16)
    logits = jnp.dot(joined, w_h, preferred_element_type=jnp.float32) + head_bias
    likely = jax.nn.sigmoid(logits)
    d_logit = (prob_cotangent * (likely * (1.0 - likely))).astype(jnp.bfloat16)
    grad_head_bias = jnp.sum(d_logit.astype(jnp.float32), 0)
    grad_wh = tdot(joined, d_logit)
    d_joined = ndot(d_logit, w_h)
    d_pooled = d_joined[:, :d_in] + d_joined[:, d_in:]
    d_branch = d_joined[:, d_in:].astype(jnp.bfloat16)
    grad_wo = tdot(low_r, d_branch)
    d_ln = ndot(d_branch, w_o) * silu_slope(pre_ln)
    grad_ln_gain = jnp.sum(d_ln * hat_z, 0)
    grad_ln_bias = jnp.sum(d_ln, 0)
    d_hat = d_ln * ln_gain
    d_mixture = (
        inverse_z
        * (
            d_hat
            - jnp.mean(d_hat, axis=-1, keepdims=True)
            - hat_z * jnp.mean(d_hat * hat_z, axis=-1, keepdims=True)
        )
    ).astype(jnp.bfloat16)
    d_attend = ndot(d_mixture, value_rows)
    d_values = tdot(attend_low, d_mixture)
    d_scores = (attend * (d_attend - jnp.sum(d_attend * attend, axis=-1, keepdims=True))).astype(
        jnp.bfloat16
    )
    d_queries = (
        jnp.dot(d_scores, key_rows, preferred_element_type=jnp.float32) * score_scale
    ).astype(jnp.bfloat16)
    d_keys = tdot(d_scores, queries) * score_scale
    grad_wq = tdot(pooled_low, d_queries)
    d_pooled = d_pooled + ndot(d_queries, w_q)
    key_sum, value_sum = side_by_side(
        (d_keys.astype(jnp.bfloat16), d_values.astype(jnp.bfloat16)), "rows", 0, 1
    )
    grad_wk = tdot(bank, key_sum.astype(jnp.bfloat16))
    grad_wv = tdot(bank, value_sum.astype(jnp.bfloat16))
    back_pieces = jnp.take(d_pooled.astype(jnp.bfloat16), flat_box, axis=0).reshape(
        owners, capacity, d_in
    )
    returned = lax.all_to_all(back_pieces, "rows", split_axis=0, concat_axis=0, tiled=True)
    d_fmap = tdot(interpolated_value, returned.reshape(slot_count, d_in))
    d_pre = d_fmap * silu_slope(pre_out)
    head_sums = lax.psum(
        (jnp.sum(d_pre, 0), jnp.sum(d_pre * hat_c, 0), grad_ln_gain, grad_ln_bias, grad_head_bias),
        ("batch", "rows"),
    )
    d_c = norm_back(
        d_pre, hat_c, inverse_c, gain_c, head_sums[0], head_sums[1], total_count
    ).astype(jnp.bfloat16)
    grad_wc = tdot(low_b, d_c)
    d_act_b = ndot(d_c, w_c) * silu_slope(act_b)
    shift_b_sum, gain_b_sum = segment_totals(d_act_b, hat_b)
    d_b = norm_back(d_act_b, hat_b, inverse_b, gain_b, shift_b_sum, gain_b_sum, total_count).astype(
        jnp.bfloat16
    )
    grad_wb = tdot(window_a, d_b)
    halo_d = padded(d_b.reshape(clip_dev, row_dev, col_count, d_mid), (("rows", 1),), 1)
    halo_d = jnp.pad(halo_d, ((0, 0), (0, 0), (1, 1), (0, 0)))
    window_d = jnp.concatenate(
        [
            halo_d[
                :, 2 - row_step : 2 - row_step + row_dev, 2 - col_step : 2 - col_step + col_count
            ]
            for row_step in range(3)
            for col_step in range(3)
        ],
        axis=3,
    ).reshape(cell_count, 9 * d_mid)
    flipped = w_b.reshape(9, d_mid, d_mid).transpose(0, 2, 1).reshape(9 * d_mid, d_mid)
    d_act_a = jnp.dot(window_d, flipped, preferred_element_type=jnp.float32) * silu_slope(act_a)
    shift_a_sum, gain_a_sum = segment_totals(d_act_a, hat_a)
    d_a = norm_back(d_act_a, hat_a, inverse_a, gain_a, shift_a_sum, gain_a_sum, total_count).astype(
        jnp.bfloat16
    )
    grad_wa = tdot(flat_x, d_a)
    grad_input = (ndot(d_a, w_a) + d_pre).astype(jnp.bfloat16).reshape(features.shape)
    partial_sums = (
        lax.psum_scatter(grad_wa, "rows", scatter_dimension=0, tiled=True),
        lax.psum_scatter(grad_wb, "rows", scatter_dimension=0, tiled=True),
        lax.psum_scatter(grad_wc, "rows", scatter_dimension=0, tiled=True),
        lax.psum_scatter(grad_wq, "rows", scatter_dimension=0, tiled=True),
        lax.psum_scatter(grad_wk, "rows", scatter_dimension=0, tiled=True),
        lax.psum_scatter(grad_wv, "rows", scatter_dimension=0, tiled=True),
        lax.psum_scatter(grad_wo, "rows", scatter_dimension=0, tiled=True),
        lax.psum_scatter(grad_wh, "rows", scatter_dimension=0, tiled=True),
    )
    finished = (
        lax.psum_scatter(
            partial_sums[0].astype(jnp.bfloat16), "batch", scatter_dimension=1, tiled=True
        ).astype(jnp.float32),
        lax.psum_scatter(
            partial_sums[1].astype(jnp.bfloat16), "batch", scatter_dimension=1, tiled=True
        ).astype(jnp.float32),
        lax.psum_scatter(
            partial_sums[2].astype(jnp.bfloat16), "batch", scatter_dimension=1, tiled=True
        ).astype(jnp.float32),
        lax.psum_scatter(
            partial_sums[3].astype(jnp.bfloat16), "batch", scatter_dimension=1, tiled=True
        ).astype(jnp.float32),
        lax.psum_scatter(
            partial_sums[4].astype(jnp.bfloat16), "batch", scatter_dimension=1, tiled=True
        ).astype(jnp.float32),
        lax.psum_scatter(
            partial_sums[5].astype(jnp.bfloat16), "batch", scatter_dimension=1, tiled=True
        ).astype(jnp.float32),
        lax.psum_scatter(
            partial_sums[6].astype(jnp.bfloat16), "batch", scatter_dimension=1, tiled=True
        ).astype(jnp.float32),
        lax.psum_scatter(
            partial_sums[7].astype(jnp.bfloat16), "batch", scatter_dimension=1, tiled=True
        ).astype(jnp.float32),
    )
    return (
        likely,
        grad_input,
        finished[0],
        finished[1],
        finished[2],
        finished[3],
        finished[4],
        finished[5],
        finished[6],
        finished[7],
        gain_a_sum,
        shift_a_sum,
        gain_b_sum,
        shift_b_sum,
        head_sums[1],
        head_sums[0],
        head_sums[2],
        head_sums[3],
        head_sums[4],
    )


def solution(mesh):
    return jax.shard_map(
        on_device,
        mesh=mesh,
        in_specs=(
            P("batch", "rows", None, None),
            P("rows", None),
            P("rows", None),
            P("rows", None),
            P("rows", None),
            P("rows", None),
            P("rows", None),
            P("rows", None),
            P("rows", None),
            P(),
            P(),
            P(),
            P(),
            P(),
            P(),
            P(),
            P(),
            P(),
            P(("batch", "rows"), None),
            P(("batch", "rows"), None),
            P(("batch", "rows"), None),
            P(("batch", "rows")),
            P(("batch", "rows"), None),
            P(("batch", "rows"), None),
            P(("batch", "rows")),
            P(("batch", "rows")),
            P(("batch", "rows"), None),
        ),
        out_specs=(
            P(("batch", "rows"), None),
            P("batch", "rows", None, None),
            P("rows", "batch"),
            P("rows", "batch"),
            P("rows", "batch"),
            P("rows", "batch"),
            P("rows", "batch"),
            P("rows", "batch"),
            P("rows", "batch"),
            P("rows", "batch"),
            P(),
            P(),
            P(),
            P(),
            P(),
            P(),
            P(),
            P(),
            P(),
        ),
        check_vma=False,
    )
```

profile of v0, /device:TPU:0, one launch (start us, length us, event | category | flops | bytes accessed | tf_op | source)
XLA Modules:
  0.0 1011.4 jit_solution(11663919438469440399)
XLA Ops:
  19.9 21.7 %all-gather.10.cloned.1.call-done = bf16[2048,512]{1,0:T(8,128)(2,1)} async-done(((bf16[256,512]{1,0:T(8,128)(2,1)}), bf16[2048,512]{1,0:T(8,128)(2,1)}) %all-gather.10.cloned.1.call-update) | async-done | bytes 2097168 | tf_op jit(solution)/shard_map/all_gather | solution.py:113
  46.9 42.2 %all-reduce.8 = (f32[512]{0:T(512)S(1)}, f32[512]{0:T(512)S(1)}) all-reduce(f32[512]{0:T(512)S(1)} %get-tuple-element.106, f32[512]{0:T(512)S(1)} %get-tuple-element.105), channel_id=1, replica_groups=mesh['batch'=4,'rows'=8] {'batch','rows'}, use_global_device_ids=true, to_apply=%region_3.0 | all-reduce | flops 1024 | bytes 8192 | tf_op jit(solution)/shard_map/psum | solution.py:63
  97.0 39.7 %all_gather.39 = bf16[4096,80]{0,1:T(8,128)(2,1)} all-gather(bf16[512,80]{0,1:T(8,128)(2,1)S(1)} %copy-done.8), channel_id=1, replica_groups=mesh['batch'=4,'rows'=8] {'rows'}, dimensions={0}, use_global_device_ids=true | all-gather | bytes 737280 | tf_op jit(solution)/shard_map/all_gather | solution.py:120
  167.2 41.5 %all-reduce.7 = (f32[512]{0:T(512)S(1)}, f32[512]{0:T(512)S(1)}) all-reduce(f32[512]{0:T(512)S(1)} %get-tuple-element.104, f32[512]{0:T(512)S(1)} %get-tuple-element.103), channel_id=1, replica_groups=mesh['batch'=4,'rows'=8] {'batch','rows'}, use_global_device_ids=true, to_apply=%region_7.8 | all-reduce | flops 1024 | bytes 8192 | tf_op jit(solution)/shard_map/psum | solution.py:63
  217.0 42.3 %all-reduce.6 = (f32[2048]{0:T(1024)S(1)}, f32[2048]{0:T(1024)S(1)}) all-reduce(f32[2048]{0:T(1024)S(1)} %get-tuple-element.98, f32[2048]{0:T(1024)S(1)} %get-tuple-element.97), channel_id=1, replica_groups=mesh['batch'=4,'rows'=8] {'batch','rows'}, use_global_device_ids=true, to_apply=%region_11.12 | all-reduce | flops 4096 | bytes 32768 | tf_op jit(solution)/shard_map/psum | solution.py:63
  275.5 15.3 %all-gather = bf16[8,10,512]{2,1,0:T(8,128)(2,1)S(1)} all-gather(bf16[1,10,512]{2,1,0:T(8,128)(2,1)S(1)} %fusion.14), channel_id=1, replica_groups=mesh['batch'=4,'rows'=8] {'rows'}, dimensions={0}, use_global_device_ids=true | all-gather | bytes 92160 | tf_op jit(solution)/shard_map/all_gather | solution.py:183
  292.9 14.4 %all-gather.1 = bf16[8,10,512]{2,1,0:T(8,128)(2,1)S(1)} all-gather(bf16[1,10,512]{2,1,0:T(8,128)(2,1)S(1)} %fusion.15), channel_id=1, replica_groups=mesh['batch'=4,'rows'=8] {'rows'}, dimensions={0}, use_global_device_ids=true | all-gather | bytes 92160 | tf_op jit(solution)/shard_map/all_gather | solution.py:184
  332.2 16.3 %all_to_all.24 = bf16[8,10,1024]{2,1,0:T(8,128)(2,1)S(1)} all-to-all(bf16[8,10,1024]{2,1,0:T(8,128)(2,1)S(1)} %reshape.231), channel_id=1, replica_groups=mesh['batch'=4,'rows'=8] {'rows'}, dimensions={0} | all-to-all | bytes 327680 | tf_op jit(solution)/shard_map/all_to_all | solution.py:32
  358.5 17.0 %all_to_all.25 = bf16[8,8,2048]{2,1,0:T(8,128)(2,1)S(1)} all-to-all(bf16[8,8,2048]{2,1,0:T(8,128)(2,1)S(1)} %bitcast_select_fusion), channel_id=1, replica_groups=mesh['batch'=4,'rows'=8] {'rows'}, dimensions={0} | all-to-all | bytes 524288 | tf_op jit(solution)/shard_map/all_to_all | solution.py:242
  375.9 14.8 %fusion.44 = (f32[2048]{0:T(1024)S(1)}, f32[2048]{0:T(1024)S(1)}, f32[1024,2048]{1,0:T(8,128)}) fusion(f32[2048]{0:T(1024)S(1)} %get-tuple-element.197, f32[1024,2048]{1,0:T(8,128)} %get-tuple-element.207, f32[2048]{0:T(1024)S(1)} %get-tuple-element.198, bf16[1024,2048]{1,0:T(8,128)(2,1)} %bitcast.111, f32[2048]{0:T(1024)} %param.41, ...), kind=kOutput, calls=%fused_computation.235 | convolution fusion | flops 309587968 | bytes 21297152 | tf_op jit(solution)/shard_map/dot_general | solution.py:46
  390.7 38.9 %all-reduce.5 = (f32[2048]{0:T(1024)S(1)}, f32[2048]{0:T(1024)S(1)}) all-reduce(f32[2048]{0:T(1024)S(1)} %get-tuple-element.96, f32[2048]{0:T(1024)S(1)} %get-tuple-element.95), channel_id=1, replica_groups=mesh['batch'=4,'rows'=8] {'batch','rows'}, use_global_device_ids=true, to_apply=%region_22.23 | all-reduce | flops 4096 | bytes 32768 | tf_op jit(solution)/shard_map/psum | solution.py:245
  452.1 42.8 %all-reduce.4 = (f32[512]{0:T(512)S(1)}, f32[512]{0:T(512)S(1)}) all-reduce(f32[512]{0:T(512)S(1)} %get-tuple-element.102, f32[512]{0:T(512)S(1)} %get-tuple-element.101), channel_id=1, replica_groups=mesh['batch'=4,'rows'=8] {'batch','rows'}, use_global_device_ids=true, to_apply=%region_26.27 | all-reduce | flops 1024 | bytes 8192 | tf_op jit(solution)/shard_map/psum | solution.py:70
  525.2 53.3 %all-reduce.3 = (f32[512]{0:T(512)S(1)}, f32[512]{0:T(512)S(1)}, f32[512]{0:T(512)}, f32[512]{0:T(512)}, f32[80]{0:T(128)}) all-reduce(f32[512]{0:T(512)S(1)} %get-tuple-element.100, f32[512]{0:T(512)S(1)} %get-tuple-element.99, f32[512]{0:T(512)S(1)} %copy-done.28, ...), channel_id=1, replica_groups=mesh['batch'=4,'rows'=8] {'batch','rows'}, use_global_device_ids=true, to_apply=%region_30.31 | all-reduce | flops 2128 | bytes 17024 | tf_op jit(solution)/shard_map/psum | solution.py:70
  586.3 11.4 %fusion.57 = f32[4608,512]{1,0:T(8,128)} fusion(bf16[1024,4608]{1,0:T(8,128)(2,1)} %constant_dynamic-update-slice_fusion, bf16[1024,512]{1,0:T(8,128)(2,1)S(1)} %multiply_convert_fusion.8), kind=kOutput, calls=%fused_computation.247 | convolution fusion | flops 4831838208 | bytes 19922944 | tf_op jit(solution)/shard_map/dot_general | solution.py:46
  619.5 49.1 %reduce-scatter.20.cloned.1.call-done = f32[256,512]{0,1:T(8,128)} async-done(((f32[2048,512]{0,1:T(8,128)}), f32[256,512]{0,1:T(8,128)}) %reduce-scatter.20.cloned.1.call-update) | async-done | bytes 524304 | tf_op jit(solution)/shard_map/reduce_scatter | solution.py:280
  670.4 98.0 %reduce-scatter.24.cloned.1.call-done = f32[576,512]{1,0:T(8,128)} async-done(((f32[4608,512]{1,0:T(8,128)}), f32[576,512]{1,0:T(8,128)}) %reduce-scatter.24.cloned.1.call-update) | async-done | bytes 1179664 | tf_op jit(solution)/shard_map/reduce_scatter | solution.py:281
  780.7 30.6 %all-reduce.11.cloned.1.call-done = bf16[512,80]{0,1:T(8,128)(2,1)} async-done(((bf16[512,80]{0,1:T(8,128)(2,1)}), bf16[512,80]{0,1:T(8,128)(2,1)}) %all-reduce.11.cloned.1.call-update) | async-done | bytes 81936
  812.6 26.3 %reduce-scatter.48.cloned.1.call-done = bf16[128,256]{1,0:T(8,128)(2,1)} async-done(((bf16[512,256]{1,0:T(8,128)(2,1)}), bf16[128,256]{1,0:T(8,128)(2,1)}) %reduce-scatter.48.cloned.1.call-update) | async-done | bytes 65552
  840.5 25.1 %reduce-scatter.42.cloned.1.call-done = bf16[64,512]{1,0:T(8,128)(2,1)} async-done(((bf16[64,2048]{1,0:T(8,128)(2,1)}), bf16[64,512]{1,0:T(8,128)(2,1)}) %reduce-scatter.42.cloned.1.call-update) | async-done | bytes 65552 | tf_op jit(solution)/shard_map/reduce_scatter | solution.py:308
  867.2 25.6 %reduce-scatter.34.cloned.1.call-done = bf16[256,128]{0,1:T(8,128)(2,1)} async-done(((bf16[256,512]{0,1:T(8,128)(2,1)}), bf16[256,128]{0,1:T(8,128)(2,1)}) %reduce-scatter.34.cloned.1.call-update) | async-done | bytes 65552 | tf_op jit(solution)/shard_map/reduce_scatter | solution.py:302
  894.4 25.1 %reduce-scatter.38.cloned.1.call-done = bf16[256,128]{0,1:T(8,128)(2,1)} async-done(((bf16[256,512]{0,1:T(8,128)(2,1)}), bf16[256,128]{0,1:T(8,128)(2,1)}) %reduce-scatter.38.cloned.1.call-update) | async-done | bytes 65552 | tf_op jit(solution)/shard_map/reduce_scatter | solution.py:305
  921.1 25.5 %reduce-scatter.28.cloned.1.call-done = bf16[64,512]{1,0:T(8,128)(2,1)} async-done(((bf16[64,2048]{1,0:T(8,128)(2,1)}), bf16[64,512]{1,0:T(8,128)(2,1)}) %reduce-scatter.28.cloned.1.call-update) | async-done | bytes 65552 | tf_op jit(solution)/shard_map/reduce_scatter | solution.py:296
  948.1 26.0 %reduce-scatter.22.cloned.1.call-done = bf16[256,128]{0,1:T(8,128)(2,1)} async-done(((bf16[256,512]{0,1:T(8,128)(2,1)}), bf16[256,128]{0,1:T(8,128)(2,1)}) %reduce-scatter.22.cloned.1.call-update) | async-done | bytes 65552 | tf_op jit(solution)/shard_map/reduce_scatter | solution.py:290
  975.6 27.0 %reduce-scatter.46.cloned.1.call-done = bf16[128,576]{1,0:T(8,128)(2,1)} async-done(((bf16[512,576]{1,0:T(8,128)(2,1)}), bf16[128,576]{1,0:T(8,128)(2,1)}) %reduce-scatter.46.cloned.1.call-update) | async-done | bytes 147472
  (436 shorter events, 224.3 us)
Async XLA Ops:
  7.9 149.2 %all-gather.12.cloned.1.call-start = ((), (), s32[]{:S(2)}) async-start(), calls=%async_computation.20 | async-start | bytes 5308416 | tf_op jit(solution)/shard_map/all_gather | solution.py:114
  8.7 200.1 %all-gather.14.cloned.1.call-start = ((), (), s32[]{:S(2)}) async-start(), calls=%async_computation.21 | async-start | bytes 2359296 | tf_op jit(solution)/shard_map/all_gather | solution.py:115
  9.4 264.1 %all-gather.18.cloned.1.call-start = ((), (), s32[]{:S(2)}) async-start(), calls=%async_computation.23 | async-start | bytes 2359296 | tf_op jit(solution)/shard_map/all_gather | solution.py:117
  10.0 280.9 %all-gather.20.cloned.1.call-start = ((), (), s32[]{:S(2)}) async-start(), calls=%async_computation.24 | async-start | bytes 2359296 | tf_op jit(solution)/shard_map/all_gather | solution.py:118
  10.6 298.0 %all-gather.16.cloned.1.call-start = ((), (), s32[]{:S(2)}) async-start(), calls=%async_computation.22 | async-start | bytes 2359296 | tf_op jit(solution)/shard_map/all_gather | solution.py:116
  11.2 126.1 %all-to-all-start = ((s32[8,1,8]{2,1,0:T(1,128)}), s32[8,1,8]{2,1,0:T(1,128)S(1)}, u32[]{:S(2)}, u32[]{:S(2)}) async-start(s32[8,1,8]{2,1,0:T(1,128)} %bitcast.138), calls=%async_computation | async-start | bytes 8192 | tf_op jit(solution)/shard_map/all_to_all | solution.py:171
  17.5 293.9 %all-gather.22.cloned.1.call-start = ((), (), s32[]{:S(2)}) async-start(), calls=%async_computation.25 | async-start | bytes 2359296 | tf_op jit(solution)/shard_map/all_gather | solution.py:119
  89.8 48.7 %collective-permute-start = (bf16[64,1,16,512]{3,2,0,1:T(8,128)(2,1)S(1)}, bf16[64,1,16,512]{3,2,0,1:T(8,128)(2,1)}, u32[]{:S(2)}, u32[]{:S(2)}) collective-permute-start(bf16[64,1,16,512]{3,2,0,1:T(8,128)(2,1)S(1)} %bitcast.117), channel_id=1, source_target_pairs={{0,1},{1,2},{2,3},{3,4},{4,5},{5,6},{6,7},{8,9},{9,10},{10,11},{11... | collective-permute-start | bytes 3145736 | tf_op jit(solution)/shard_map/ppermute | solution.py:15
  273.5 324.3 %reduce-scatter.44.cloned.1.call-start = ((), (), s32[]{:S(2)}) async-start(), calls=%async_computation.38 | async-start | bytes 1474560 | tf_op jit(solution)/shard_map/reduce_scatter | solution.py:287
  318.1 281.4 %reduce-scatter.30.cloned.1.call-start = ((), (), s32[]{:S(2)}) async-start(), calls=%async_computation.31 | async-start | bytes 4718592 | tf_op jit(solution)/shard_map/reduce_scatter | solution.py:283
  327.5 274.0 %reduce-scatter.40.cloned.1.call-start = ((), (), s32[]{:S(2)}) async-start(), calls=%async_computation.36 | async-start | bytes 4718592 | tf_op jit(solution)/shard_map/reduce_scatter | solution.py:286
  331.8 271.6 %reduce-scatter.32.cloned.1.call-start = ((), (), s32[]{:S(2)}) async-start(), calls=%async_computation.32 | async-start | bytes 4718592 | tf_op jit(solution)/shard_map/reduce_scatter | solution.py:284
  351.4 254.0 %reduce-scatter.36.cloned.1.call-start = ((), (), s32[]{:S(2)}) async-start(), calls=%async_computation.34 | async-start | bytes 4718592 | tf_op jit(solution)/shard_map/reduce_scatter | solution.py:285
  354.5 263.1 %reduce-scatter.26.cloned.1.call-start = ((), (), s32[]{:S(2)}) async-start(), calls=%async_computation.29 | async-start | bytes 4718592 | tf_op jit(solution)/shard_map/reduce_scatter | solution.py:282
  443.7 224.8 %reduce-scatter.20.cloned.1.call-start = ((), (), s32[]{:S(2)}) async-start(), calls=%async_computation.26 | async-start | bytes 4718592 | tf_op jit(solution)/shard_map/reduce_scatter | solution.py:280
  586.3 182.1 %reduce-scatter.24.cloned.1.call-start = ((), (), s32[]{:S(2)}) async-start(), calls=%async_computation.28 | async-start | bytes 10616832 | tf_op jit(solution)/shard_map/reduce_scatter | solution.py:281
  597.8 213.5 %all-reduce.11.cloned.1.call-start = ((), (), s32[]{:S(2)}) async-start(), calls=%async_computation.41 | async-start | bytes 163840
  599.4 239.5 %reduce-scatter.48.cloned.1.call-start = ((), (), s32[]{:S(2)}) async-start(), calls=%async_computation.40 | async-start | bytes 327680
  601.4 264.2 %reduce-scatter.42.cloned.1.call-start = ((), (), s32[]{:S(2)}) async-start(), calls=%async_computation.37 | async-start | bytes 327680 | tf_op jit(solution)/shard_map/reduce_scatter | solution.py:308
  603.3 289.4 %reduce-scatter.34.cloned.1.call-start = ((), (), s32[]{:S(2)}) async-start(), calls=%async_computation.33 | async-start | bytes 327680 | tf_op jit(solution)/shard_map/reduce_scatter | solution.py:302
  605.3 314.1 %reduce-scatter.38.cloned.1.call-start = ((), (), s32[]{:S(2)}) async-start(), calls=%async_computation.35 | async-start | bytes 327680 | tf_op jit(solution)/shard_map/reduce_scatter | solution.py:305
  607.2 339.4 %reduce-scatter.28.cloned.1.call-start = ((), (), s32[]{:S(2)}) async-start(), calls=%async_computation.30 | async-start | bytes 327680 | tf_op jit(solution)/shard_map/reduce_scatter | solution.py:296
  619.4 354.6 %reduce-scatter.22.cloned.1.call-start = ((), (), s32[]{:S(2)}) async-start(), calls=%async_computation.27 | async-start | bytes 327680 | tf_op jit(solution)/shard_map/reduce_scatter | solution.py:290
  670.3 332.3 %reduce-scatter.46.cloned.1.call-start = ((), (), s32[]{:S(2)}) async-start(), calls=%async_computation.39 | async-start | bytes 819200
  (129 other events, 8531.0 us)
Sparse Core Ops, SparseCore 0:
  9.6 31.8 all-gather.9
  43.2 51.9 all-gather.11
  96.8 35.5 all-gather.13
  133.9 28.7 all-gather.17
  164.2 29.0 all-gather.19
  194.7 28.8 all-gather.15
  225.2 29.4 all-gather.21
  318.2 34.8 reduce-scatter.43
  355.4 53.8 reduce-scatter.29
  411.4 49.2 reduce-scatter.39
  463.0 51.3 reduce-scatter.31
  516.6 50.5 reduce-scatter.35
  569.4 48.1 reduce-scatter.25
  620.4 48.1 reduce-scatter.19
  670.7 97.6 reduce-scatter.23
  771.7 39.4 all-reduce.10
  814.1 24.8 reduce-scatter.47
  841.5 24.0 reduce-scatter.41
  868.6 24.0 reduce-scatter.33
  895.4 24.0 reduce-scatter.37
  922.4 24.0 reduce-scatter.27
  949.9 24.0 reduce-scatter.21
  977.2 25.3 reduce-scatter.45
where the time goes:
time: 1020 us; the launch traced here: 1010 us
  waiting for transfers between devices  395 us (39%)
  blocking collectives  364 us (36%)
  matrix products  128 us (13%)
  local copies, waits for them, and re-layouts  45.6 us (4%)
  other arithmetic  43.2 us (4%)
  starting transfers between devices  18.9 us (2%)
  between operations  17.1 us (2%)
    psum x3, blocking collectives, normalize(): lax.psum((jnp.sum(field, 0), jnp.sum(field * field, 0)), ('batch', 'rows'))  126 us
    reduce_scatter x1, waiting for transfers between devices, on_device(): lax.psum_scatter(grad_wb, 'rows', scatter_dimension=0, tiled=True)  98 us
    psum x2, blocking collectives, segment_totals(): lax.psum((jnp.sum(grad, 0), jnp.sum(grad * normed, 0)), ('batch', 'rows'))  96 us
    unnamed x26, waiting for transfers between devices  88.4 us
    dot_general x11, matrix products, tdot(): lax.dot_general(left, right, (((0,), (0,)), ((), ())), preferred_element_...  49.2 us
    reduce_scatter x1, waiting for transfers between devices, on_device(): lax.psum_scatter(grad_wa, 'rows', scatter_dimension=0, tiled=True)  49.1 us
    all_gather x1, blocking collectives, on_device(): lax.all_gather(w_head, 'rows', axis=0, tiled=True)  39.7 us
    psum x1, blocking collectives, on_device(): lax.psum((jnp.sum(d_pre, 0), jnp.sum(d_pre * hat_c, 0), grad_ln_gain, gra...  38.9 us
  transfers between devices with their start and end apart: 29, of which 12 were waited for; matrix products, arithmetic and copies ran while one was open for 20% of the time, Pallas kernels for 0%

commit v1 on v0

--- a/solution.py
+++ b/solution.py
@@ -1,6 +1,8 @@
 import jax
 import jax.numpy as jnp
 from jax import lax
+from jax.experimental import pallas as pl
+from jax.experimental.pallas import tpu as pltpu
 from jax.sharding import PartitionSpec as P
 
 
@@ -42,6 +44,73 @@
     return tuple(jnp.split(sum_at_owner(both, axis, dim), ends, axis=along))
 
 
+def total_kernel(part, result, held, from_rows, from_batch, send_rows, recv_rows, send_batch, recv_batch):
+    groups, ranks = lax.axis_size("batch"), lax.axis_size("rows")
+    here_g, here_r = lax.axis_index("batch"), lax.axis_index("rows")
+    along_rows = [(here_g, lax.rem(here_r + k, ranks)) for k in range(1, ranks)]
+    along_batch = [(lax.rem(here_g + k, groups), here_r) for k in range(1, groups)]
+    barrier = pltpu.get_barrier_semaphore()
+    for peer in along_rows + along_batch:
+        pl.semaphore_signal(
+            barrier, inc=1, device_id=peer, device_id_type=pl.DeviceIdType.MESH
+        )
+    pl.semaphore_wait(barrier, len(along_rows) + len(along_batch))
+    held[...] = part[...]
+    for peers, landing, send, recv in (
+        (along_rows, from_rows, send_rows, recv_rows),
+        (along_batch, from_batch, send_batch, recv_batch),
+    ):
+        copies = [
+            pltpu.make_async_remote_copy(
+                src_ref=held,
+                dst_ref=landing.at[k],
+                send_sem=send.at[k],
+                recv_sem=recv.at[k],
+                device_id=peer,
+                device_id_type=pl.DeviceIdType.MESH,
+            )
+            for k, peer in enumerate(peers)
+        ]
+        for copy in copies:
+            copy.start()
+        for copy in copies:
+            copy.wait()
+        total = held[...]
+        for k in range(len(peers)):
+            total = total + landing[k]
+        held[...] = total
+    result[...] = held[...]
+
+
+def total_over_all(arrays, channel):
+    groups, ranks = lax.axis_size("batch"), lax.axis_size("rows")
+    flat = jnp.concatenate([a.reshape(-1) for a in arrays])
+    width = -(-flat.shape[0] // 1024) * 128
+    packed = jnp.pad(flat, (0, 8 * width - flat.shape[0])).reshape(8, width)
+    dma = pltpu.SemaphoreType.DMA
+    summed = pl.pallas_call(
+        total_kernel,
+        out_shape=jax.ShapeDtypeStruct((8, width), jnp.float32),
+        in_specs=[pl.BlockSpec(memory_space=pltpu.VMEM)],
+        out_specs=pl.BlockSpec(memory_space=pltpu.VMEM),
+        scratch_shapes=[
+            pltpu.VMEM((8, width), jnp.float32),
+            pltpu.VMEM((ranks - 1, 8, width), jnp.float32),
+            pltpu.VMEM((groups - 1, 8, width), jnp.float32),
+            dma((ranks - 1,)),
+            dma((ranks - 1,)),
+            dma((groups - 1,)),
+            dma((groups - 1,)),
+        ],
+        compiler_params=pltpu.CompilerParams(collective_id=channel, has_side_effects=True),
+    )(packed).reshape(-1)
+    results, at = [], 0
+    for a in arrays:
+        results.append(summed[at : at + a.size].reshape(a.shape))
+        at += a.size
+    return tuple(results)
+
+
 def tdot(left, right):
     return lax.dot_general(
         left, right, (((0,), (0,)), ((), ())), preferred_element_type=jnp.float32
@@ -60,14 +129,18 @@
 
 
 def normalize(field, total_count):
-    sums, squares = lax.psum((jnp.sum(field, 0), jnp.sum(field * field, 0)), ("batch", "rows"))
+    sums, squares = total_over_all(
+        (jnp.sum(field, 0), jnp.sum(field * field, 0)), field.shape[1] // 512
+    )
     centre_value = sums / total_count
     inverse = lax.rsqrt(squares / total_count - centre_value * centre_value + 1e-05)
     return ((field - centre_value) * inverse, inverse)
 
 
 def segment_totals(grad, normed):
-    return lax.psum((jnp.sum(grad, 0), jnp.sum(grad * normed, 0)), ("batch", "rows"))
+    return total_over_all(
+        (jnp.sum(grad, 0), jnp.sum(grad * normed, 0)), grad.shape[1] // 512
+    )
 
 
 def norm_back(grad, normed, inverse, gain, shift_sum, gain_total_grad, total_count):
@@ -242,9 +315,9 @@
     returned = lax.all_to_all(back_pieces, "rows", split_axis=0, concat_axis=0, tiled=True)
     d_fmap = tdot(interpolated_value, returned.reshape(slot_count, d_in))
     d_pre = d_fmap * silu_slope(pre_out)
-    head_sums = lax.psum(
+    head_sums = total_over_all(
         (jnp.sum(d_pre, 0), jnp.sum(d_pre * hat_c, 0), grad_ln_gain, grad_ln_bias, grad_head_bias),
-        ("batch", "rows"),
+        9,
     )
     d_c = norm_back(
         d_pre, hat_c, inverse_c, gain_c, head_sums[0], head_sums[1], total_count

time: 1020 us -> 972 us (0.953)
  blocking collectives: 364 us -> 110 us
  waiting for transfers between devices: 395 us -> 498 us
  Pallas kernels: 0 us -> 84.4 us
    psum x6 -> x0, blocking collectives: 261 us -> none  [the longest x3 126 us: normalize(): lax.psum((jnp.sum(field, 0), jnp.sum(field * field, 0)), ('batch', 'rows'))]
    pallas_call x0 -> x6, Pallas kernels: none -> 84.4 us  [total_over_all(): pl.pallas_call(total_kernel, out_shape=jax.ShapeDtypeStruct((8, width), j...]
    reduce_scatter x1, waiting for transfers between devices: 0.02 us -> 40 us  [on_device(): lax.psum_scatter(grad_wv, 'rows', scatter_dimension=0, tiled=True)]
    reduce_scatter x1, waiting for transfers between devices: 10.4 us -> 48.7 us  [on_device(): lax.psum_scatter(grad_wc, 'rows', scatter_dimension=0, tiled=True)]
    all_gather x1, waiting for transfers between devices: 0.02 us -> 25.8 us  [on_device(): lax.all_gather(w_out, 'rows', axis=0, tiled=True)]
    unnamed x273 -> x301, local copies, waits for them, and re-layouts: 28.3 us -> 28.4 us
  transfers between devices with their start and end apart: 29 -> 29, of which waited for: 12 -> 14; matrix products, arithmetic and copies ran while one was open for 20% -> 23% of each run, Pallas kernels for 0% -> 9%
where the time goes in v1:
time: 972 us; the launch traced here: 961 us
  waiting for transfers between devices  498 us (51%)
  matrix products  128 us (13%)
  blocking collectives  110 us (11%)
  Pallas kernels  84.4 us (9%)
  other arithmetic  53 us (5%)
  local copies, waits for them, and re-layouts  50.3 us (5%)
  starting transfers between devices  20.2 us (2%)
  between operations  17.1 us (2%)
    reduce_scatter x1, waiting for transfers between devices, on_device(): lax.psum_scatter(grad_wb, 'rows', scatter_dimension=0, tiled=True)  98 us
    unnamed x26, waiting for transfers between devices  87.3 us
    pallas_call x6, Pallas kernels, total_over_all(): pl.pallas_call(total_kernel, out_shape=jax.ShapeDtypeStruct((8, width), j...  84.4 us
    dot_general x11, matrix products, tdot(): lax.dot_general(left, right, (((0,), (0,)), ((), ())), preferred_element_...  49.2 us
    reduce_scatter x1, waiting for transfers between devices, on_device(): lax.psum_scatter(grad_wa, 'rows', scatter_dimension=0, tiled=True)  49.1 us
    reduce_scatter x1, waiting for transfers between devices, on_device(): lax.psum_scatter(grad_wc, 'rows', scatter_dimension=0, tiled=True)  48.7 us
    all_gather x1, blocking collectives, on_device(): lax.all_gather(w_head, 'rows', axis=0, tiled=True)  47.8 us
    reduce_scatter x1, waiting for transfers between devices, on_device(): lax.psum_scatter(grad_wv, 'rows', scatter_dimension=0, tiled=True)  40 us
  transfers between devices with their start and end apart: 29, of which 14 were waited for; matrix products, arithmetic and copies ran while one was open for 23% of the time, Pallas kernels for 9%

profile of v1, /device:TPU:0, one launch (start us, length us, event | category | flops | bytes accessed | tf_op | source)
XLA Modules:
  0.0 961.4 jit_solution(8441374619011463074)
XLA Ops:
  19.9 21.7 %all-gather.10.cloned.1.call-done = bf16[2048,512]{1,0:T(8,128)(2,1)} async-done(((bf16[256,512]{1,0:T(8,128)(2,1)}), bf16[2048,512]{1,0:T(8,128)(2,1)}) %all-gather.10.cloned.1.call-update) | async-done | bytes 2097168 | tf_op jit(solution)/shard_map/all_gather | solution.py:186
  67.4 47.8 %all_gather.39 = bf16[4096,80]{0,1:T(8,128)(2,1)} all-gather(bf16[512,80]{0,1:T(8,128)(2,1)S(1)} %copy-done.8), channel_id=1, replica_groups=mesh['batch'=4,'rows'=8] {'rows'}, dimensions={0}, use_global_device_ids=true | all-gather | bytes 737280 | tf_op jit(solution)/shard_map/all_gather | solution.py:193
  196.7 15.5 %all-gather = bf16[8,10,512]{2,1,0:T(8,128)(2,1)S(1)} all-gather(bf16[1,10,512]{2,1,0:T(8,128)(2,1)S(1)} %fusion.14), channel_id=1, replica_groups=mesh['batch'=4,'rows'=8] {'rows'}, dimensions={0}, use_global_device_ids=true | all-gather | bytes 92160 | tf_op jit(solution)/shard_map/all_gather | solution.py:256
  214.2 14.3 %all-gather.1 = bf16[8,10,512]{2,1,0:T(8,128)(2,1)S(1)} all-gather(bf16[1,10,512]{2,1,0:T(8,128)(2,1)S(1)} %fusion.15), channel_id=1, replica_groups=mesh['batch'=4,'rows'=8] {'rows'}, dimensions={0}, use_global_device_ids=true | all-gather | bytes 92160 | tf_op jit(solution)/shard_map/all_gather | solution.py:257
  232.6 25.8 %all-gather.22.cloned.1.call-done = bf16[512,2048]{1,0:T(8,128)(2,1)} async-done(((bf16[64,2048]{1,0:T(8,128)(2,1)}), bf16[512,2048]{1,0:T(8,128)(2,1)}) %all-gather.22.cloned.1.call-update) | async-done | bytes 2097168 | tf_op jit(solution)/shard_map/all_gather | solution.py:192
  279.4 15.9 %all_to_all.24 = bf16[8,10,1024]{2,1,0:T(8,128)(2,1)S(1)} all-to-all(bf16[8,10,1024]{2,1,0:T(8,128)(2,1)S(1)} %reshape.336), channel_id=1, replica_groups=mesh['batch'=4,'rows'=8] {'rows'}, dimensions={0} | all-to-all | bytes 327680 | tf_op jit(solution)/shard_map/all_to_all | solution.py:34
  305.3 16.8 %all_to_all.25 = bf16[8,8,2048]{2,1,0:T(8,128)(2,1)S(1)} all-to-all(bf16[8,8,2048]{2,1,0:T(8,128)(2,1)S(1)} %bitcast_select_fusion), channel_id=1, replica_groups=mesh['batch'=4,'rows'=8] {'rows'}, dimensions={0} | all-to-all | bytes 524288 | tf_op jit(solution)/shard_map/all_to_all | solution.py:315
  322.4 14.8 %multiply_reduce_fusion = (f32[2048]{0:T(1024)S(1)}, f32[2048]{0:T(1024)S(1)}, f32[1024,2048]{1,0:T(8,128)}) fusion(f32[1024,2048]{1,0:T(8,128)} %get-tuple-element.200, f32[2048]{0:T(1024)S(1)} %get-tuple-element.191, f32[2048]{0:T(1024)S(1)} %bitcast.189, bf16[1024,2048]{1,0:T(8,128)(2,1)} %bitcast.163, f32[2048]{0:T(1024)} %param.41, ...), kind=kOutput, calls=%fused_computation.6 | convolution fusion | flops 309587968 | bytes 21297152 | tf_op jit(solution)/shard_map/dot_general | solution.py:115
  338.6 14.4 %shard_map.405 = f32[8,768]{1,0:T(8,128)} custom-call(f32[8,768]{1,0:T(8,128)} %reshape.330.part), custom_call_target="tpu_custom_call" | custom-call | tf_op jit(solution)/shard_map/pallas_call | solution.py:91
  377.3 11.2 %shard_map.406 = f32[8,128]{1,0:T(8,128)} custom-call(f32[8,128]{1,0:T(8,128)} %pad_maximum_fusion.7.part), custom_call_target="tpu_custom_call" | custom-call | tf_op jit(solution)/shard_map/pallas_call | solution.py:91
  421.6 26.5 %shard_map.407 = f32[8,128]{1,0:T(8,128)} custom-call(f32[8,128]{1,0:T(8,128)} %pad_maximum_fusion.8.part), custom_call_target="tpu_custom_call" | custom-call | tf_op jit(solution)/shard_map/pallas_call | solution.py:91
  458.4 11.4 %fusion.61 = f32[4608,512]{1,0:T(8,128)} fusion(bf16[1024,4608]{1,0:T(8,128)(2,1)} %constant_dynamic-update-slice_fusion, bf16[1024,512]{1,0:T(8,128)(2,1)S(1)} %multiply_convert_fusion.8), kind=kOutput, calls=%fused_computation.268 | convolution fusion | flops 4831838208 | bytes 19922944 | tf_op jit(solution)/shard_map/dot_general | solution.py:115
  477.4 40.0 %reduce-scatter.36.cloned.1.call-done = f32[256,512]{0,1:T(8,128)} async-done(((f32[2048,512]{0,1:T(8,128)}), f32[256,512]{0,1:T(8,128)}) %reduce-scatter.36.cloned.1.call-update) | async-done | bytes 524304 | tf_op jit(solution)/shard_map/reduce_scatter | solution.py:358
  519.3 48.7 %reduce-scatter.26.cloned.1.call-done = f32[64,2048]{1,0:T(8,128)} async-done(((f32[512,2048]{1,0:T(8,128)}), f32[64,2048]{1,0:T(8,128)}) %reduce-scatter.26.cloned.1.call-update) | async-done | bytes 524304 | tf_op jit(solution)/shard_map/reduce_scatter | solution.py:355
  569.8 49.1 %reduce-scatter.20.cloned.1.call-done = f32[256,512]{0,1:T(8,128)} async-done(((f32[2048,512]{0,1:T(8,128)}), f32[256,512]{0,1:T(8,128)}) %reduce-scatter.20.cloned.1.call-update) | async-done | bytes 524304 | tf_op jit(solution)/shard_map/reduce_scatter | solution.py:353
  620.7 98.0 %reduce-scatter.24.cloned.1.call-done = f32[576,512]{1,0:T(8,128)} async-done(((f32[4608,512]{1,0:T(8,128)}), f32[576,512]{1,0:T(8,128)}) %reduce-scatter.24.cloned.1.call-update) | async-done | bytes 1179664 | tf_op jit(solution)/shard_map/reduce_scatter | solution.py:354
  732.0 29.4 %all-reduce.6.cloned.1.call-done = bf16[512,80]{0,1:T(8,128)(2,1)} async-done(((bf16[512,80]{0,1:T(8,128)(2,1)}), bf16[512,80]{0,1:T(8,128)(2,1)}) %all-reduce.6.cloned.1.call-update) | async-done | bytes 81936
  762.9 26.3 %reduce-scatter.48.cloned.1.call-done = bf16[128,256]{1,0:T(8,128)(2,1)} async-done(((bf16[512,256]{1,0:T(8,128)(2,1)}), bf16[128,256]{1,0:T(8,128)(2,1)}) %reduce-scatter.48.cloned.1.call-update) | async-done | bytes 65552
  790.8 25.1 %reduce-scatter.42.cloned.1.call-done = bf16[64,512]{1,0:T(8,128)(2,1)} async-done(((bf16[64,2048]{1,0:T(8,128)(2,1)}), bf16[64,512]{1,0:T(8,128)(2,1)}) %reduce-scatter.42.cloned.1.call-update) | async-done | bytes 65552 | tf_op jit(solution)/shard_map/reduce_scatter | solution.py:381
  817.4 25.6 %reduce-scatter.34.cloned.1.call-done = bf16[256,128]{0,1:T(8,128)(2,1)} async-done(((bf16[256,512]{0,1:T(8,128)(2,1)}), bf16[256,128]{0,1:T(8,128)(2,1)}) %reduce-scatter.34.cloned.1.call-update) | async-done | bytes 65552 | tf_op jit(solution)/shard_map/reduce_scatter | solution.py:375
  844.6 25.1 %reduce-scatter.38.cloned.1.call-done = bf16[256,128]{0,1:T(8,128)(2,1)} async-done(((bf16[256,512]{0,1:T(8,128)(2,1)}), bf16[256,128]{0,1:T(8,128)(2,1)}) %reduce-scatter.38.cloned.1.call-update) | async-done | bytes 65552 | tf_op jit(solution)/shard_map/reduce_scatter | solution.py:378
  871.3 25.5 %reduce-scatter.28.cloned.1.call-done = bf16[64,512]{1,0:T(8,128)(2,1)} async-done(((bf16[64,2048]{1,0:T(8,128)(2,1)}), bf16[64,512]{1,0:T(8,128)(2,1)}) %reduce-scatter.28.cloned.1.call-update) | async-done | bytes 65552 | tf_op jit(solution)/shard_map/reduce_scatter | solution.py:369
  898.3 26.0 %reduce-scatter.22.cloned.1.call-done = bf16[256,128]{0,1:T(8,128)(2,1)} async-done(((bf16[256,512]{0,1:T(8,128)(2,1)}), bf16[256,128]{0,1:T(8,128)(2,1)}) %reduce-scatter.22.cloned.1.call-update) | async-done | bytes 65552 | tf_op jit(solution)/shard_map/reduce_scatter | solution.py:363
  925.9 27.0 %reduce-scatter.46.cloned.1.call-done = bf16[128,576]{1,0:T(8,128)(2,1)} async-done(((bf16[512,576]{1,0:T(8,128)(2,1)}), bf16[128,576]{1,0:T(8,128)(2,1)}) %reduce-scatter.46.cloned.1.call-update) | async-done | bytes 147472
  (482 shorter events, 262.3 us)
Async XLA Ops:
  7.9 127.6 %all-gather.12.cloned.1.call-start = ((), (), s32[]{:S(2)}) async-start(), calls=%async_computation.20 | async-start | bytes 5308416 | tf_op jit(solution)/shard_map/all_gather | solution.py:187
  8.7 150.4 %all-gather.14.cloned.1.call-start = ((), (), s32[]{:S(2)}) async-start(), calls=%async_computation.21 | async-start | bytes 2359296 | tf_op jit(solution)/shard_map/all_gather | solution.py:188
  9.4 185.2 %all-gather.18.cloned.1.call-start = ((), (), s32[]{:S(2)}) async-start(), calls=%async_computation.23 | async-start | bytes 2359296 | tf_op jit(solution)/shard_map/all_gather | solution.py:190
  10.0 202.2 %all-gather.20.cloned.1.call-start = ((), (), s32[]{:S(2)}) async-start(), calls=%async_computation.24 | async-start | bytes 2359296 | tf_op jit(solution)/shard_map/all_gather | solution.py:191
  10.6 219.2 %all-gather.16.cloned.1.call-start = ((), (), s32[]{:S(2)}) async-start(), calls=%async_computation.22 | async-start | bytes 2359296 | tf_op jit(solution)/shard_map/all_gather | solution.py:189
  11.2 104.5 %all-to-all-start = ((s32[8,1,8]{2,1,0:T(1,128)}), s32[8,1,8]{2,1,0:T(1,128)S(1)}, u32[]{:S(2)}, u32[]{:S(2)}) async-start(s32[8,1,8]{2,1,0:T(1,128)} %bitcast.195), calls=%async_computation | async-start | bytes 8192 | tf_op jit(solution)/shard_map/all_to_all | solution.py:244
  17.5 240.9 %all-gather.22.cloned.1.call-start = ((), (), s32[]{:S(2)}) async-start(), calls=%async_computation.25 | async-start | bytes 2359296 | tf_op jit(solution)/shard_map/all_gather | solution.py:192
  60.4 56.5 %collective-permute-start = (bf16[64,1,16,512]{3,2,0,1:T(8,128)(2,1)S(1)}, bf16[64,1,16,512]{3,2,0,1:T(8,128)(2,1)}, u32[]{:S(2)}, u32[]{:S(2)}) collective-permute-start(bf16[64,1,16,512]{3,2,0,1:T(8,128)(2,1)S(1)} %bitcast.169), channel_id=1, source_target_pairs={{0,1},{1,2},{2,3},{3,4},{4,5},{5,6},{6,7},{8,9},{9,10},{10,11},{11... | collective-permute-start | bytes 3145736 | tf_op jit(solution)/shard_map/ppermute | solution.py:17
  194.6 275.3 %reduce-scatter.44.cloned.1.call-start = ((), (), s32[]{:S(2)}) async-start(), calls=%async_computation.38 | async-start | bytes 1474560 | tf_op jit(solution)/shard_map/reduce_scatter | solution.py:360
  265.1 206.4 %reduce-scatter.30.cloned.1.call-start = ((), (), s32[]{:S(2)}) async-start(), calls=%async_computation.31 | async-start | bytes 4718592 | tf_op jit(solution)/shard_map/reduce_scatter | solution.py:356
  274.8 198.7 %reduce-scatter.40.cloned.1.call-start = ((), (), s32[]{:S(2)}) async-start(), calls=%async_computation.36 | async-start | bytes 4718592 | tf_op jit(solution)/shard_map/reduce_scatter | solution.py:359
  279.0 196.5 %reduce-scatter.32.cloned.1.call-start = ((), (), s32[]{:S(2)}) async-start(), calls=%async_computation.32 | async-start | bytes 4718592 | tf_op jit(solution)/shard_map/reduce_scatter | solution.py:357
  298.1 219.3 %reduce-scatter.36.cloned.1.call-start = ((), (), s32[]{:S(2)}) async-start(), calls=%async_computation.34 | async-start | bytes 4718592 | tf_op jit(solution)/shard_map/reduce_scatter | solution.py:358
  301.3 266.6 %reduce-scatter.26.cloned.1.call-start = ((), (), s32[]{:S(2)}) async-start(), calls=%async_computation.29 | async-start | bytes 4718592 | tf_op jit(solution)/shard_map/reduce_scatter | solution.py:355
  368.3 250.5 %reduce-scatter.20.cloned.1.call-start = ((), (), s32[]{:S(2)}) async-start(), calls=%async_computation.26 | async-start | bytes 4718592 | tf_op jit(solution)/shard_map/reduce_scatter | solution.py:353
  458.2 260.5 %reduce-scatter.24.cloned.1.call-start = ((), (), s32[]{:S(2)}) async-start(), calls=%async_computation.28 | async-start | bytes 10616832 | tf_op jit(solution)/shard_map/reduce_scatter | solution.py:354
  469.8 291.7 %all-reduce.6.cloned.1.call-start = ((), (), s32[]{:S(2)}) async-start(), calls=%async_computation.41 | async-start | bytes 163840
  471.5 317.7 %reduce-scatter.48.cloned.1.call-start = ((), (), s32[]{:S(2)}) async-start(), calls=%async_computation.40 | async-start | bytes 327680
  473.5 342.4 %reduce-scatter.42.cloned.1.call-start = ((), (), s32[]{:S(2)}) async-start(), calls=%async_computation.37 | async-start | bytes 327680 | tf_op jit(solution)/shard_map/reduce_scatter | solution.py:381
  475.4 367.6 %reduce-scatter.34.cloned.1.call-start = ((), (), s32[]{:S(2)}) async-start(), calls=%async_computation.33 | async-start | bytes 327680 | tf_op jit(solution)/shard_map/reduce_scatter | solution.py:375
  477.3 392.4 %reduce-scatter.38.cloned.1.call-start = ((), (), s32[]{:S(2)}) async-start(), calls=%async_computation.35 | async-start | bytes 327680 | tf_op jit(solution)/shard_map/reduce_scatter | solution.py:378
  519.2 377.6 %reduce-scatter.28.cloned.1.call-start = ((), (), s32[]{:S(2)}) async-start(), calls=%async_computation.30 | async-start | bytes 327680 | tf_op jit(solution)/shard_map/reduce_scatter | solution.py:369
  569.7 354.6 %reduce-scatter.22.cloned.1.call-start = ((), (), s32[]{:S(2)}) async-start(), calls=%async_computation.27 | async-start | bytes 327680 | tf_op jit(solution)/shard_map/reduce_scatter | solution.py:363
  620.6 332.2 %reduce-scatter.46.cloned.1.call-start = ((), (), s32[]{:S(2)}) async-start(), calls=%async_computation.39 | async-start | bytes 819200
  (140 other events, 6750.8 us)
Sparse Core Ops, SparseCore 0:
  9.6 31.8 all-gather.9
  43.2 60.1 all-gather.11
  105.0 31.2 all-gather.13
  137.7 29.7 all-gather.17
  168.9 28.0 all-gather.19
  198.5 29.6 all-gather.15
  229.8 28.5 all-gather.21
  265.2 33.8 reduce-scatter.43
  301.5 56.9 reduce-scatter.29
  360.6 53.3 reduce-scatter.39
  416.2 50.7 reduce-scatter.31
  469.2 48.1 reduce-scatter.35
  519.7 48.1 reduce-scatter.25
  570.6 48.1 reduce-scatter.19
  621.0 97.6 reduce-scatter.23
  722.0 39.3 all-reduce.5
  764.3 24.8 reduce-scatter.47
  791.8 24.0 reduce-scatter.41
  818.9 24.0 reduce-scatter.33
  845.6 24.0 reduce-scatter.37
  872.7 24.0 reduce-scatter.27
  900.1 24.0 reduce-scatter.21
  927.4 25.3 reduce-scatter.45

commit v2 on v0

--- a/solution.py
+++ b/solution.py
@@ -1,6 +1,8 @@
 import jax
 import jax.numpy as jnp
 from jax import lax
+from jax.experimental import pallas as pl
+from jax.experimental.pallas import tpu as pltpu
 from jax.sharding import PartitionSpec as P
 
 
@@ -59,24 +61,1356 @@
     return sig * (1.0 + value * (1.0 - sig))
 
 
-def normalize(field, total_count):
+def norm_back(grad, normed, inverse, gain, shift_sum, gain_total_grad, total_count):
+    return (
+        gain * inverse * (grad - shift_sum / total_count - normed * gain_total_grad / total_count)
+    )
+
+
+MESH = pl.DeviceIdType.MESH
+LOW = jnp.bfloat16
+F32 = jnp.float32
+
+
+class Wires:
+    def __init__(self, send, recv):
+        self.send, self.recv, self.at, self.open = send, recv, 0, []
+
+    def push(self, source, target, peer):
+        copy = pltpu.make_async_remote_copy(
+            src_ref=source,
+            dst_ref=target,
+            send_sem=self.send.at[self.at],
+            recv_sem=self.recv.at[self.at],
+            device_id=peer,
+            device_id_type=MESH,
+        )
+        self.at += 1
+        copy.start()
+        self.open.append(copy)
+        return copy
+
+    def close(self):
+        for copy in self.open:
+            copy.wait_send()
+
+
+def greet(peers):
+    barrier = pltpu.get_barrier_semaphore()
+    for peer in peers:
+        pl.semaphore_signal(barrier, inc=1, device_id=peer, device_id_type=MESH)
+    pl.semaphore_wait(barrier, len(peers))
+
+
+class Place:
+    def __init__(self):
+        self.groups, self.ranks = lax.axis_size("batch"), lax.axis_size("rows")
+        self.g, self.s = lax.axis_index("batch"), lax.axis_index("rows")
+        self.chips = self.ranks // 2
+        self.z, self.core = self.s // 2, lax.rem(self.s, 2)
+        self.other = 1 - self.core
+
+    def row_peers(self):
+        return [(self.g, lax.rem(self.s + k, self.ranks)) for k in range(1, self.ranks)]
+
+    def batch_peers(self):
+        return [(lax.rem(self.g + k, self.groups), self.s) for k in range(1, self.groups)]
+
+    def line_peers(self):
+        return [
+            (self.g, lax.rem(self.z + k, self.chips) * 2 + self.core) for k in range(1, self.chips)
+        ]
+
+    def twin(self):
+        return (self.g, self.z * 2 + self.other)
+
+
+def rows_of(ref, index, size):
+    return ref.at[pl.ds(pl.multiple_of(index * size, size), size)]
+
+
+def total_start(net, place, held, from_rows):
+    return [net.push(held, from_rows.at[k], peer) for k, peer in enumerate(place.row_peers())]
+
+
+def total_finish(net, place, copies, held, from_rows, second, from_batch):
+    for copy in copies:
+        copy.wait_recv()
+    total = held[...]
+    for k in range(len(copies)):
+        total = total + from_rows[k]
+    second[...] = total
+    more = [net.push(second, from_batch.at[k], peer) for k, peer in enumerate(place.batch_peers())]
+    for copy in more:
+        copy.wait_recv()
+    for k in range(len(more)):
+        total = total + from_batch[k]
+    return total
+
+
+def spread(ref, values):
+    quarter = values[0].shape[1] // 4
+    for n, value in enumerate(values):
+        for k in range(4):
+            ref[4 * n + k : 4 * n + k + 1, 0:quarter] = value[:, k * quarter : (k + 1) * quarter]
+
+
+def gathered(block, n, quarter, at=0):
+    return jnp.concatenate(
+        [block[4 * n + k : 4 * n + k + 1, at : at + quarter] for k in range(4)], axis=1
+    )
+
+
+class Scatter:
+    def __init__(self, net, place, shard, part, from_twin, from_batch, partial, from_line, result):
+        self.net, self.place, self.shard, self.part = net, place, shard, part
+        self.from_twin, self.from_batch, self.partial = from_twin, from_batch, partial
+        self.from_line, self.result = from_line, result
+
+    def pair(self):
+        place = self.place
+        self.first = [
+            self.net.push(self.shard(2 * z + place.other), self.from_twin.at[z], place.twin())
+            for z in range(place.chips)
+        ]
+
+    def batch(self):
+        place = self.place
+        self.second = []
+        for z in range(place.chips):
+            self.first[z].wait_recv()
+            mine = self.shard(2 * z + place.core)
+            rows = mine.shape[0]
+            step = next(n for n in (64, 32, 16) if rows % n == 0)
+
+            @pl.loop(0, rows // step)
+            def _(n):
+                at = pl.ds(pl.multiple_of(n * step, step), step)
+                mine[at, :] = (
+                    mine[at, :].astype(F32) + self.from_twin[z, at, :].astype(F32)
+                ).astype(LOW)
+
+            for k, peer in enumerate(place.batch_peers()):
+                self.second.append(
+                    self.net.push(self.part(mine, peer[0]), self.from_batch.at[k, z], peer)
+                )
+
+    def line(self):
+        place = self.place
+        peers = place.groups - 1
+        self.third = []
+        for copy in self.second:
+            copy.wait_recv()
+        for z in range(place.chips):
+            mine = self.part(self.shard(2 * z + place.core), place.g)
+            total = mine[...].astype(F32)
+            for k in range(peers):
+                total = total + self.from_batch[k, z].astype(F32)
+            self.partial[z] = total.astype(LOW)
+        for k, peer in enumerate(place.line_peers()):
+            self.third.append(
+                self.net.push(self.partial.at[peer[1] // 2], self.from_line.at[k], peer)
+            )
+
+    def finish(self):
+        for copy in self.third:
+            copy.wait_recv()
+        total = self.partial[self.place.z].astype(F32)
+        for k in range(self.place.chips - 1):
+            total = total + self.from_line[k].astype(F32)
+        self.result[...] = total
+
+
+def slope_of(value):
+    sig = 0.5 * jnp.tanh(0.5 * value) + 0.5
+    return sig * (1.0 + value * (1.0 - sig))
+
+
+def column_of(shape, columns):
+    return lax.rem(lax.broadcasted_iota(jnp.int32, shape, 0), columns)
+
+
+def from_left(value, columns):
+    return jnp.where(
+        column_of(value.shape, columns) == 0, 0.0, pltpu.roll(value, 1, 0)
+    )
+
+
+def from_right(value, columns):
+    return jnp.where(
+        column_of(value.shape, columns) == columns - 1,
+        0.0,
+        pltpu.roll(value, value.shape[0] - 1, 0),
+    )
+
+
+def folded(value):
+    rows, width = value.shape
+    return jnp.sum(value.reshape(rows // 8, 8, width), axis=0)
+
+
+def backward_kernel(geometry, r):
+    cells, d_in, d_mid, columns, total_count, capacity, entries, samples = geometry
+    place = Place()
+    net = Wires(r.send, r.recv)
+    ranks, groups, chips = place.ranks, place.groups, place.chips
+    half = d_in // 2
+    greet(place.row_peers() + place.batch_peers())
+    local = r.local
+    loads = {}
+    for n, (key, source, target) in enumerate(
+        (
+            (0, r.in_hat_c, r.hat_c),
+            (1, r.in_slope, r.slope),
+            (2, r.in_w_c, r.w_c),
+            (3, r.in_hat_b, r.hat_b),
+            (4, r.in_low_bt, r.low_bt),
+            ("q", r.in_g_q, r.g_q),
+            ("o", r.in_g_o, r.g_o),
+            ("h", r.in_g_h, r.g_h),
+            (5, r.in_low_t, r.low_t),
+            (6, r.in_w_b, r.w_b),
+        )
+    ):
+        loads[key] = pltpu.make_async_copy(source, target, local.at[n])
+        loads[key].start()
+
+    back = r.back
+    dkv, dkv_in, dkv_own, dkv_all = r.dkv, r.dkv_in, r.dkv_own, r.dkv_all
+    bank_cols = r.bank_cols
+    depth = d_in // ranks
+    entry = bank_cols.shape[0] // ranks
+    kv = [
+        net.push(dkv.at[:, pl.ds(pl.multiple_of(peer[1] * entry, entry), entry)], dkv_in.at[k], peer)
+        for k, peer in enumerate(place.row_peers())
+    ]
+
+    def block_rows(ref, count):
+        return lambda s: rows_of(ref, s, ref.shape[0] // count)
+
+    def by_columns(width):
+        return lambda view, g: view.at[:, pl.ds(pl.multiple_of(g * width, width), width)]
+
+    def by_rows(height):
+        return lambda view, g: view.at[pl.ds(pl.multiple_of(g * height, height), height)]
+
+    def scatter(key, shard, part):
+        return Scatter(
+            net, place, shard, part, *(getattr(r, n + key) for n in ("tw_", "ba_", "pa_", "li_", "out_"))
+        )
+
+    per = cells // depth
+
+    def shard_a(s):
+        at = pl.ds(pl.multiple_of(lax.rem(s, per) * depth, depth), depth)
+        return r.low_t.at[s // per, :, at]
+
+    sc = {
+        "q": scatter("q", block_rows(r.g_q, ranks), by_columns(d_mid // groups)),
+        "o": scatter("o", block_rows(r.g_o, ranks), by_columns(d_in // groups)),
+        "h": scatter("h", lambda s: r.g_h.at[s], by_rows(r.g_h.shape[1] // groups)),
+        "c": scatter("c", block_rows(r.g_c, ranks), by_columns(d_in // groups)),
+        "b": scatter("b", block_rows(r.g_b, ranks), by_columns(d_mid // groups)),
+        "a": scatter("a", shard_a, by_rows(d_mid // groups)),
+    }
+    for key in "qoh":
+        loads[key].wait()
+        sc[key].pair()
+
+    for key in (0, 1):
+        loads[key].wait()
+    hat_c, slope, d_pre, d_c = r.hat_c, r.slope, r.d_pre, r.slope
+    acc = r.acc
+    acc[...] = jnp.zeros_like(acc)
+    tile = 128
+
+    @pl.loop(0, cells // tile)
+    def _(t):
+        at = pl.ds(pl.multiple_of(t * tile, tile), tile)
+        for h in range(2):
+            on = slice(h * half, (h + 1) * half)
+            grad = jnp.dot(
+                r.et[h, at, :], back[...], preferred_element_type=F32
+            ) * slope[at, on].astype(F32)
+            d_pre[at, on] = grad.astype(LOW)
+            acc[0, :, on] += folded(grad)
+            acc[1, :, on] += folded(grad * hat_c[at, on].astype(F32))
+
+    own1 = r.own1
+    own1[...] = r.head_part[...]
+    spread(own1, [jnp.sum(acc[n], axis=0, keepdims=True) for n in range(2)])
+    started = total_start(net, place, own1, r.rows1)
+    for key in "qoh":
+        sc[key].batch()
+    total = total_finish(net, place, started, own1, r.rows1, r.mid1, r.batch1)
+    r.out_head[...] = total
+    shift_c = gathered(total, 0, d_in // 4) / total_count
+    gain_c = gathered(total, 1, d_in // 4) / total_count
+    scale_c = r.scale_c[...]
+
+    for key in (2, 3):
+        loads[key].wait()
+    w_c, hat_b, d_act = r.w_c, r.hat_b, r.d_act
+    acc[...] = jnp.zeros_like(acc)
+    norm_b, norm_a = r.norm_b, r.norm_a
+
+    @pl.loop(0, cells // tile)
+    def _(t):
+        at = pl.ds(pl.multiple_of(t * tile, tile), tile)
+        grad = scale_c * (
+            d_pre[at, :].astype(F32) - shift_c - hat_c[at, :].astype(F32) * gain_c
+        )
+        low = grad.astype(LOW)
+        d_c[at, :] = low
+        hat = hat_b[at, :].astype(F32)
+        back_b = ndot(low, w_c[...]) * slope_of(norm_b[0:1, :] * hat + norm_b[1:2, :])
+        d_act[at, :] = back_b
+        acc[0, :, 0:d_mid] += folded(back_b)
+        acc[1, :, 0:d_mid] += folded(back_b * hat)
+
+    reload = pltpu.make_async_copy(r.in_x, r.hat_c, local.at[20])
+    reload.start()
+    own2 = r.own2
+    spread(own2, [jnp.sum(acc[n, :, 0:d_mid], axis=0, keepdims=True) for n in range(2)])
+    started = total_start(net, place, own2, r.rows2)
+    loads[4].wait()
+    wide = 256
+
+    @pl.loop(0, d_in // wide)
+    def _(t):
+        at = pl.ds(pl.multiple_of(t * wide, wide), wide)
+        r.g_c[:, at] = jnp.dot(
+            r.low_bt[...], d_c[:, at], preferred_element_type=F32
+        ).astype(LOW)
+
+    sc["c"].pair()
+    total = total_finish(net, place, started, own2, r.rows2, r.mid2, r.batch2)
+    r.out_b_sums[...] = total
+    shift_b = gathered(total, 0, d_mid // 4) / total_count
+    gain_b = gathered(total, 1, d_mid // 4) / total_count
+
+    d_b, d_up, d_down = r.d_b, r.d_up, r.d_down
+    big = 256
+    tiles = cells // big
+    first, last = place.s == 0, place.s == ranks - 1
+    halo_send, halo_recv = r.halo_send, r.halo_recv
+
+    def halo(t, way):
+        at = pl.ds(pl.multiple_of(t * big, big), big)
+        return pltpu.make_async_remote_copy(
+            src_ref=d_b.at[1, at],
+            dst_ref=(d_up if way == 0 else d_down).at[at],
+            send_sem=halo_send.at[way, t],
+            recv_sem=halo_recv.at[way, t],
+            device_id=(place.g, place.s + 1 if way == 0 else place.s - 1),
+            device_id_type=MESH,
+        )
+
+    @pl.when(first)
+    def _():
+        d_up[...] = jnp.zeros_like(d_up)
+
+    @pl.when(last)
+    def _():
+        d_down[...] = jnp.zeros_like(d_down)
+
+    @pl.loop(0, tiles)
+    def _(t):
+        at = pl.ds(pl.multiple_of(t * big, big), big)
+        grad = norm_b[2:3, :] * (
+            d_act[at, :] - shift_b - hat_b[at, :].astype(F32) * gain_b
+        )
+        d_b[1, at, :] = grad.astype(LOW)
+
+        @pl.when(jnp.logical_not(last))
+        def _():
+            halo(t, 0).start()
+
+        @pl.when(jnp.logical_not(first))
+        def _():
+            halo(t, 1).start()
+
+        d_b[0, at, :] = from_right(grad, columns).astype(LOW)
+        d_b[2, at, :] = from_left(grad, columns).astype(LOW)
+
+    loads[5].wait()
+
+    @pl.loop(0, 9)
+    def _(t):
+        i, j = t // 3, lax.rem(t, 3)
+        r.g_b[pl.ds(pl.multiple_of(t * d_mid, d_mid), d_mid), :] = jnp.dot(
+            r.low_t[i], d_b[j], preferred_element_type=F32
+        ).astype(LOW)
+
+    more = pltpu.make_async_copy(r.in_hat_a, hat_b, local.at[18])
+    more.start()
+    sc["b"].pair()
+    for key in "qoh":
+        sc[key].line()
+    sc["c"].batch()
+
+    loads[6].wait()
+    more.wait()
+    w_b, hat_a = r.w_b, hat_b
+    acc[...] = jnp.zeros_like(acc)
+
+    @pl.loop(0, tiles)
+    def _(t):
+        at = pl.ds(pl.multiple_of(t * big, big), big)
+
+        @pl.when(jnp.logical_not(first))
+        def _():
+            halo(t, 0).wait_recv()
+
+        @pl.when(jnp.logical_not(last))
+        def _():
+            halo(t, 1).wait_recv()
+
+        parts = []
+        for j in range(3):
+            taps = [w_b[(3 * i + j) * d_mid : (3 * i + j + 1) * d_mid, :] for i in range(3)]
+            parts.append(
+                ndot(d_down[at, :], taps[0]) + ndot(d_b[1, at, :], taps[1]) + ndot(d_up[at, :], taps[2])
+            )
+        grad = from_right(parts[0], columns) + parts[1] + from_left(parts[2], columns)
+        hat = hat_a[at, :].astype(F32)
+        grad = grad * slope_of(norm_a[0:1, :] * hat + norm_a[1:2, :])
+        d_act[at, :] = grad
+        acc[0, :, 0:d_mid] += folded(grad)
+        acc[1, :, 0:d_mid] += folded(grad * hat)
+
+    again = pltpu.make_async_copy(r.in_w_a, w_b.at[0:d_in], local.at[19])
+    again.start()
+    own3 = r.own3
+    spread(own3, [jnp.sum(acc[n, :, 0:d_mid], axis=0, keepdims=True) for n in range(2)])
+    started = total_start(net, place, own3, r.rows3)
+    sc["b"].batch()
+    total = total_finish(net, place, started, own3, r.rows3, r.mid3, r.batch3)
+    r.out_a_sums[...] = total
+    shift_a = gathered(total, 0, d_mid // 4) / total_count
+    gain_a = gathered(total, 1, d_mid // 4) / total_count
+    d_a, d_at = d_b.at[0], r.low_bt
+
+    @pl.loop(0, tiles)
+    def _(t):
+        at = pl.ds(pl.multiple_of(t * big, big), big)
+        grad = norm_a[2:3, :] * (
+            d_act[at, :] - shift_a - hat_a[at, :].astype(F32) * gain_a
+        )
+        d_a[at, :] = grad.astype(LOW)
+        d_at[:, at] = jnp.transpose(grad).astype(LOW)
+
+    reload.wait()
+    x = r.hat_c
+
+    @pl.loop(0, ranks)
+    def _(s):
+        shard_a(s)[...] = jnp.dot(
+            d_at[...],
+            x[:, pl.ds(pl.multiple_of(s * depth, depth), depth)],
+            preferred_element_type=F32,
+        ).astype(LOW)
+
+    sc["a"].pair()
+    sc["c"].line()
+    sc["b"].line()
+
+    for copy in kv:
+        copy.wait_recv()
+    own = pl.ds(pl.multiple_of(place.s * entry, entry), entry)
+    for n in range(2):
+        total = dkv[n, own, :].astype(F32)
+        for k in range(ranks - 1):
+            total = total + dkv_in[k, n].astype(F32)
+        dkv_own[n] = total.astype(LOW)
+        dkv_all[n, own, :] = total.astype(LOW)
+    every = [
+        net.push(dkv_own, dkv_all.at[:, own], peer)
+        for peer in place.row_peers()
+    ]
+    sc["a"].batch()
+    for copy in every:
+        copy.wait_recv()
+    kv_out, kv_in = r.kv_out, r.kv_in
+    for n in range(2):
+        kv_out[n] = tdot(bank_cols[...], dkv_all[n]).astype(LOW)
+    share = d_mid // groups
+    crossing = [
+        net.push(
+            kv_out.at[:, :, pl.ds(pl.multiple_of(peer[0] * share, share), share)], kv_in.at[k], peer
+        )
+        for k, peer in enumerate(place.batch_peers())
+    ]
+
+    again.wait()
+    out_x = r.out_x
+
+    def leave(t):
+        at = pl.ds(pl.multiple_of(t * tile, tile), tile)
+        return pltpu.make_async_copy(d_pre.at[at], out_x.at[at], local.at[21 + t])
+
+    @pl.loop(0, cells // tile)
+    def _(t):
+        at = pl.ds(pl.multiple_of(t * tile, tile), tile)
+        d_pre[at, :] = (
+            ndot(d_a[at, :], w_b[0:d_in, :]) + d_pre[at, :].astype(F32)
+        ).astype(LOW)
+        leave(t).start()
+
+    sc["a"].line()
+    for key in "qohcb":
+        sc[key].finish()
+    for copy in crossing:
+        copy.wait_recv()
+    for n, key in enumerate((r.out_k, r.out_v)):
+        total = kv_out[n, :, pl.ds(pl.multiple_of(place.g * share, share), share)].astype(F32)
+        for k in range(groups - 1):
+            total = total + kv_in[k, n].astype(F32)
+        key[...] = total
+    sc["a"].finish()
+
+    @pl.loop(0, cells // tile)
+    def _(t):
+        leave(t).wait()
+
+    @pl.loop(0, tiles)
+    def _(t):
+        @pl.when(jnp.logical_not(last))
+        def _():
+            halo(t, 0).wait_send()
+
+        @pl.when(jnp.logical_not(first))
+        def _():
+            halo(t, 1).wait_send()
+
+    net.close()
+
+
+class Gather:
+    def __init__(self, net, place, shard, whole, local):
+        self.net, self.place, self.shard, self.whole = net, place, shard, whole
+        self.rows = whole.shape[0] // place.ranks
+        self.own = pltpu.make_async_copy(shard, self.block(place.s), local)
+
+    def block(self, s):
+        return rows_of(self.whole, s, self.rows)
+
+    def quarter(self, s, g):
+        part = self.rows // self.place.groups
+        return self.whole.at[pl.ds(pl.multiple_of(s * self.rows + g * part, part), part)]
+
+    def line(self):
+        place = self.place
+        part = self.rows // place.groups
+        source = self.shard.at[pl.ds(pl.multiple_of(place.g * part, part), part)]
+        self.first = [
+            self.net.push(source, self.quarter(place.s, place.g), peer)
+            for peer in place.line_peers()
+        ]
+        self.own.start()
+        self.third = [self.net.push(self.shard, self.block(place.s), place.twin())]
+
+    def batch(self):
+        place = self.place
+        self.blocks = [
+            lax.rem(place.z + place.chips - k, place.chips) * 2 + place.core
+            for k in range(1, place.chips)
+        ]
+        self.second = []
+        for copy, s in zip(self.first, self.blocks):
+            copy.wait_recv()
+            view = self.quarter(s, place.g)
+            self.second.append(
+                [self.net.push(view, view, peer) for peer in place.batch_peers()]
+            )
+
+    def pair(self):
+        for copies, s in zip(self.second, self.blocks):
+            for copy in copies:
+                copy.wait_recv()
+            self.third.append(self.net.push(self.block(s), self.block(s), self.place.twin()))
+
+    def ready(self):
+        self.own.wait()
+        for copy in self.third:
+            copy.wait_recv()
+
+
+def moments(total, width, total_count):
+    centre = gathered(total, 0, width // 4) / total_count
+    square = gathered(total, 1, width // 4) / total_count
+    return centre, lax.rsqrt(square - centre * centre + 1e-05)
+
+
+def sigma(value):
+    return 0.5 * jnp.tanh(0.5 * value) + 0.5
+
+
+def forward_kernel(geometry, r):
+    cells, d_in, d_mid, columns, total_count, capacity, entries, samples = geometry
+    place = Place()
+    net = Wires(r.send, r.recv)
+    ranks, groups = place.ranks, place.groups
+    half, size = d_in // 2, 2 * capacity
+    depth = d_in // ranks
+    entry = r.bank16.shape[0]
+    local = r.local
+    load_x = pltpu.make_async_copy(r.features, r.x, local.at[0])
+    load_x.start()
+    greet(place.row_peers() + place.batch_peers())
+    a, b, c, q, o, h = (
+        Gather(net, place, shard, whole, local.at[n + 1])
+        for n, (shard, whole) in enumerate(
+            (
+                (r.w_reduce, r.w_a),
+                (r.w_spatial, r.w_b),
+                (r.w_expand, r.w_c),
+                (r.w_query, r.w_q),
+                (r.w_out, r.w_o),
+                (r.w_head, r.w_h),
+            )
+        )
+    )
+    a.line()
+
+    def at_block(s):
+        return pl.ds(pl.multiple_of(s * entry, entry), entry)
+
+    def at_depth(s):
+        return pl.ds(pl.multiple_of(s * depth, depth), depth)
+
+    asked = [
+        net.push(r.bank16.at[:, at_depth(peer[1])], rows_of(r.bank_cols, place.s, entry), peer)
+        for peer in place.row_peers()
+    ]
+    named = [
+        net.push(rows_of(r.box16, peer[1], size), rows_of(r.box_in, place.s, size), peer)
+        for peer in place.row_peers()
+    ]
+    r.bank_cols[at_block(place.s), :] = r.bank16[:, at_depth(place.s)]
+    mine = pl.ds(pl.multiple_of(place.s * size, size), size)
+    r.box_in[mine, :] = r.box16[mine, :]
+
+    strip = 64
+    lane = lax.rem(lax.broadcasted_iota(jnp.int32, (strip, ranks * size), 1), size)
+
+    @pl.loop(0, cells // strip)
+    def _(t):
+        at = pl.ds(pl.multiple_of(t * strip, strip), strip)
+        cell = lax.broadcasted_iota(jnp.int32, (strip, ranks * size), 0) + t * strip
+        total = jnp.zeros((strip, ranks * size), F32)
+        for j in range(samples):
+            total = total + jnp.where(
+                cell == r.slot_cells[j : j + 1, :], r.slot_weights[j : j + 1, :], 0.0
+            )
+        r.et[0, at, :] = jnp.where(lane < capacity, total, 0.0).astype(LOW)
+        r.et[1, at, :] = jnp.where(lane < capacity, 0.0, total).astype(LOW)
+
+    a.batch()
+    b.line()
+    for copy in asked:
+        copy.wait_recv()
+    for n, weight in enumerate((r.w_key, r.w_value)):
+        r.kv_part[n] = jnp.dot(r.bank_cols[...], weight[...], preferred_element_type=F32)
+    kv = [
+        net.push(r.kv_part.at[:, at_block(peer[1])], r.kv_in.at[k], peer)
+        for k, peer in enumerate(place.row_peers())
+    ]
+    a.pair()
+    b.batch()
+    c.line()
+    load_x.wait()
+    a.ready()
+
+    acc = r.acc
+    acc[...] = jnp.zeros_like(acc)
+    big = 256
+    tiles = cells // big
+
+    @pl.loop(0, tiles)
+    def _(t):
+        at = pl.ds(pl.multiple_of(t * big, big), big)
+        value = jnp.dot(r.x[at, :], r.w_a[...], preferred_element_type=F32)
+        r.pre_a[at, :] = value
+        acc[0, :, 0:d_mid] += folded(value)
+        acc[1, :, 0:d_mid] += folded(value * value)
+
+    spread(r.own1, [jnp.sum(acc[n, :, 0:d_mid], axis=0, keepdims=True) for n in range(2)])
+    started = total_start(net, place, r.own1, r.rows1)
+    keep_a = pltpu.make_async_copy(r.w_a, r.out_w_a, local.at[8])
+    keep_a.start()
+    total = total_finish(net, place, started, r.own1, r.rows1, r.mid1, r.batch1)
+    centre, inverse = moments(total, d_mid, total_count)
+    gain, bias = r.norm_a[0:1, :], r.norm_a[1:2, :]
+    r.out_norm_a[...] = r.norm_a[...]
+    r.out_norm_a[2:3, :] = gain * inverse
+
+    first, last = place.s == 0, place.s == ranks - 1
+    low_a, low_up, low_down = r.low_a, r.low_up, r.low_down
+
+    def halo(t, way):
+        at = pl.ds(pl.multiple_of(t * big, big), big)
+        return pltpu.make_async_remote_copy(
+            src_ref=low_a.at[at],
+            dst_ref=(low_up if way == 0 else low_down).at[at],
+            send_sem=r.halo_send.at[way, t],
+            recv_sem=r.halo_recv.at[way, t],
+            device_id=(place.g, place.s + 1 if way == 0 else place.s - 1),
+            device_id_type=MESH,
+        )
+
+    @pl.when(first)
+    def _():
+        low_up[...] = jnp.zeros_like(low_up)
+
+    @pl.when(last)
+    def _():
+        low_down[...] = jnp.zeros_like(low_down)
+
+    @pl.loop(0, tiles)
+    def _(t):
+        at = pl.ds(pl.multiple_of(t * big, big), big)
+        hat = (r.pre_a[at, :] - centre) * inverse
+        r.hat_a[at, :] = hat.astype(LOW)
+        act = gain * hat + bias
+        low_a[at, :] = (act * sigma(act)).astype(LOW)
+
+        @pl.when(jnp.logical_not(last))
+        def _():
+            halo(t, 0).start()
+
+        @pl.when(jnp.logical_not(first))
+        def _():
+            halo(t, 1).start()
+
+    keep_hat_a = pltpu.make_async_copy(r.hat_a, r.out_hat_a, local.at[9])
+    keep_hat_a.start()
+    b.pair()
+    c.batch()
+    q.line()
+
+    @pl.loop(0, tiles)
+    def _(t):
+        at = pl.ds(pl.multiple_of(t * big, big), big)
+        r.low_t[1, :, at] = jnp.transpose(low_a[at, :].astype(F32)).astype(LOW)
+
+    b.ready()
+    acc[...] = jnp.zeros_like(acc)
+
+    @pl.loop(0, tiles)
+    def _(t):
+        at = pl.ds(pl.multiple_of(t * big, big), big)
+
+        @pl.when(jnp.logical_not(first))
+        def _():
+            halo(t, 0).wait_recv()
+
+        @pl.when(jnp.logical_not(last))
+        def _():
+            halo(t, 1).wait_recv()
+
+        parts = []
+        for j in range(3):
+            taps = [r.w_b[(3 * i + j) * d_mid : (3 * i + j + 1) * d_mid, :] for i in range(3)]
+            parts.append(
+                jnp.dot(low_up[at, :], taps[0], preferred_element_type=F32)
+                + jnp.dot(low_a[at, :], taps[1], preferred_element_type=F32)
+                + jnp.dot(low_down[at, :], taps[2], preferred_element_type=F32)
+            )
+        value = from_left(parts[0], columns) + parts[1] + from_right(parts[2], columns)
+        r.pre_b[at, :] = value
+        acc[0, :, 0:d_mid] += folded(value)
+        acc[1, :, 0:d_mid] += folded(value * value)
+
+    spread(r.own2, [jnp.sum(acc[n, :, 0:d_mid], axis=0, keepdims=True) for n in range(2)])
+    started = total_start(net, place, r.own2, r.rows2)
+    keep_b = pltpu.make_async_copy(r.w_b, r.out_w_b, local.at[10])
+    keep_b.start()
+
+    @pl.loop(0, tiles)
+    def _(t):
+        at = pl.ds(pl.multiple_of(t * big, big), big)
+        r.low_t[0, :, at] = jnp.transpose(low_up[at, :].astype(F32)).astype(LOW)
+        r.low_t[2, :, at] = jnp.transpose(low_down[at, :].astype(F32)).astype(LOW)
+
+    keep_low_t = pltpu.make_async_copy(r.low_t, r.out_low_t, local.at[11])
+    keep_low_t.start()
+    total = total_finish(net, place, started, r.own2, r.rows2, r.mid2, r.batch2)
+    centre, inverse = moments(total, d_mid, total_count)
+    gain, bias = r.norm_b[0:1, :], r.norm_b[1:2, :]
+    r.out_norm_b[...] = r.norm_b[...]
+    r.out_norm_b[2:3, :] = gain * inverse
+    c.pair()
+    q.batch()
+    o.line()
+    h.line()
+    c.ready()
+    acc[...] = jnp.zeros_like(acc)
+
+    @pl.loop(0, tiles)
+    def _(t):
+        at = pl.ds(pl.multiple_of(t * big, big), big)
+        hat = (r.pre_b[at, :] - centre) * inverse
+        r.hat_b[at, :] = hat.astype(LOW)
+        act = gain * hat + bias
+        low = (act * sigma(act)).astype(LOW)
+        r.low_b[at, :] = low
+        for k in range(4):
+            on = slice(k * (d_in // 4), (k + 1) * (d_in // 4))
+            value = jnp.dot(low, r.w_c[:, on], preferred_element_type=F32)
+            r.pre_c[at, on] = value
+            acc[0, :, on] += folded(value)
+            acc[1, :, on] += folded(value * value)
+
+    keep_c = pltpu.make_async_copy(r.w_c, r.out_w_c, local.at[12])
+    keep_c.start()
+    keep_hat_b = pltpu.make_async_copy(r.hat_b, r.out_hat_b, local.at[13])
+    keep_hat_b.start()
+    spread(r.own3, [jnp.sum(acc[n], axis=0, keepdims=True) for n in range(2)])
+    started = total_start(net, place, r.own3, r.rows3)
+
+    for copy in kv:
+        copy.wait_recv()
+    for n in range(2):
+        total = r.kv_part[n, at_block(place.s), :]
+        for k in range(ranks - 1):
+            total = total + r.kv_in[k, n]
+        r.kv_own[n] = total.astype(LOW)
+        r.kv_all[n, at_block(place.s), :] = total.astype(LOW)
+    every = [
+        net.push(r.kv_own, r.kv_all.at[:, at_block(place.s)], peer) for peer in place.row_peers()
+    ]
+
+    @pl.loop(0, tiles)
+    def _(t):
+        at = pl.ds(pl.multiple_of(t * big, big), big)
+        r.low_bt[:, at] = jnp.transpose(r.low_b[at, :].astype(F32)).astype(LOW)
+
+    keep_low_bt = pltpu.make_async_copy(r.low_bt, r.out_low_bt, local.at[14])
+    keep_low_bt.start()
+    total = total_finish(net, place, started, r.own3, r.rows3, r.mid3, r.batch3)
+    centre, inverse = moments(total, d_in, total_count)
+    r.scale_c[...] = r.norm_c[0:1, :] * inverse
+    r.centre_c[0:1, :] = centre
+    r.centre_c[1:2, :] = inverse
+    q.pair()
+    o.batch()
+    h.batch()
+    r.pieces[...] = jnp.zeros_like(r.pieces)
+    tile = 128
+
+    @pl.loop(0, cells // tile)
+    def _(t):
+        at = pl.ds(pl.multiple_of(t * tile, tile), tile)
+        for k in range(4):
+            on = slice(k * (d_in // 4), (k + 1) * (d_in // 4))
+            into = slice((k % 2) * (d_in // 4), (k % 2 + 1) * (d_in // 4))
+            hat = (r.pre_c[at, on] - r.centre_c[0:1, on]) * r.centre_c[1:2, on]
+            r.hat_c[at, on] = hat.astype(LOW)
+            value = r.norm_c[0:1, on] * hat + r.norm_c[1:2, on] + r.x[at, on].astype(F32)
+            sig = sigma(value)
+            fmap = value * sig
+            r.x[at, on] = (sig + fmap * (1.0 - sig)).astype(LOW)
+            r.pieces[:, into] += tdot(r.et[k // 2, at, :], fmap.astype(LOW))
+
+    keep_hat_c = pltpu.make_async_copy(r.hat_c, r.out_hat_c, local.at[15])
+    keep_hat_c.start()
+    keep_slope = pltpu.make_async_copy(r.x, r.out_slope, local.at[16])
+    keep_slope.start()
+    r.blocks[...] = r.pieces[...].astype(LOW)
+    pushed = [
+        net.push(rows_of(r.blocks, peer[1], size), rows_of(r.arrived, place.s, size), peer)
+        for peer in place.row_peers()
+    ]
+    r.arrived[mine, :] = r.blocks[mine, :]
+    o.pair()
+    h.pair()
+    for copy in named + every + pushed:
+        copy.wait_recv()
+
+    boxes = r.windows.shape[0]
+    slot = lax.rem(lax.broadcasted_iota(jnp.int32, (ranks * size, boxes), 0), size)
+    hit = r.box_in[...] == lax.broadcasted_iota(jnp.int32, (ranks * size, boxes), 1)
+    picks = [
+        jnp.where(hit & (slot < capacity), 1.0, 0.0).astype(LOW),
+        jnp.where(hit & (slot >= capacity), 1.0, 0.0).astype(LOW),
+    ]
+    for k in range(2):
+        r.pooled[:, k * half : (k + 1) * half] = tdot(picks[k], r.arrived[...])
+    r.joined[:, 0:d_in] = r.pooled[...].astype(LOW)
+    pooled_low = r.joined.at[:, 0:d_in]
+    keys, vals = r.kv_all.at[0], r.kv_all.at[1]
+    scale = d_mid ** (-0.5)
+    q.ready()
+    queries = jnp.dot(pooled_low[...], r.w_q[...], preferred_element_type=F32).astype(LOW)
+    scores = jnp.where(r.windows[...] > 0, ndot(queries, keys[...]) * scale, -1e30)
+    raised = jnp.exp(scores - jnp.max(scores, axis=1, keepdims=True))
+    attend = raised / jnp.sum(raised, axis=1, keepdims=True)
+    attend_low = attend.astype(LOW)
+    mixture = jnp.dot(attend_low, vals[...], preferred_element_type=F32)
+    centred = mixture - jnp.mean(mixture, axis=1, keepdims=True)
+    inverse_z = lax.rsqrt(jnp.mean(centred * centred, axis=1, keepdims=True) + 1e-05)
+    hat_z = centred * inverse_z
+    pre_ln = r.norm_z[0:1, :] * hat_z + r.norm_z[1:2, :]
+    sig_z = sigma(pre_ln)
+    low_r = (pre_ln * sig_z).astype(LOW)
+    slope_z = sig_z * (1.0 + pre_ln * (1.0 - sig_z))
+    o.ready()
+    for k in range(4):
+        on = slice(k * (d_in // 4), (k + 1) * (d_in // 4))
+        into = slice(d_in + k * (d_in // 4), d_in + (k + 1) * (d_in // 4))
+        r.joined[:, into] = (
+            r.pooled[:, on] + jnp.dot(low_r, r.w_o[:, on], preferred_element_type=F32)
+        ).astype(LOW)
+    h.ready()
+    logits = (
+        jnp.dot(r.joined[...], r.w_h[...], preferred_element_type=F32) + r.head_bias[...]
+    )
+    likely = jax.nn.sigmoid(logits)
+    r.out_probs[...] = likely
+    d_logit = (r.cotangent[...] * (likely * (1.0 - likely))).astype(LOW)
+    for k in range(4):
+        on = slice(k * (d_in // 4), (k + 1) * (d_in // 4))
+        below = slice(d_in + k * (d_in // 4), d_in + (k + 1) * (d_in // 4))
+        upper = ndot(d_logit, r.w_h[below, :])
+        r.d_branch[:, on] = upper.astype(LOW)
+        r.pooled[:, on] = ndot(d_logit, r.w_h[on, :]) + upper
+    d_ln = ndot(r.d_branch[...], r.w_o[...]) * slope_z
+    d_hat = d_ln * r.norm_z[0:1, :]
+    d_mixture = (
+        inverse_z
+        * (
+            d_hat
+            - jnp.mean(d_hat, axis=1, keepdims=True)
+            - hat_z * jnp.mean(d_hat * hat_z, axis=1, keepdims=True)
+        )
+    ).astype(LOW)
+    d_attend = ndot(d_mixture, vals[...])
+    d_scores = (attend * (d_attend - jnp.sum(d_attend * attend, axis=1, keepdims=True))).astype(LOW)
+    d_queries = (jnp.dot(d_scores, keys[...], preferred_element_type=F32) * scale).astype(LOW)
+    for k in range(4):
+        on = slice(k * (d_in // 4), (k + 1) * (d_in // 4))
+        r.d_pooled[:, on] = (r.pooled[:, on] + ndot(d_queries, r.w_q[on, :])).astype(LOW)
+    r.blocks_out[...] = (
+        jnp.dot(picks[0], r.d_pooled[:, 0:half], preferred_element_type=F32)
+        + jnp.dot(picks[1], r.d_pooled[:, half:d_in], preferred_element_type=F32)
+    ).astype(LOW)
+    returned = [
+        net.push(rows_of(r.blocks_out, peer[1], size), rows_of(r.back_in, place.s, size), peer)
+        for peer in place.row_peers()
+    ]
+    r.back_in[mine, :] = r.blocks_out[mine, :]
+
+    r.out_dkv[0] = (tdot(d_scores, queries) * scale).astype(LOW)
+    r.out_dkv[1] = tdot(attend_low, d_mixture).astype(LOW)
+    for k in range(4):
+        on = slice(k * (d_in // 4), (k + 1) * (d_in // 4))
+        r.g_q[on, :] = tdot(r.joined[:, on], d_queries).astype(LOW)
+        r.g_o[:, on] = tdot(low_r, r.d_branch[:, on]).astype(LOW)
+    width = 2 * depth
+    for s in range(ranks):
+        r.g_h[s] = tdot(d_logit, r.joined[:, s * width : (s + 1) * width]).astype(LOW)
+    keeps = []
+    for n, (source, target) in enumerate(((r.g_q, r.out_g_q), (r.g_o, r.out_g_o), (r.g_h, r.out_g_h))):
+        keeps.append(pltpu.make_async_copy(source, target, local.at[17 + n]))
+        keeps[-1].start()
+    quarter = d_mid // 4
+    r.out_head_part[...] = jnp.zeros_like(r.out_head_part)
+    for n, value in enumerate(
+        (jnp.sum(d_ln * hat_z, axis=0, keepdims=True), jnp.sum(d_ln, axis=0, keepdims=True))
+    ):
+        for k in range(4):
+            r.out_head_part[4 * n + k : 4 * n + k + 1, d_in // 4 : d_in // 4 + quarter] = value[
+                :, k * quarter : (k + 1) * quarter
+            ]
+    classes = d_logit.shape[1]
+    r.out_head_part[0:1, d_in // 4 + quarter : d_in // 4 + quarter + classes] = jnp.sum(
+        d_logit.astype(F32), axis=0, keepdims=True
+    )
+    for copy in keeps + [
+        keep_a, keep_hat_a, keep_b, keep_low_t, keep_c, keep_hat_b, keep_low_bt, keep_hat_c, keep_slope
+    ]:
+        copy.wait()
+    for copy in returned:
+        copy.wait_recv()
+    r.out_back[...] = r.back_in[...]
+    r.bank_cols_out[...] = r.bank_cols[...]
+
+    @pl.loop(0, tiles)
+    def _(t):
+        @pl.when(jnp.logical_not(last))
+        def _():
+            halo(t, 0).wait_send()
+
+        @pl.when(jnp.logical_not(first))
+        def _():
+            halo(t, 1).wait_send()
+
+    net.close()
+
+
+class Refs:
+    def __init__(self, names, refs):
+        self.__dict__.update(zip(names, refs))
+
+
+def run_kernel(body, geometry, channel, held, far, outs, far_outs, scratch):
+    anywhere = pl.BlockSpec(memory_space=pl.ANY)
+    inside = pl.BlockSpec(memory_space=pltpu.VMEM)
+    names = [*held, *far, *outs, *far_outs, *scratch]
+    results = pl.pallas_call(
+        lambda *refs: body(geometry, Refs(names, refs)),
+        out_shape=(*outs.values(), *far_outs.values()),
+        in_specs=[inside] * len(held) + [anywhere] * len(far),
+        out_specs=(inside,) * len(outs) + (anywhere,) * len(far_outs),
+        scratch_shapes=[*scratch.values()],
+        compiler_params=pltpu.CompilerParams(
+            collective_id=channel, has_side_effects=True, vmem_limit_bytes=64 << 20
+        ),
+    )(*held.values(), *far.values())
+    return Refs([*outs, *far_outs], results)
+
+
+def shape(kind, *sizes):
+    return jax.ShapeDtypeStruct(sizes, kind)
+
+
+def room(kind, *sizes):
+    return pltpu.VMEM(sizes, kind)
+
+
+def sums_room(scratch, ranks, groups, widths):
+    for n, width in widths:
+        scratch["own%d" % n] = room(F32, 8, width)
+        scratch["mid%d" % n] = room(F32, 8, width)
+        scratch["rows%d" % n] = room(F32, ranks - 1, 8, width)
+        scratch["batch%d" % n] = room(F32, groups - 1, 8, width)
+    return scratch
+
+
+def wires_room(cells):
+    dma = pltpu.SemaphoreType.DMA
+    return dict(
+        halo_send=dma((2, cells // 256)),
+        halo_recv=dma((2, cells // 256)),
+        local=dma((32,)),
+        send=dma((256,)),
+        recv=dma((256,)),
+    )
+
+
+def run_forward(geometry, held, far):
+    cells, d_in, d_mid, columns, total_count, capacity, entries, samples = geometry
+    groups, ranks = lax.axis_size("batch"), lax.axis_size("rows")
+    slots = ranks * 2 * capacity
+    entry = held["bank16"].shape[0]
+    bank = ranks * entry
+    boxes = held["windows"].shape[0]
+    classes = held["head_bias"].shape[1]
+    spatial = far["w_spatial"].shape[0] * ranks
+    half = d_in // 2
+    outs = dict(
+        out_norm_a=shape(F32, 8, d_mid),
+        out_norm_b=shape(F32, 8, d_mid),
+        scale_c=shape(F32, 1, d_in),
+        out_probs=shape(F32, boxes, classes),
+        out_dkv=shape(LOW, 2, bank, d_mid),
+        out_back=shape(LOW, slots, half),
+        out_head_part=shape(F32, 8, d_in // 4 + d_mid // 4 + classes),
+        et=shape(LOW, 2, cells, slots),
+        bank_cols_out=shape(LOW, bank, d_in // ranks),
+    )
+    far_outs = dict(
+        out_w_a=shape(LOW, d_in, d_mid),
+        out_w_b=shape(LOW, spatial, d_mid),
+        out_w_c=shape(LOW, d_mid, d_in),
+        out_hat_a=shape(LOW, cells, d_mid),
+        out_hat_b=shape(LOW, cells, d_mid),
+        out_hat_c=shape(LOW, cells, d_in),
+        out_slope=shape(LOW, cells, d_in),
+        out_low_t=shape(LOW, 3, d_mid, cells),
+        out_low_bt=shape(LOW, d_mid, cells),
+        out_g_q=shape(LOW, d_in, d_mid),
+        out_g_o=shape(LOW, d_mid, d_in),
+        out_g_h=shape(LOW, ranks, classes, 2 * d_in // ranks),
+    )
+    scratch = dict(
+        x=room(LOW, cells, d_in),
+        w_a=room(LOW, d_in, d_mid),
+        w_b=room(LOW, spatial, d_mid),
+        w_c=room(LOW, d_mid, d_in),
+        w_q=room(LOW, d_in, d_mid),
+        w_o=room(LOW, d_mid, d_in),
+        w_h=room(LOW, 2 * d_in, classes),
+        bank_cols=room(LOW, bank, d_in // ranks),
+        box_in=room(jnp.int32, slots, boxes),
+        kv_part=room(F32, 2, bank, d_mid),
+        kv_in=room(F32, ranks - 1, 2, entry, d_mid),
+        kv_own=room(LOW, 2, entry, d_mid),
+        kv_all=room(LOW, 2, bank, d_mid),
+        acc=room(F32, 2, 8, d_in),
+        pre_a=room(F32, cells, d_mid),
+        hat_a=room(LOW, cells, d_mid),
+        low_a=room(LOW, cells, d_mid),
+        low_up=room(LOW, cells, d_mid),
+        low_down=room(LOW, cells, d_mid),
+        low_t=room(LOW, 3, d_mid, cells),
+        pre_b=room(F32, cells, d_mid),
+        hat_b=room(LOW, cells, d_mid),
+        low_b=room(LOW, cells, d_mid),
+        low_bt=room(LOW, d_mid, cells),
+        pre_c=room(F32, cells, d_in),
+        hat_c=room(LOW, cells, d_in),
+        centre_c=room(F32, 8, d_in),
+        pieces=room(F32, slots, half),
+        blocks=room(LOW, slots, half),
+        arrived=room(LOW, slots, half),
+        pooled=room(F32, boxes, d_in),
+        joined=room(LOW, boxes, 2 * d_in),
+        d_branch=room(LOW, boxes, d_in),
+        d_pooled=room(LOW, boxes, d_in),
+        blocks_out=room(LOW, slots, half),
+        back_in=room(LOW, slots, half),
+        g_q=room(LOW, d_in, d_mid),
+        g_o=room(LOW, d_mid, d_in),
+        g_h=room(LOW, ranks, classes, 2 * d_in // ranks),
+        **wires_room(cells),
+    )
+    sums_room(scratch, ranks, groups, ((1, d_mid // 4), (2, d_mid // 4), (3, d_in // 4)))
+    return run_kernel(forward_kernel, geometry, 11, held, far, outs, far_outs, scratch)
+
+
+def run_backward(geometry, held, far):
+    cells, d_in, d_mid, columns, total_count, capacity, entries, samples = geometry
+    groups, ranks = lax.axis_size("batch"), lax.axis_size("rows")
+    chips = ranks // 2
+    slots = ranks * 2 * capacity
+    depth = d_in // ranks
+    entry = held["bank_cols"].shape[0] // ranks
+    spatial = far["in_w_b"].shape[0]
+    classes = far["in_g_h"].shape[1]
+    share = dict(
+        q=(d_in // ranks, d_mid // groups),
+        o=(d_mid // ranks, d_in // groups),
+        h=(classes // groups, 2 * d_in // ranks),
+        c=(d_mid // ranks, d_in // groups),
+        b=(spatial // ranks, d_mid // groups),
+        a=(d_mid // groups, d_in // ranks),
+    )
+    block = dict(
+        q=(d_in // ranks, d_mid),
+        o=(d_mid // ranks, d_in),
+        h=(classes, 2 * d_in // ranks),
+        c=(d_mid // ranks, d_in),
+        b=(spatial // ranks, d_mid),
+        a=(d_mid, d_in // ranks),
+    )
+    head = held["head_part"].shape[1]
+    outs = dict(
+        out_head=shape(F32, 8, head),
+        out_b_sums=shape(F32, 8, d_mid // 4),
+        out_a_sums=shape(F32, 8, d_mid // 4),
+        out_k=shape(F32, depth, d_mid // groups),
+        out_v=shape(F32, depth, d_mid // groups),
+    )
+    scratch = dict(
+        hat_c=room(LOW, cells, d_in),
+        slope=room(LOW, cells, d_in),
+        d_pre=room(LOW, cells, d_in),
+        w_c=room(LOW, d_mid, d_in),
+        hat_b=room(LOW, cells, d_mid),
+        low_bt=room(LOW, d_mid, cells),
+        low_t=room(LOW, 3, d_mid, cells),
+        w_b=room(LOW, spatial, d_mid),
+        g_q=room(LOW, d_in, d_mid),
+        g_o=room(LOW, d_mid, d_in),
+        g_h=room(LOW, ranks, classes, 2 * d_in // ranks),
+        g_c=room(LOW, d_mid, d_in),
+        g_b=room(LOW, spatial, d_mid),
+        d_act=room(F32, cells, d_mid),
+        d_b=room(LOW, 3, cells, d_mid),
+        d_up=room(LOW, cells, d_mid),
+        d_down=room(LOW, cells, d_mid),
+        acc=room(F32, 2, 8, d_in),
+        dkv_in=room(LOW, ranks - 1, 2, entry, d_mid),
+        dkv_own=room(LOW, 2, entry, d_mid),
+        dkv_all=room(LOW, 2, ranks * entry, d_mid),
+        kv_out=room(LOW, 2, depth, d_mid),
+        kv_in=room(LOW, groups - 1, 2, depth, d_mid // groups),
+        **wires_room(cells),
+    )
+    sums_room(scratch, ranks, groups, ((1, head), (2, d_mid // 4), (3, d_mid // 4)))
+    for key in share:
+        outs["out_" + key] = shape(F32, *share[key])
+        scratch["tw_" + key] = room(LOW, chips, *block[key])
+        scratch["ba_" + key] = room(LOW, groups - 1, chips, *share[key])
+        scratch["pa_" + key] = room(LOW, chips, *share[key])
+        scratch["li_" + key] = room(LOW, chips - 1, *share[key])
+    far_outs = dict(out_x=shape(LOW, cells, d_in))
+    return run_kernel(backward_kernel, geometry, 12, held, far, outs, far_outs, scratch)
+
+
+def fused_device(
+    features,
+    w_reduce,
+    w_spatial,
+    w_expand,
+    query_weight,
+    w_key,
+    w_value,
+    w_out,
+    w_head,
+    gain_a,
+    bias_a,
+    gain_b,
+    bias_b,
+    gain_c,
+    bias_c,
+    ln_gain,
+    ln_bias,
+    head_bias,
+    bank,
+    piece_box,
+    piece_clip,
+    send_count,
+    sample_pos,
+    sample_weight,
+    win_start,
+    win_len,
+    prob_cotangent,
+):
+    groups, ranks = lax.axis_size("batch"), lax.axis_size("rows")
+    clip_dev, row_dev, columns, d_in = features.shape
+    d_mid = w_reduce.shape[1]
+    cells = clip_dev * row_dev * columns
+    total_count = cells * ranks * groups
+    capacity = piece_box.shape[1]
+    samples = sample_pos.shape[1] // capacity
+    entries = bank.shape[0]
+    entry = -(-entries // 16) * 16
+    classes = head_bias.shape[0]
+    class_share = classes // groups
+    geometry = (cells, d_in, d_mid, columns, total_count, capacity, entries, samples)
+    twice = lambda v: jnp.concatenate([v, v], axis=-1)
+
+    def by_class(value):
+        rows = value.reshape(-1, groups, class_share)
+        return jnp.pad(rows, ((0, 0), (0, 0), (0, 32 - class_share))).reshape(-1, groups * 32)
+
+    def from_class(value):
+        rows = value.reshape(-1, groups, 32)[:, :, :class_share]
+        return rows.reshape(-1, classes)
+
+    def stacked(*rows):
+        return jnp.pad(jnp.stack(rows), ((0, 8 - len(rows)), (0, 0)))
+
+    def by_slot(value):
+        rows = value.reshape(ranks, capacity, samples).transpose(2, 0, 1)
+        rows = twice(rows).reshape(samples, ranks * 2 * capacity)
+        return jnp.pad(rows, ((0, -samples % 8), (0, 0)))
+
+    at_clip = jnp.repeat(piece_clip * (row_dev * columns), samples, axis=1)
+    is_live = (jnp.arange(capacity)[None, :] < send_count[:, None]).astype(F32)
+    live = jnp.repeat(is_live, samples, axis=1)
+    boxes = win_start.shape[0]
+    box16 = jnp.broadcast_to(
+        twice(piece_box).reshape(ranks * 2 * capacity, 1), (ranks * 2 * capacity, boxes)
+    )
+    spot = jnp.arange(ranks * entry)
+    position = spot // entry * entries + spot % entry
+    windows = (
+        (spot % entry < entries)
+        & (position >= win_start[:, None])
+        & (position < (win_start + win_len)[:, None])
+    ).astype(jnp.int32)
+    held = dict(
+        bank16=jnp.pad(bank, ((0, entry - entries), (0, 0))),
+        box16=box16,
+        slot_cells=by_slot(at_clip + sample_pos),
+        slot_weights=by_slot(sample_weight * live),
+        w_key=w_key,
+        w_value=w_value,
+        norm_a=stacked(gain_a, bias_a),
+        norm_b=stacked(gain_b, bias_b),
+        norm_c=stacked(gain_c, bias_c),
+        norm_z=stacked(ln_gain, ln_bias),
+        windows=windows,
+        head_bias=by_class(head_bias),
+        cotangent=by_class(prob_cotangent),
+    )
+    far = dict(
+        features=features.reshape(cells, d_in),
+        w_reduce=w_reduce,
+        w_spatial=w_spatial,
+        w_expand=w_expand,
+        w_query=query_weight,
+        w_out=w_out,
+        w_head=by_class(w_head),
+    )
+    one = run_forward(geometry, held, far)
+    back_held = dict(
+        back=one.out_back,
+        et=one.et,
+        dkv=one.out_dkv,
+        bank_cols=one.bank_cols_out,
+        head_part=one.out_head_part,
+        scale_c=one.scale_c,
+        norm_b=one.out_norm_b,
+        norm_a=one.out_norm_a,
+    )
+    back_far = dict(
+        in_hat_c=one.out_hat_c,
+        in_slope=one.out_slope,
+        in_w_c=one.out_w_c,
+        in_hat_b=one.out_hat_b,
+        in_low_bt=one.out_low_bt,
+        in_low_t=one.out_low_t,
+        in_w_b=one.out_w_b,
+        in_hat_a=one.out_hat_a,
+        in_w_a=one.out_w_a,
+        in_x=far["features"],
+        in_g_q=one.out_g_q,
+        in_g_o=one.out_g_o,
+        in_g_h=one.out_g_h,
+    )
+    two = run_backward(geometry, back_held, back_far)
+    head, wide, quarter = two.out_head, d_in // 4, d_mid // 4
+    b_sums, a_sums = two.out_b_sums.reshape(2, d_mid), two.out_a_sums.reshape(2, d_mid)
+    return (
+        from_class(one.out_probs),
+        two.out_x.reshape(features.shape),
+        two.out_a.T,
+        two.out_b,
+        two.out_c,
+        two.out_q,
+        two.out_k,
+        two.out_v,
+        two.out_o,
+        two.out_h[:class_share].T,
+        a_sums[1],
+        a_sums[0],
+        b_sums[1],
+        b_sums[0],
+        head[4:8, :wide].reshape(d_in),
+        head[0:4, :wide].reshape(d_in),
+        head[0:4, wide : wide + quarter].reshape(d_mid),
+        head[4:8, wide : wide + quarter].reshape(d_mid),
+        from_class(head[0:1, wide + quarter :]).reshape(classes),
+    )
+
+
+def plain_normalize(field, total_count):
     sums, squares = lax.psum((jnp.sum(field, 0), jnp.sum(field * field, 0)), ("batch", "rows"))
     centre_value = sums / total_count
     inverse = lax.rsqrt(squares / total_count - centre_value * centre_value + 1e-05)
     return ((field - centre_value) * inverse, inverse)
 
 
-def segment_totals(grad, normed):
+def plain_totals(grad, normed):
     return lax.psum((jnp.sum(grad, 0), jnp.sum(grad * normed, 0)), ("batch", "rows"))
 
 
-def norm_back(grad, normed, inverse, gain, shift_sum, gain_total_grad, total_count):
-    return (
-        gain * inverse * (grad - shift_sum / total_count - normed * gain_total_grad / total_count)
-    )
-
-
-def on_device(
+def plain_device(
     features,
     w_reduce,
     w_spatial,
@@ -122,7 +1456,7 @@
     d_mid = w_a.shape[1]
     flat_x = features.reshape(cell_count, d_in)
     pre_a = jnp.dot(flat_x, w_a, preferred_element_type=jnp.float32)
-    hat_a, inverse_a = normalize(pre_a, total_count)
+    hat_a, inverse_a = plain_normalize(pre_a, total_count)
     act_a = gain_a * hat_a + bias_a
     low_a = jax.nn.silu(act_a).astype(jnp.bfloat16)
     halo_a = padded(low_a.reshape(clip_dev, row_dev, col_count, d_mid), (("rows", 1),), 1)
@@ -136,11 +1470,11 @@
         axis=3,
     ).reshape(cell_count, 9 * d_mid)
     pre_b = jnp.dot(window_a, w_b, preferred_element_type=jnp.float32)
-    hat_b, inverse_b = normalize(pre_b, total_count)
+    hat_b, inverse_b = plain_normalize(pre_b, total_count)
     act_b = gain_b * hat_b + bias_b
     low_b = jax.nn.silu(act_b).astype(jnp.bfloat16)
     pre_c = jnp.dot(low_b, w_c, preferred_element_type=jnp.float32)
-    hat_c, inverse_c = normalize(pre_c, total_count)
+    hat_c, inverse_c = plain_normalize(pre_c, total_count)
     pre_out = gain_c * hat_c + bias_c + flat_x.astype(jnp.float32)
     fmap = jax.nn.silu(pre_out).astype(jnp.bfloat16)
     capacity = piece_box.shape[1]
@@ -251,7 +1585,7 @@
     ).astype(jnp.bfloat16)
     grad_wc = tdot(low_b, d_c)
     d_act_b = ndot(d_c, w_c) * silu_slope(act_b)
-    shift_b_sum, gain_b_sum = segment_totals(d_act_b, hat_b)
+    shift_b_sum, gain_b_sum = plain_totals(d_act_b, hat_b)
     d_b = norm_back(d_act_b, hat_b, inverse_b, gain_b, shift_b_sum, gain_b_sum, total_count).astype(
         jnp.bfloat16
     )
@@ -270,7 +1604,7 @@
     ).reshape(cell_count, 9 * d_mid)
     flipped = w_b.reshape(9, d_mid, d_mid).transpose(0, 2, 1).reshape(9 * d_mid, d_mid)
     d_act_a = jnp.dot(window_d, flipped, preferred_element_type=jnp.float32) * silu_slope(act_a)
-    shift_a_sum, gain_a_sum = segment_totals(d_act_a, hat_a)
+    shift_a_sum, gain_a_sum = plain_totals(d_act_a, hat_a)
     d_a = norm_back(d_act_a, hat_a, inverse_a, gain_a, shift_a_sum, gain_a_sum, total_count).astype(
         jnp.bfloat16
     )
@@ -333,6 +1667,11 @@
         head_sums[3],
         head_sums[4],
     )
+
+
+def on_device(*args):
+    fits = all(a.shape[0] % 64 == 0 for a in args[1:9]) and lax.axis_size("rows") % 2 == 0
+    return (fused_device if fits else plain_device)(*args)
 
 
 def solution(mesh):

time: 1020 us -> 316 us (0.31)
  waiting for transfers between devices: 395 us -> 0 us
  blocking collectives: 364 us -> 0 us
  Pallas kernels: 0 us -> 274 us
  matrix products: 128 us -> 0 us
  other arithmetic: 43.2 us -> 9.78 us
  starting transfers between devices: 18.9 us -> 0 us
  between operations: 17.1 us -> 0.75 us
  local copies, waits for them, and re-layouts: 45.6 us -> 29.6 us
    reduce_scatter x13 -> x0, waiting for transfers between devices: 285 us -> none  [the longest x1 98 us: on_device(): lax.psum_scatter(grad_wb, 'rows', scatter_dimension=0, tiled=True)]
    pallas_call x0 -> x2, Pallas kernels: none -> 274 us  [run_kernel(): pl.pallas_call(lambda *refs: body(geometry, Refs(names, refs)), out_shape...]
    psum x6 -> x0, blocking collectives: 261 us -> none  [the longest x3 126 us: normalize(): lax.psum((jnp.sum(field, 0), jnp.sum(field * field, 0)), ('batch', 'rows'))]
    dot_general x31 -> x0, matrix products: 128 us -> none  [the longest x11 49.2 us: tdot(): lax.dot_general(left, right, (((0,), (0,)), ((), ())), preferred_element_...]
    unnamed x26 -> x0, waiting for transfers between devices: 88.4 us -> none
    all_gather x3 -> x0, blocking collectives: 69.4 us -> none  [the longest x1 39.7 us: on_device(): lax.all_gather(w_head, 'rows', axis=0, tiled=True)]
    all_to_all x2 -> x0, blocking collectives: 33.3 us -> none  [the longest x1 17 us: on_device(): lax.all_to_all(back_pieces, 'rows', split_axis=0, concat_axis=0, tiled=True)]
    convert_element_type x20 -> x2, other arithmetic: 32.3 us -> 2.11 us  [the longest x1 1.39 us: fused_device(): windows = ((spot % entry < entries) & (position >= win_start[:, None]) &...]
  transfers between devices with their start and end apart: 29 -> 0, of which waited for: 12 -> 0; matrix products, arithmetic and copies ran while one was open for 20% -> 0% of each run, Pallas kernels for 0% -> 0%
where the time goes in v2:
time: 316 us; the launch traced here: 314 us
  Pallas kernels  274 us (87%)
  local copies, waits for them, and re-layouts  29.6 us (9%)
  other arithmetic  9.78 us (3%)
    pallas_call x2, Pallas kernels, run_kernel(): pl.pallas_call(lambda *refs: body(geometry, Refs(names, refs)), out_shape...  274 us
    unnamed x23, local copies, waits for them, and re-layouts  12.5 us

profile of v2, /device:TPU:0, one launch (start us, length us, event | category | flops | bytes accessed | tf_op | source)
XLA Modules:
  0.0 314.1 jit_solution(5674839632605849262)
XLA Ops:
  1.3 0.7 reshape.148
  2.7 0.8 pad_add_fusion.1
  4.3 0.7 fusion
  5.0 1.3 select_maximum_fusion.3.refs_6_
  7.4 0.7 add.59
  9.6 1.3 select_maximum_fusion.1
  11.0 0.8 reshape.150
  11.8 0.7 copy.55.refs_12_
  12.5 1.4 and_convert_fusion.refs_10_
  14.6 1.4 select_maximum_fusion.refs_8_
  16.0 1.5 pad.38.refs_0_
  17.4 0.9 reshape.153
  18.4 0.8 copy.56.refs_19_
  19.1 123.1 %shard_map.402 = (f32[8,512]{1,0:T(8,128)}, f32[8,512]{1,0:T(8,128)}, f32[1,2048]{1,0:T(1,128)}, f32[128,128]{1,0:T(8,128)}, bf16[2,128,512]{2,1,0:T(8,128)(2,1)...) custom-call(bf16[16,2048]{1,0:T(8,128)(2,1)} %pad.38.refs_0_, ...), custom_call_target="tpu_custom_call" | custom-call | tf_op jit(solution)/shard_map/pallas_call | solution.py:1061
  142.3 0.9 copy.57
  143.8 150.9 %shard_map.403 = (f32[8,768]{1,0:T(8,128)}, f32[8,128]{1,0:T(8,128)}, f32[8,128]{1,0:T(8,128)}, f32[256,128]{1,0:T(8,128)}, f32[256,128]{1,0:T(8,128)}, /*index=...) custom-call(bf16[128,1024]{1,0:T(8,128)(2,1)} %get-tuple-element.53., ...), custom_call_target="tpu_custom_call" | custom-call | tf_op jit(solution)/shard_map/pallas_call | solution.py:1061
  294.7 1.7 copy.59
  297.8 1.3 slice_bitcast_fusion.7
  299.1 1.3 slice_bitcast_fusion.5
  300.4 1.3 slice_bitcast_fusion.3
  301.8 0.8 slice_bitcast_fusion.1
  303.8 1.4 slice_bitcast_fusion
  305.2 4.9 %copy.69 = bf16[64,1,16,2048]{3,2,1,0:T(8,128)(2,1)} copy(bf16[64,1,16,2048]{3,2,1,0:T(8,128)(2,1)} %bitcast.49) | data formatting | bytes 8388608
  310.1 0.7 copy.70
  (47 shorter events, 11.9 us)
Async XLA Ops:
  305.2 4.9 %copy-start = (f32[576,128]{1,0:T(8,128)S(1)}, f32[576,128]{1,0:T(8,128)}, u32[]{:S(2)}) copy-start(f32[576,128]{1,0:T(8,128)} %get-tuple-element.155) | copy-start | bytes 884740
  305.2 5.6 %copy-start.5 = (f32[64,512]{1,0:T(8,128)S(1)}, f32[64,512]{1,0:T(8,128)}, u32[]{:S(2)}) copy-start(f32[64,512]{1,0:T(8,128)} %get-tuple-element.156) | copy-start | bytes 393220
  305.2 6.3 %copy-start.4 = (f32[256,128]{1,0:T(8,128)S(1)}, f32[256,128]{1,0:T(8,128)}, u32[]{:S(2)}) copy-start(f32[256,128]{1,0:T(8,128)} %get-tuple-element.157) | copy-start | bytes 393220
  305.2 6.9 %copy-start.3 = (f32[256,128]{1,0:T(8,128)S(1)}, f32[256,128]{1,0:T(8,128)}, u32[]{:S(2)}) copy-start(f32[256,128]{1,0:T(8,128)} %get-tuple-element.158) | copy-start | bytes 393220
  305.2 7.6 %copy-start.2 = (f32[256,128]{1,0:T(8,128)S(1)}, f32[256,128]{1,0:T(8,128)}, u32[]{:S(2)}) copy-start(f32[256,128]{1,0:T(8,128)} %get-tuple-element.159) | copy-start | bytes 393220
  305.2 8.2 %copy-start.1 = (f32[64,512]{1,0:T(8,128)S(1)}, f32[64,512]{1,0:T(8,128)}, u32[]{:S(2)}) copy-start(f32[64,512]{1,0:T(8,128)} %get-tuple-element.160) | copy-start | bytes 393220

commit v3 on v2

--- a/solution.py
+++ b/solution.py
@@ -133,7 +133,7 @@
     return [net.push(held, from_rows.at[k], peer) for k, peer in enumerate(place.row_peers())]
 
 
-def total_finish(net, place, copies, held, from_rows, second, from_batch):
+def total_finish(net, place, copies, held, from_rows, second, from_batch, behind=None):
     for copy in copies:
         copy.wait_recv()
     total = held[...]
@@ -141,6 +141,8 @@
         total = total + from_rows[k]
     second[...] = total
     more = [net.push(second, from_batch.at[k], peer) for k, peer in enumerate(place.batch_peers())]
+    if behind is not None:
+        behind()
     for copy in more:
         copy.wait_recv()
     for k in range(len(more)):
@@ -169,15 +171,15 @@
 
     def pair(self):
         place = self.place
+        self.second = []
         self.first = [
             self.net.push(self.shard(2 * z + place.other), self.from_twin.at[z], place.twin())
             for z in range(place.chips)
         ]
 
-    def batch(self):
+    def batch(self, turns=None):
         place = self.place
-        self.second = []
-        for z in range(place.chips):
+        for z in range(place.chips) if turns is None else turns:
             self.first[z].wait_recv()
             mine = self.shard(2 * z + place.core)
             rows = mine.shape[0]
@@ -250,7 +252,7 @@
 
 
 def backward_kernel(geometry, r):
-    cells, d_in, d_mid, columns, total_count, capacity, entries, samples = geometry
+    cells, d_in, d_mid, columns, total_count, capacity, entries, samples, clips = geometry
     place = Place()
     net = Wires(r.send, r.recv)
     ranks, groups, chips = place.ranks, place.groups, place.chips
@@ -316,6 +318,7 @@
     for key in "qoh":
         loads[key].wait()
         sc[key].pair()
+    sc["h"].batch()
 
     for key in (0, 1):
         loads[key].wait()
@@ -340,9 +343,9 @@
     own1[...] = r.head_part[...]
     spread(own1, [jnp.sum(acc[n], axis=0, keepdims=True) for n in range(2)])
     started = total_start(net, place, own1, r.rows1)
-    for key in "qoh":
-        sc[key].batch()
-    total = total_finish(net, place, started, own1, r.rows1, r.mid1, r.batch1)
+    total = total_finish(
+        net, place, started, own1, r.rows1, r.mid1, r.batch1, sc["q"].batch
+    )
     r.out_head[...] = total
     shift_c = gathered(total, 0, d_in // 4) / total_count
     gain_c = gathered(total, 1, d_in // 4) / total_count
@@ -384,7 +387,12 @@
         ).astype(LOW)
 
     sc["c"].pair()
-    total = total_finish(net, place, started, own2, r.rows2, r.mid2, r.batch2)
+
+    def middle():
+        sc["o"].batch()
+        sc["c"].batch()
+
+    total = total_finish(net, place, started, own2, r.rows2, r.mid2, r.batch2, middle)
     r.out_b_sums[...] = total
     shift_b = gathered(total, 0, d_mid // 4) / total_count
     gain_b = gathered(total, 1, d_mid // 4) / total_count
@@ -445,9 +453,8 @@
     more = pltpu.make_async_copy(r.in_hat_a, hat_b, local.at[18])
     more.start()
     sc["b"].pair()
-    for key in "qoh":
-        sc[key].line()
-    sc["c"].batch()
+    sc["h"].line()
+    sc["q"].line()
 
     loads[6].wait()
     more.wait()
@@ -479,13 +486,15 @@
         acc[0, :, 0:d_mid] += folded(grad)
         acc[1, :, 0:d_mid] += folded(grad * hat)
 
+    sc["b"].batch((0, 1))
     again = pltpu.make_async_copy(r.in_w_a, w_b.at[0:d_in], local.at[19])
     again.start()
     own3 = r.own3
     spread(own3, [jnp.sum(acc[n, :, 0:d_mid], axis=0, keepdims=True) for n in range(2)])
     started = total_start(net, place, own3, r.rows3)
-    sc["b"].batch()
-    total = total_finish(net, place, started, own3, r.rows3, r.mid3, r.batch3)
+    total = total_finish(
+        net, place, started, own3, r.rows3, r.mid3, r.batch3, lambda: sc["b"].batch((2, 3))
+    )
     r.out_a_sums[...] = total
     shift_a = gathered(total, 0, d_mid // 4) / total_count
     gain_a = gathered(total, 1, d_mid // 4) / total_count
@@ -512,8 +521,8 @@
         ).astype(LOW)
 
     sc["a"].pair()
+    sc["o"].line()
     sc["c"].line()
-    sc["b"].line()
 
     for copy in kv:
         copy.wait_recv()
@@ -529,6 +538,7 @@
         for peer in place.row_peers()
     ]
     sc["a"].batch()
+    sc["b"].line()
     for copy in every:
         copy.wait_recv()
     kv_out, kv_in = r.kv_out, r.kv_in
@@ -587,39 +597,43 @@
 
 
 class Gather:
-    def __init__(self, net, place, shard, whole, local):
+    def __init__(self, net, place, shard, whole, local, dim=0):
         self.net, self.place, self.shard, self.whole = net, place, shard, whole
-        self.rows = whole.shape[0] // place.ranks
+        self.dim, self.rows = dim, whole.shape[dim] // place.ranks
         self.own = pltpu.make_async_copy(shard, self.block(place.s), local)
 
+    def cut(self, ref, start, size):
+        at = pl.ds(pl.multiple_of(start, size), size)
+        return ref.at[at] if self.dim == 0 else ref.at[:, at]
+
     def block(self, s):
-        return rows_of(self.whole, s, self.rows)
+        return self.cut(self.whole, s * self.rows, self.rows)
 
     def quarter(self, s, g):
         part = self.rows // self.place.groups
-        return self.whole.at[pl.ds(pl.multiple_of(s * self.rows + g * part, part), part)]
+        return self.cut(self.whole, s * self.rows + g * part, part)
 
     def line(self):
         place = self.place
         part = self.rows // place.groups
-        source = self.shard.at[pl.ds(pl.multiple_of(place.g * part, part), part)]
+        source = self.cut(self.shard, place.g * part, part)
         self.first = [
             self.net.push(source, self.quarter(place.s, place.g), peer)
             for peer in place.line_peers()
         ]
         self.own.start()
-        self.third = [self.net.push(self.shard, self.block(place.s), place.twin())]
-
-    def batch(self):
-        place = self.place
+        self.second = []
         self.blocks = [
             lax.rem(place.z + place.chips - k, place.chips) * 2 + place.core
             for k in range(1, place.chips)
         ]
-        self.second = []
-        for copy, s in zip(self.first, self.blocks):
-            copy.wait_recv()
-            view = self.quarter(s, place.g)
+        self.third = [self.net.push(self.shard, self.block(place.s), place.twin())]
+
+    def batch(self, turns=None):
+        place = self.place
+        for k in range(len(self.first)) if turns is None else turns:
+            self.first[k].wait_recv()
+            view = self.quarter(self.blocks[k], place.g)
             self.second.append(
                 [self.net.push(view, view, peer) for peer in place.batch_peers()]
             )
@@ -647,7 +661,7 @@
 
 
 def forward_kernel(geometry, r):
-    cells, d_in, d_mid, columns, total_count, capacity, entries, samples = geometry
+    cells, d_in, d_mid, columns, total_count, capacity, entries, samples, clips = geometry
     place = Place()
     net = Wires(r.send, r.recv)
     ranks, groups = place.ranks, place.groups
@@ -659,7 +673,7 @@
     load_x.start()
     greet(place.row_peers() + place.batch_peers())
     a, b, c, q, o, h = (
-        Gather(net, place, shard, whole, local.at[n + 1])
+        Gather(net, place, shard, whole, local.at[n + 1], n // 5)
         for n, (shard, whole) in enumerate(
             (
                 (r.w_reduce, r.w_a),
@@ -672,6 +686,7 @@
         )
     )
     a.line()
+    b.line()
 
     def at_block(s):
         return pl.ds(pl.multiple_of(s * entry, entry), entry)
@@ -679,46 +694,49 @@
     def at_depth(s):
         return pl.ds(pl.multiple_of(s * depth, depth), depth)
 
+    r.bank16[...] = jnp.zeros_like(r.bank16)
+    r.bank16[0:entries, :] = r.bank[...]
+    for n in range(ranks):
+        r.box16[n, 0:1, 0:capacity] = r.piece_box[n : n + 1, :]
+    owner = lax.broadcasted_iota(jnp.int32, (ranks, 1), 0)
+    count = jnp.zeros((ranks, 1), jnp.int32)
+    for n in range(ranks):
+        count = jnp.where(owner == n, r.send_count[n], count)
+    for k in range(capacity):
+        on = slice(k * samples, (k + 1) * samples)
+        r.slot_cells[k] = r.sample_pos[:, on] + r.piece_clip[:, k : k + 1] * (cells // clips)
+        r.slot_weights[k] = jnp.where(k < count, r.sample_weight[:, on], 0.0)
     asked = [
         net.push(r.bank16.at[:, at_depth(peer[1])], rows_of(r.bank_cols, place.s, entry), peer)
         for peer in place.row_peers()
     ]
     named = [
-        net.push(rows_of(r.box16, peer[1], size), rows_of(r.box_in, place.s, size), peer)
-        for peer in place.row_peers()
+        net.push(r.box16.at[peer[1]], r.box_in.at[place.s], peer) for peer in place.row_peers()
     ]
     r.bank_cols[at_block(place.s), :] = r.bank16[:, at_depth(place.s)]
     mine = pl.ds(pl.multiple_of(place.s * size, size), size)
-    r.box_in[mine, :] = r.box16[mine, :]
-
-    strip = 64
-    lane = lax.rem(lax.broadcasted_iota(jnp.int32, (strip, ranks * size), 1), size)
-
-    @pl.loop(0, cells // strip)
-    def _(t):
-        at = pl.ds(pl.multiple_of(t * strip, strip), strip)
-        cell = lax.broadcasted_iota(jnp.int32, (strip, ranks * size), 0) + t * strip
-        total = jnp.zeros((strip, ranks * size), F32)
+    r.box_in[place.s] = r.box16[place.s]
+
+    by_rank = (capacity * ranks, ranks * size)
+    row, slot = (lax.broadcasted_iota(jnp.int32, by_rank, n) for n in range(2))
+    goal = lax.rem(row, ranks) * size + row // ranks
+    perms = [jnp.where(slot == goal + n * capacity, 1.0, 0.0).astype(LOW) for n in range(2)]
+
+    @pl.loop(0, capacity)
+    def _(k):
+        cell = lax.broadcasted_iota(jnp.int32, (ranks, cells), 1)
+        spots, weights = r.slot_cells[k], r.slot_weights[k]
+        total = jnp.zeros((ranks, cells), F32)
         for j in range(samples):
-            total = total + jnp.where(
-                cell == r.slot_cells[j : j + 1, :], r.slot_weights[j : j + 1, :], 0.0
-            )
-        r.et[0, at, :] = jnp.where(lane < capacity, total, 0.0).astype(LOW)
-        r.et[1, at, :] = jnp.where(lane < capacity, 0.0, total).astype(LOW)
+            total = total + jnp.where(cell == spots[:, j : j + 1], weights[:, j : j + 1], 0.0)
+        r.by_slot[pl.ds(pl.multiple_of(k * ranks, ranks), ranks), :] = total
+
+    for n in range(2):
+        r.et[n] = tdot(r.by_slot[...].astype(LOW), perms[n]).astype(LOW)
 
     a.batch()
-    b.line()
-    for copy in asked:
-        copy.wait_recv()
-    for n, weight in enumerate((r.w_key, r.w_value)):
-        r.kv_part[n] = jnp.dot(r.bank_cols[...], weight[...], preferred_element_type=F32)
-    kv = [
-        net.push(r.kv_part.at[:, at_block(peer[1])], r.kv_in.at[k], peer)
-        for k, peer in enumerate(place.row_peers())
-    ]
     a.pair()
-    b.batch()
-    c.line()
+    b.batch((0,))
     load_x.wait()
     a.ready()
 
@@ -737,13 +755,26 @@
 
     spread(r.own1, [jnp.sum(acc[n, :, 0:d_mid], axis=0, keepdims=True) for n in range(2)])
     started = total_start(net, place, r.own1, r.rows1)
+    c.line()
+    for copy in asked:
+        copy.wait_recv()
+    for n, weight in enumerate((r.w_key, r.w_value)):
+        r.kv_part[n] = jnp.dot(
+            r.bank_cols[...], weight[...], preferred_element_type=F32
+        ).astype(LOW)
+    kv = [
+        net.push(r.kv_part.at[:, at_block(peer[1])], r.kv_in.at[k], peer)
+        for k, peer in enumerate(place.row_peers())
+    ]
     keep_a = pltpu.make_async_copy(r.w_a, r.out_w_a, local.at[8])
     keep_a.start()
-    total = total_finish(net, place, started, r.own1, r.rows1, r.mid1, r.batch1)
+    total = total_finish(
+        net, place, started, r.own1, r.rows1, r.mid1, r.batch1, lambda: b.batch((1, 2))
+    )
     centre, inverse = moments(total, d_mid, total_count)
-    gain, bias = r.norm_a[0:1, :], r.norm_a[1:2, :]
-    r.out_norm_a[...] = r.norm_a[...]
-    r.out_norm_a[2:3, :] = gain * inverse
+    gain, bias = r.gain_a[...], r.bias_a[...]
+    for n, value in enumerate((gain, bias, gain * inverse)):
+        r.out_norm_a[n : n + 1, :] = value
 
     first, last = place.s == 0, place.s == ranks - 1
     low_a, low_up, low_down = r.low_a, r.low_up, r.low_down
@@ -785,8 +816,6 @@
 
     keep_hat_a = pltpu.make_async_copy(r.hat_a, r.out_hat_a, local.at[9])
     keep_hat_a.start()
-    b.pair()
-    c.batch()
     q.line()
 
     @pl.loop(0, tiles)
@@ -794,6 +823,8 @@
         at = pl.ds(pl.multiple_of(t * big, big), big)
         r.low_t[1, :, at] = jnp.transpose(low_a[at, :].astype(F32)).astype(LOW)
 
+    b.pair()
+    c.batch()
     b.ready()
     acc[...] = jnp.zeros_like(acc)
 
@@ -824,6 +855,8 @@
 
     spread(r.own2, [jnp.sum(acc[n, :, 0:d_mid], axis=0, keepdims=True) for n in range(2)])
     started = total_start(net, place, r.own2, r.rows2)
+    o.line()
+    h.line()
     keep_b = pltpu.make_async_copy(r.w_b, r.out_w_b, local.at[10])
     keep_b.start()
 
@@ -835,15 +868,12 @@
 
     keep_low_t = pltpu.make_async_copy(r.low_t, r.out_low_t, local.at[11])
     keep_low_t.start()
-    total = total_finish(net, place, started, r.own2, r.rows2, r.mid2, r.batch2)
+    total = total_finish(net, place, started, r.own2, r.rows2, r.mid2, r.batch2, q.batch)
     centre, inverse = moments(total, d_mid, total_count)
-    gain, bias = r.norm_b[0:1, :], r.norm_b[1:2, :]
-    r.out_norm_b[...] = r.norm_b[...]
-    r.out_norm_b[2:3, :] = gain * inverse
+    gain, bias = r.gain_b[...], r.bias_b[...]
+    for n, value in enumerate((gain, bias, gain * inverse)):
+        r.out_norm_b[n : n + 1, :] = value
     c.pair()
-    q.batch()
-    o.line()
-    h.line()
     c.ready()
     acc[...] = jnp.zeros_like(acc)
 
@@ -872,9 +902,9 @@
     for copy in kv:
         copy.wait_recv()
     for n in range(2):
-        total = r.kv_part[n, at_block(place.s), :]
+        total = r.kv_part[n, at_block(place.s), :].astype(F32)
         for k in range(ranks - 1):
-            total = total + r.kv_in[k, n]
+            total = total + r.kv_in[k, n].astype(F32)
         r.kv_own[n] = total.astype(LOW)
         r.kv_all[n, at_block(place.s), :] = total.astype(LOW)
     every = [
@@ -888,14 +918,17 @@
 
     keep_low_bt = pltpu.make_async_copy(r.low_bt, r.out_low_bt, local.at[14])
     keep_low_bt.start()
-    total = total_finish(net, place, started, r.own3, r.rows3, r.mid3, r.batch3)
+
+    def rest():
+        o.batch()
+        h.batch()
+
+    total = total_finish(net, place, started, r.own3, r.rows3, r.mid3, r.batch3, rest)
     centre, inverse = moments(total, d_in, total_count)
-    r.scale_c[...] = r.norm_c[0:1, :] * inverse
+    r.scale_c[...] = r.gain_c[...] * inverse
     r.centre_c[0:1, :] = centre
     r.centre_c[1:2, :] = inverse
     q.pair()
-    o.batch()
-    h.batch()
     r.pieces[...] = jnp.zeros_like(r.pieces)
     tile = 128
 
@@ -907,7 +940,7 @@
             into = slice((k % 2) * (d_in // 4), (k % 2 + 1) * (d_in // 4))
             hat = (r.pre_c[at, on] - r.centre_c[0:1, on]) * r.centre_c[1:2, on]
             r.hat_c[at, on] = hat.astype(LOW)
-            value = r.norm_c[0:1, on] * hat + r.norm_c[1:2, on] + r.x[at, on].astype(F32)
+            value = r.gain_c[:, on] * hat + r.bias_c[:, on] + r.x[at, on].astype(F32)
             sig = sigma(value)
             fmap = value * sig
             r.x[at, on] = (sig + fmap * (1.0 - sig)).astype(LOW)
@@ -928,13 +961,26 @@
     for copy in named + every + pushed:
         copy.wait_recv()
 
-    boxes = r.windows.shape[0]
-    slot = lax.rem(lax.broadcasted_iota(jnp.int32, (ranks * size, boxes), 0), size)
-    hit = r.box_in[...] == lax.broadcasted_iota(jnp.int32, (ranks * size, boxes), 1)
-    picks = [
-        jnp.where(hit & (slot < capacity), 1.0, 0.0).astype(LOW),
-        jnp.where(hit & (slot >= capacity), 1.0, 0.0).astype(LOW),
-    ]
+    boxes = r.cotangent.shape[1]
+    number = jnp.concatenate([r.box_in[n, 0:1, :] for n in range(ranks)], axis=0)
+    box = lax.broadcasted_iota(jnp.int32, (ranks, boxes), 1)
+    hits = jnp.concatenate(
+        [jnp.where(number[:, k : k + 1] == box, 1.0, 0.0) for k in range(capacity)], axis=0
+    ).astype(LOW)
+    picks = [tdot(perm, hits).astype(LOW) for perm in perms]
+    across = lax.broadcasted_iota(jnp.int32, (boxes, boxes), 0) == lax.broadcasted_iota(
+        jnp.int32, (boxes, boxes), 1
+    )
+
+    def upright(value):
+        wide = jnp.broadcast_to(value.astype(F32), (boxes, boxes))
+        return jnp.sum(jnp.where(across, wide, 0.0), axis=1, keepdims=True)
+
+    bank_row = lax.broadcasted_iota(jnp.int32, (boxes, ranks * entry), 1)
+    inner = lax.rem(bank_row, entry)
+    spot = (bank_row // entry * entries + inner).astype(F32)
+    start, length = upright(r.win_start[...]), upright(r.win_len[...])
+    window = (inner < entries) & (spot >= start) & (spot < start + length)
     for k in range(2):
         r.pooled[:, k * half : (k + 1) * half] = tdot(picks[k], r.arrived[...])
     r.joined[:, 0:d_in] = r.pooled[...].astype(LOW)
@@ -943,7 +989,7 @@
     scale = d_mid ** (-0.5)
     q.ready()
     queries = jnp.dot(pooled_low[...], r.w_q[...], preferred_element_type=F32).astype(LOW)
-    scores = jnp.where(r.windows[...] > 0, ndot(queries, keys[...]) * scale, -1e30)
+    scores = jnp.where(window, ndot(queries, keys[...]) * scale, -1e30)
     raised = jnp.exp(scores - jnp.max(scores, axis=1, keepdims=True))
     attend = raised / jnp.sum(raised, axis=1, keepdims=True)
     attend_low = attend.astype(LOW)
@@ -951,7 +997,7 @@
     centred = mixture - jnp.mean(mixture, axis=1, keepdims=True)
     inverse_z = lax.rsqrt(jnp.mean(centred * centred, axis=1, keepdims=True) + 1e-05)
     hat_z = centred * inverse_z
-    pre_ln = r.norm_z[0:1, :] * hat_z + r.norm_z[1:2, :]
+    pre_ln = r.ln_gain[...] * hat_z + r.ln_bias[...]
     sig_z = sigma(pre_ln)
     low_r = (pre_ln * sig_z).astype(LOW)
     slope_z = sig_z * (1.0 + pre_ln * (1.0 - sig_z))
@@ -964,19 +1010,21 @@
         ).astype(LOW)
     h.ready()
     logits = (
-        jnp.dot(r.joined[...], r.w_h[...], preferred_element_type=F32) + r.head_bias[...]
+        ndot(r.joined[...], r.w_h[...]) + r.head_bias[...]
     )
     likely = jax.nn.sigmoid(logits)
     r.out_probs[...] = likely
-    d_logit = (r.cotangent[...] * (likely * (1.0 - likely))).astype(LOW)
+    d_logit = (jnp.transpose(r.cotangent[...]) * (likely * (1.0 - likely))).astype(LOW)
     for k in range(4):
         on = slice(k * (d_in // 4), (k + 1) * (d_in // 4))
         below = slice(d_in + k * (d_in // 4), d_in + (k + 1) * (d_in // 4))
-        upper = ndot(d_logit, r.w_h[below, :])
+        upper = jnp.dot(d_logit, r.w_h[:, below], preferred_element_type=F32)
         r.d_branch[:, on] = upper.astype(LOW)
-        r.pooled[:, on] = ndot(d_logit, r.w_h[on, :]) + upper
+        r.pooled[:, on] = (
+            jnp.dot(d_logit, r.w_h[:, on], preferred_element_type=F32) + upper
+        )
     d_ln = ndot(r.d_branch[...], r.w_o[...]) * slope_z
-    d_hat = d_ln * r.norm_z[0:1, :]
+    d_hat = d_ln * r.ln_gain[...]
     d_mixture = (
         inverse_z
         * (
@@ -1008,8 +1056,16 @@
         r.g_q[on, :] = tdot(r.joined[:, on], d_queries).astype(LOW)
         r.g_o[:, on] = tdot(low_r, r.d_branch[:, on]).astype(LOW)
     width = 2 * depth
+    classes = d_logit.shape[1]
+    share = classes // groups
+    held, kind = (
+        lax.broadcasted_iota(jnp.int32, (classes, r.g_h.shape[1]), n) for n in range(2)
+    )
+    padded_class = held // share * (r.g_h.shape[1] // groups) + lax.rem(held, share)
+    spaced = jnp.where(kind == padded_class, 1.0, 0.0).astype(LOW)
+    d_spaced = jnp.dot(d_logit, spaced, preferred_element_type=F32).astype(LOW)
     for s in range(ranks):
-        r.g_h[s] = tdot(d_logit, r.joined[:, s * width : (s + 1) * width]).astype(LOW)
+        r.g_h[s] = tdot(d_spaced, r.joined[:, s * width : (s + 1) * width]).astype(LOW)
     keeps = []
     for n, (source, target) in enumerate(((r.g_q, r.out_g_q), (r.g_o, r.out_g_o), (r.g_h, r.out_g_h))):
         keeps.append(pltpu.make_async_copy(source, target, local.at[17 + n]))
@@ -1023,7 +1079,6 @@
             r.out_head_part[4 * n + k : 4 * n + k + 1, d_in // 4 : d_in // 4 + quarter] = value[
                 :, k * quarter : (k + 1) * quarter
             ]
-    classes = d_logit.shape[1]
     r.out_head_part[0:1, d_in // 4 + quarter : d_in // 4 + quarter + classes] = jnp.sum(
         d_logit.astype(F32), axis=0, keepdims=True
     )
@@ -1050,18 +1105,19 @@
 
 
 class Refs:
-    def __init__(self, names, refs):
-        self.__dict__.update(zip(names, refs))
+    def __init__(self, names, refs, **more):
+        self.__dict__.update(zip(names, refs), **more)
 
 
 def run_kernel(body, geometry, channel, held, far, outs, far_outs, scratch):
     anywhere = pl.BlockSpec(memory_space=pl.ANY)
     inside = pl.BlockSpec(memory_space=pltpu.VMEM)
     names = [*held, *far, *outs, *far_outs, *scratch]
+    scalars = pl.BlockSpec(memory_space=pltpu.SMEM)
     results = pl.pallas_call(
         lambda *refs: body(geometry, Refs(names, refs)),
         out_shape=(*outs.values(), *far_outs.values()),
-        in_specs=[inside] * len(held) + [anywhere] * len(far),
+        in_specs=[scalars if v.ndim == 1 else inside for v in held.values()] + [anywhere] * len(far),
         out_specs=(inside,) * len(outs) + (anywhere,) * len(far_outs),
         scratch_shapes=[*scratch.values()],
         compiler_params=pltpu.CompilerParams(
@@ -1100,13 +1156,13 @@
 
 
 def run_forward(geometry, held, far):
-    cells, d_in, d_mid, columns, total_count, capacity, entries, samples = geometry
+    cells, d_in, d_mid, columns, total_count, capacity, entries, samples, clips = geometry
     groups, ranks = lax.axis_size("batch"), lax.axis_size("rows")
     slots = ranks * 2 * capacity
-    entry = held["bank16"].shape[0]
+    entry = -(-entries // 16) * 16
     bank = ranks * entry
-    boxes = held["windows"].shape[0]
-    classes = held["head_bias"].shape[1]
+    classes, boxes = held["cotangent"].shape
+    spaced = groups * (-(-classes // groups // 16) * 16)
     spatial = far["w_spatial"].shape[0] * ranks
     half = d_in // 2
     outs = dict(
@@ -1116,7 +1172,7 @@
         out_probs=shape(F32, boxes, classes),
         out_dkv=shape(LOW, 2, bank, d_mid),
         out_back=shape(LOW, slots, half),
-        out_head_part=shape(F32, 8, d_in // 4 + d_mid // 4 + classes),
+        out_head_part=shape(F32, 8, d_in // 4 + d_mid // 4 + spaced),
         et=shape(LOW, 2, cells, slots),
         bank_cols_out=shape(LOW, bank, d_in // ranks),
     )
@@ -1132,7 +1188,7 @@
         out_low_bt=shape(LOW, d_mid, cells),
         out_g_q=shape(LOW, d_in, d_mid),
         out_g_o=shape(LOW, d_mid, d_in),
-        out_g_h=shape(LOW, ranks, classes, 2 * d_in // ranks),
+        out_g_h=shape(LOW, ranks, spaced, 2 * d_in // ranks),
     )
     scratch = dict(
         x=room(LOW, cells, d_in),
@@ -1141,11 +1197,16 @@
         w_c=room(LOW, d_mid, d_in),
         w_q=room(LOW, d_in, d_mid),
         w_o=room(LOW, d_mid, d_in),
-        w_h=room(LOW, 2 * d_in, classes),
+        w_h=room(LOW, classes, 2 * d_in),
         bank_cols=room(LOW, bank, d_in // ranks),
-        box_in=room(jnp.int32, slots, boxes),
-        kv_part=room(F32, 2, bank, d_mid),
-        kv_in=room(F32, ranks - 1, 2, entry, d_mid),
+        bank16=room(LOW, entry, d_in),
+        box16=room(jnp.int32, ranks, 8, 128),
+        box_in=room(jnp.int32, ranks, 8, 128),
+        slot_cells=room(jnp.int32, capacity, ranks, samples),
+        slot_weights=room(F32, capacity, ranks, samples),
+        by_slot=room(F32, capacity * ranks, cells),
+        kv_part=room(LOW, 2, bank, d_mid),
+        kv_in=room(LOW, ranks - 1, 2, entry, d_mid),
         kv_own=room(LOW, 2, entry, d_mid),
         kv_all=room(LOW, 2, bank, d_mid),
         acc=room(F32, 2, 8, d_in),
@@ -1173,7 +1234,7 @@
         back_in=room(LOW, slots, half),
         g_q=room(LOW, d_in, d_mid),
         g_o=room(LOW, d_mid, d_in),
-        g_h=room(LOW, ranks, classes, 2 * d_in // ranks),
+        g_h=room(LOW, ranks, spaced, 2 * d_in // ranks),
         **wires_room(cells),
     )
     sums_room(scratch, ranks, groups, ((1, d_mid // 4), (2, d_mid // 4), (3, d_in // 4)))
@@ -1181,7 +1242,7 @@
 
 
 def run_backward(geometry, held, far):
-    cells, d_in, d_mid, columns, total_count, capacity, entries, samples = geometry
+    cells, d_in, d_mid, columns, total_count, capacity, entries, samples, clips = geometry
     groups, ranks = lax.axis_size("batch"), lax.axis_size("rows")
     chips = ranks // 2
     slots = ranks * 2 * capacity
@@ -1248,6 +1309,99 @@
         scratch["li_" + key] = room(LOW, chips - 1, *share[key])
     far_outs = dict(out_x=shape(LOW, cells, d_in))
     return run_kernel(backward_kernel, geometry, 12, held, far, outs, far_outs, scratch)
+
+
+def finish_kernel(r):
+    chunk = r.in_x.shape[0] // 8
+
+    def across(n, leave):
+        at = pl.ds(n * chunk, chunk)
+        source, target = (r.stage, r.x) if leave else (r.in_x, r.stage)
+        return pltpu.make_async_copy(source.at[at], target.at[at], r.local.at[leave, n])
+
+    for n in range(8):
+        across(n, 0).start()
+    for n in range(8):
+        across(n, 0).wait()
+        across(n, 1).start()
+    r.probs[...] = jnp.transpose(r.in_probs[...])
+    r.a[...] = jnp.transpose(r.in_a[...])
+    r.b[...] = r.in_b[...]
+    r.c[...] = r.in_c[...]
+    r.q[...] = r.in_q[...]
+    r.k[...] = r.in_k[...]
+    r.v[...] = r.in_v[...]
+    r.o[...] = r.in_o[...]
+    r.h[...] = r.in_h[0 : r.h.shape[0], :]
+    r.bias_a[...], r.gain_a[...] = r.in_a_sums[0:4, :], r.in_a_sums[4:8, :]
+    r.bias_b[...], r.gain_b[...] = r.in_b_sums[0:4, :], r.in_b_sums[4:8, :]
+    lanes = r.ln_gain.shape[1]
+    per = r.gain_c.shape[0] // 4
+    for n in range(4):
+        for k in range(per):
+            on = slice(k * lanes, (k + 1) * lanes)
+            r.bias_c[per * n + k : per * n + k + 1, :] = r.in_head[n : n + 1, on]
+            r.gain_c[per * n + k : per * n + k + 1, :] = r.in_head[4 + n : 5 + n, on]
+    on = slice(per * lanes, (per + 1) * lanes)
+    r.ln_gain[...], r.ln_bias[...] = r.in_head[0:4, on], r.in_head[4:8, on]
+    at = (per + 1) * lanes
+    r.head_bias[...] = r.in_head[0:1, at : at + r.head_bias.shape[1]]
+    for n in range(8):
+        across(n, 1).wait()
+
+
+def run_finish(probs, two, groups, d_mid, classes):
+    held = dict(
+        in_probs=probs,
+        in_a=two.out_a,
+        in_b=two.out_b,
+        in_c=two.out_c,
+        in_q=two.out_q,
+        in_k=two.out_k,
+        in_v=two.out_v,
+        in_o=two.out_o,
+        in_h=two.out_h,
+        in_a_sums=two.out_a_sums,
+        in_b_sums=two.out_b_sums,
+        in_head=two.out_head,
+    )
+    like = lambda v: shape(F32, *v.shape)
+    lanes = two.out_a_sums.shape[1]
+    row = shape(F32, 4, lanes)
+    wide = shape(F32, 4 * (two.out_x.shape[1] // 4 // lanes), lanes)
+    outs = dict(
+        probs=shape(F32, *probs.shape[::-1]),
+        a=shape(F32, *two.out_a.shape[::-1]),
+        b=like(two.out_b),
+        c=like(two.out_c),
+        q=like(two.out_q),
+        k=like(two.out_k),
+        v=like(two.out_v),
+        o=like(two.out_o),
+        h=shape(F32, classes // groups, two.out_h.shape[1]),
+        gain_a=row,
+        bias_a=row,
+        gain_b=row,
+        bias_b=row,
+        gain_c=wide,
+        bias_c=wide,
+        ln_gain=row,
+        ln_bias=row,
+        head_bias=shape(F32, 1, classes),
+    )
+    far_outs = dict(x=shape(LOW, *two.out_x.shape))
+    anywhere = pl.BlockSpec(memory_space=pl.ANY)
+    inside = pl.BlockSpec(memory_space=pltpu.VMEM)
+    names = [*held, "in_x", *outs, *far_outs, "stage", "local"]
+    results = pl.pallas_call(
+        lambda *refs: finish_kernel(Refs(names, refs)),
+        out_shape=(*outs.values(), *far_outs.values()),
+        in_specs=[inside] * len(held) + [anywhere],
+        out_specs=(inside,) * len(outs) + (anywhere,),
+        scratch_shapes=[room(LOW, *two.out_x.shape), pltpu.SemaphoreType.DMA((2, 8))],
+        compiler_params=pltpu.CompilerParams(vmem_limit_bytes=64 << 20),
+    )(*held.values(), two.out_x)
+    return Refs([*outs, *far_outs], results)
 
 
 def fused_device(
@@ -1287,56 +1441,29 @@
     capacity = piece_box.shape[1]
     samples = sample_pos.shape[1] // capacity
     entries = bank.shape[0]
-    entry = -(-entries // 16) * 16
-    classes = head_bias.shape[0]
-    class_share = classes // groups
-    geometry = (cells, d_in, d_mid, columns, total_count, capacity, entries, samples)
-    twice = lambda v: jnp.concatenate([v, v], axis=-1)
-
-    def by_class(value):
-        rows = value.reshape(-1, groups, class_share)
-        return jnp.pad(rows, ((0, 0), (0, 0), (0, 32 - class_share))).reshape(-1, groups * 32)
-
-    def from_class(value):
-        rows = value.reshape(-1, groups, 32)[:, :, :class_share]
-        return rows.reshape(-1, classes)
-
-    def stacked(*rows):
-        return jnp.pad(jnp.stack(rows), ((0, 8 - len(rows)), (0, 0)))
-
-    def by_slot(value):
-        rows = value.reshape(ranks, capacity, samples).transpose(2, 0, 1)
-        rows = twice(rows).reshape(samples, ranks * 2 * capacity)
-        return jnp.pad(rows, ((0, -samples % 8), (0, 0)))
-
-    at_clip = jnp.repeat(piece_clip * (row_dev * columns), samples, axis=1)
-    is_live = (jnp.arange(capacity)[None, :] < send_count[:, None]).astype(F32)
-    live = jnp.repeat(is_live, samples, axis=1)
-    boxes = win_start.shape[0]
-    box16 = jnp.broadcast_to(
-        twice(piece_box).reshape(ranks * 2 * capacity, 1), (ranks * 2 * capacity, boxes)
-    )
-    spot = jnp.arange(ranks * entry)
-    position = spot // entry * entries + spot % entry
-    windows = (
-        (spot % entry < entries)
-        & (position >= win_start[:, None])
-        & (position < (win_start + win_len)[:, None])
-    ).astype(jnp.int32)
+    geometry = (cells, d_in, d_mid, columns, total_count, capacity, entries, samples, clip_dev)
+    line = lambda v: v.reshape(1, -1)
     held = dict(
-        bank16=jnp.pad(bank, ((0, entry - entries), (0, 0))),
-        box16=box16,
-        slot_cells=by_slot(at_clip + sample_pos),
-        slot_weights=by_slot(sample_weight * live),
+        bank=bank,
+        piece_box=piece_box,
+        piece_clip=piece_clip,
+        send_count=send_count,
+        sample_pos=sample_pos,
+        sample_weight=sample_weight,
         w_key=w_key,
         w_value=w_value,
-        norm_a=stacked(gain_a, bias_a),
-        norm_b=stacked(gain_b, bias_b),
-        norm_c=stacked(gain_c, bias_c),
-        norm_z=stacked(ln_gain, ln_bias),
-        windows=windows,
-        head_bias=by_class(head_bias),
-        cotangent=by_class(prob_cotangent),
+        gain_a=line(gain_a),
+        bias_a=line(bias_a),
+        gain_b=line(gain_b),
+        bias_b=line(bias_b),
+        gain_c=line(gain_c),
+        bias_c=line(bias_c),
+        ln_gain=line(ln_gain),
+        ln_bias=line(ln_bias),
+        win_start=line(win_start),
+        win_len=line(win_len),
+        head_bias=line(head_bias),
+        cotangent=prob_cotangent.T,
     )
     far = dict(
         features=features.reshape(cells, d_in),
@@ -1345,7 +1472,7 @@
         w_expand=w_expand,
         w_query=query_weight,
         w_out=w_out,
-        w_head=by_class(w_head),
+        w_head=w_head.T,
     )
     one = run_forward(geometry, held, far)
     back_held = dict(
@@ -1374,28 +1501,28 @@
         in_g_h=one.out_g_h,
     )
     two = run_backward(geometry, back_held, back_far)
-    head, wide, quarter = two.out_head, d_in // 4, d_mid // 4
-    b_sums, a_sums = two.out_b_sums.reshape(2, d_mid), two.out_a_sums.reshape(2, d_mid)
+    last = run_finish(one.out_probs, two, groups, d_mid, prob_cotangent.shape[1])
+    flat = lambda v: v.reshape(-1)
     return (
-        from_class(one.out_probs),
-        two.out_x.reshape(features.shape),
-        two.out_a.T,
-        two.out_b,
-        two.out_c,
-        two.out_q,
-        two.out_k,
-        two.out_v,
-        two.out_o,
-        two.out_h[:class_share].T,
-        a_sums[1],
-        a_sums[0],
-        b_sums[1],
-        b_sums[0],
-        head[4:8, :wide].reshape(d_in),
-        head[0:4, :wide].reshape(d_in),
-        head[0:4, wide : wide + quarter].reshape(d_mid),
-        head[4:8, wide : wide + quarter].reshape(d_mid),
-        from_class(head[0:1, wide + quarter :]).reshape(classes),
+        last.probs.T,
+        last.x.reshape(features.shape),
+        last.a,
+        last.b,
+        last.c,
+        last.q,
+        last.k,
+        last.v,
+        last.o,
+        last.h.T,
+        flat(last.gain_a),
+        flat(last.bias_a),
+        flat(last.gain_b),
+        flat(last.bias_b),
+        flat(last.gain_c),
+        flat(last.bias_c),
+        flat(last.ln_gain),
+        flat(last.ln_bias),
+        flat(last.head_bias),
     )
 
 

time: 316 us -> 245 us (0.78)
  Pallas kernels: 274 us -> 244 us
  local copies, waits for them, and re-layouts: 29.6 us -> 0 us
  other arithmetic: 9.78 us -> 0 us
    pallas_call x2, Pallas kernels: 274 us -> 238 us  [run_kernel(): pl.pallas_call(lambda *refs: body(geometry, Refs(names, refs)), out_shape...]
    unnamed x23 -> x0, local copies, waits for them, and re-layouts: 12.5 us -> none
    reshape x15 -> x0, local copies, waits for them, and re-layouts: 6.99 us -> none  [the longest x3 2.43 us: by_class(): rows = value.reshape(-1, groups, class_share)]
    pallas_call x0 -> x1, Pallas kernels: none -> 5.96 us  [run_finish(): pl.pallas_call(lambda *refs: finish_kernel(Refs(names, refs)), out_shape=...]
    another operation x3 -> x0, other arithmetic: 4.02 us -> none  [stacked(): return jnp.pad(jnp.stack(rows), ((0, 8 - len(rows)), (0, 0)))]
where the time goes in v3:
time: 245 us
  Pallas kernels  244 us (100%)
    pallas_call x2, Pallas kernels, run_kernel(): pl.pallas_call(lambda *refs: body(geometry, Refs(names, refs)), out_shape...  238 us
    pallas_call x1, Pallas kernels, run_finish(): pl.pallas_call(lambda *refs: finish_kernel(Refs(names, refs)), out_shape=...  5.96 us

profile of v3, /device:TPU:0, one launch (start us, length us, event | category | flops | bytes accessed | tf_op | source)
XLA Modules:
  0.0 244.5 jit_solution(9179083821385141597)
XLA Ops:
  0.7 112.1 %shard_map.402 = (f32[8,512]{1,0:T(8,128)}, f32[8,512]{1,0:T(8,128)}, f32[1,2048]{1,0:T(1,128)}, f32[128,80]{1,0:T(8,128)}, bf16[2,128,512]{2,1,0:T(8,128)(2,1)}...) custom-call(bf16[10,2048]{1,0:T(8,128)(2,1)} %refs_0_.1, ...), custom_call_target="tpu_custom_call" | custom-call | tf_op jit(solution)/shard_map/pallas_call | solution.py:1117
  112.8 125.6 %shard_map.403 = (f32[8,768]{1,0:T(8,128)}, f32[8,128]{1,0:T(8,128)}, f32[8,128]{1,0:T(8,128)}, f32[256,128]{1,0:T(8,128)}, f32[256,128]{1,0:T(8,128)}, /*index=...) custom-call(bf16[128,1024]{1,0:T(8,128)(2,1)} %get-tuple-element.72., ...), custom_call_target="tpu_custom_call" | custom-call | tf_op jit(solution)/shard_map/pallas_call | solution.py:1117
  238.4 6.0 %shard_map.404 = (f32[80,128]{1,0:T(8,128)}, f32[256,128]{1,0:T(8,128)}, f32[576,128]{1,0:T(8,128)}, f32[64,512]{1,0:T(8,128)}, f32[256,128]{1,0:T(8,128)}, /*in...) custom-call(f32[128,80]{1,0:T(8,128)} %get-tuple-element.71.refs_0_,, ...), custom_call_target="tpu_custom_call" | custom-call | tf_op jit(solution)/shard_map/pallas_call | solution.py:1396

commit v4 on v0

--- a/solution.py
+++ b/solution.py
@@ -1,6 +1,8 @@
 import jax
 import jax.numpy as jnp
 from jax import lax
+from jax.experimental import pallas as pl
+from jax.experimental.pallas import tpu as pltpu
 from jax.sharding import PartitionSpec as P
 
 
@@ -59,24 +61,1450 @@
     return sig * (1.0 + value * (1.0 - sig))
 
 
-def normalize(field, total_count):
+def norm_back(grad, normed, inverse, gain, shift_sum, gain_total_grad, total_count):
+    return (
+        gain * inverse * (grad - shift_sum / total_count - normed * gain_total_grad / total_count)
+    )
+
+
+MESH = pl.DeviceIdType.MESH
+LOW = jnp.bfloat16
+F32 = jnp.float32
+
+
+class Wires:
+    def __init__(self, send, recv):
+        self.send, self.recv, self.at, self.open = send, recv, 0, []
+
+    def plan(self, source, target, peer):
+        copy = pltpu.make_async_remote_copy(
+            src_ref=source,
+            dst_ref=target,
+            send_sem=self.send.at[self.at],
+            recv_sem=self.recv.at[self.at],
+            device_id=peer,
+            device_id_type=MESH,
+        )
+        self.at += 1
+        self.open.append(copy)
+        return copy
+
+    def push(self, source, target, peer):
+        return start(self.plan(source, target, peer))
+
+    def settle(self, copies):
+        for copy in copies:
+            copy.wait_send()
+        done = {id(copy) for copy in copies}
+        self.open = [copy for copy in self.open if id(copy) not in done]
+
+    def close(self):
+        for copy in self.open:
+            copy.wait_send()
+
+
+def start(copy):
+    copy.start()
+    return copy
+
+
+def greet(peers):
+    barrier = pltpu.get_barrier_semaphore()
+    for peer in peers:
+        pl.semaphore_signal(barrier, inc=1, device_id=peer, device_id_type=MESH)
+    pl.semaphore_wait(barrier, len(peers))
+
+
+class Place:
+    def __init__(self):
+        self.groups, self.ranks = lax.axis_size("batch"), lax.axis_size("rows")
+        self.g, self.s = lax.axis_index("batch"), lax.axis_index("rows")
+        self.chips = self.ranks // 2
+        self.z, self.core = self.s // 2, lax.rem(self.s, 2)
+        self.other = 1 - self.core
+        self.row_peers = [(self.g, lax.rem(self.s + k, self.ranks)) for k in range(1, self.ranks)]
+        self.batch_peers = [
+            (lax.rem(self.g + k, self.groups), self.s) for k in range(1, self.groups)
+        ]
+        self.line = [lax.rem(self.z + k, self.chips) for k in range(self.chips)]
+        self.line_peers = [(self.g, z * 2 + self.core) for z in self.line[1:]]
+        self.twin = (self.g, self.z * 2 + self.other)
+        low, high = lax.rem(self.g, 2), self.g // 2
+        beside, above = high * 2 + 1 - low, (1 - high) * 2 + low
+        self.near = beside + self.core * (above - beside)
+        self.far, self.across = beside + above - self.near, 3 - self.g
+
+
+def rows_of(ref, index, size):
+    return ref.at[pl.ds(pl.multiple_of(index * size, size), size)]
+
+
+class Total:
+    def __init__(self, net, place, held, from_rows, second, from_batch):
+        self.held, self.from_rows, self.second, self.from_batch = (
+            held,
+            from_rows,
+            second,
+            from_batch,
+        )
+        self.rows = [
+            net.plan(held, from_rows.at[k], peer) for k, peer in enumerate(place.row_peers)
+        ]
+        self.batch = [
+            net.plan(second, from_batch.at[k], peer) for k, peer in enumerate(place.batch_peers)
+        ]
+
+    def start(self):
+        for copy in self.rows:
+            copy.start()
+
+    def finish(self, behind=None):
+        for copy in self.rows:
+            copy.wait_recv()
+        total = self.held[...]
+        for k in range(len(self.rows)):
+            total = total + self.from_rows[k]
+        self.second[...] = total
+        for copy in self.batch:
+            copy.start()
+        if behind is not None:
+            behind()
+        for copy in self.batch:
+            copy.wait_recv()
+        for k in range(len(self.batch)):
+            total = total + self.from_batch[k]
+        return total
+
+
+def spread(ref, values):
+    quarter = values[0].shape[1] // 4
+    for n, value in enumerate(values):
+        for k in range(4):
+            ref[4 * n + k : 4 * n + k + 1, 0:quarter] = value[:, k * quarter : (k + 1) * quarter]
+
+
+def gathered(block, n, quarter, at=0):
+    return jnp.concatenate(
+        [block[4 * n + k : 4 * n + k + 1, at : at + quarter] for k in range(4)], axis=1
+    )
+
+
+class Corner:
+    def __init__(self, ref, height, width):
+        self.ref, self.height, self.width = ref, height, width
+
+    def __getitem__(self, z):
+        beside = self.ref.shape[1] // self.width
+        down, along = z // beside * self.height, z % beside * self.width
+        return self.ref.at[down : down + self.height, along : along + self.width]
+
+
+class Scatter:
+    def __init__(self, net, place, shard, part, from_twin, from_batch, partial, from_line, result):
+        self.place, self.shard, self.part = place, shard, part
+        self.from_twin, self.from_batch, self.partial = from_twin, from_batch, partial
+        self.from_line, self.result = from_line, result
+        self.first, self.second, self.last = [], [], []
+        for z in range(place.chips):
+            self.first.append(net.plan(shard(2 * z + place.other), from_twin[z], place.twin))
+            mine = shard(2 * z + place.core)
+            self.second.append(
+                [
+                    net.plan(part(mine, g), from_batch.at[k, z], (near, place.s))
+                    for k, (g, near) in enumerate(
+                        (
+                            (place.near, place.near),
+                            (place.across, place.near),
+                            (place.far, place.far),
+                        )
+                    )
+                ]
+            )
+        self.third = [
+            net.plan(partial.at[k + 1], from_line.at[k], peer)
+            for k, peer in enumerate(place.line_peers)
+        ]
+
+    def pair(self):
+        for copy in self.first:
+            copy.start()
+
+    def batch(self, *turns):
+        place = self.place
+        for z in turns or range(place.chips):
+            self.first[z].wait_recv()
+            mine = self.shard(2 * z + place.core)
+            rows = mine.shape[0]
+            step = next(n for n in (64, 32, 16) if rows % n == 0)
+
+            @pl.loop(0, rows // step)
+            def _(n):
+                at = pl.ds(pl.multiple_of(n * step, step), step)
+                mine[at, :] = (
+                    mine[at, :].astype(F32) + self.from_twin[z][at, :].astype(F32)
+                ).astype(LOW)
+
+            for copy in self.second[z][:2]:
+                copy.start()
+
+    def forward(self, *turns):
+        place = self.place
+        for z in turns or range(place.chips):
+            for copy in self.second[z][:2]:
+                copy.wait_recv()
+            theirs = self.part(self.shard(2 * z + place.core), place.far)
+            theirs[...] = (
+                theirs[...].astype(F32) + self.from_batch[1, z].astype(F32)
+            ).astype(LOW)
+            self.second[z][2].start()
+
+    def line(self):
+        place = self.place
+        for copies in self.second:
+            copies[2].wait_recv()
+        for k, z in enumerate(place.line):
+            mine = self.part(self.shard(2 * z + place.core), place.g)
+            total = mine[...].astype(F32)
+            for n in (0, 2):
+                total = total + self.from_batch[n, z].astype(F32)
+            self.partial[k] = total.astype(LOW)
+            if k:
+                self.third[k - 1].start()
+
+    def finish(self):
+        for copy in self.third:
+            copy.wait_recv()
+        total = self.partial[0].astype(F32)
+        for k in range(self.place.chips - 1):
+            total = total + self.from_line[k].astype(F32)
+        self.result[...] = total
+
+
+def slope_of(value):
+    sig = 0.5 * jnp.tanh(0.5 * value) + 0.5
+    return sig * (1.0 + value * (1.0 - sig))
+
+
+def column_of(shape, columns):
+    return lax.rem(lax.broadcasted_iota(jnp.int32, shape, 0), columns)
+
+
+def from_left(value, columns):
+    return jnp.where(
+        column_of(value.shape, columns) == 0, 0.0, pltpu.roll(value, 1, 0)
+    )
+
+
+def from_right(value, columns):
+    return jnp.where(
+        column_of(value.shape, columns) == columns - 1,
+        0.0,
+        pltpu.roll(value, value.shape[0] - 1, 0),
+    )
+
+
+def folded(value):
+    rows, width = value.shape
+    return jnp.sum(value.reshape(rows // 8, 8, width), axis=0)
+
+
+class Gather:
+    def __init__(self, net, place, shard, whole, local, dim=0):
+        self.net, self.place, self.shard, self.whole = net, place, shard, whole
+        self.dim, self.rows = dim, whole.shape[dim] // place.ranks
+        self.own = pltpu.make_async_copy(shard, self.block(place.s), local)
+        part = self.rows // place.groups
+        source = self.cut(shard, place.g * part, part)
+        self.first = [
+            net.plan(source, self.quarter(place.s, place.g), peer) for peer in place.line_peers
+        ]
+        self.second, self.third = [], [net.plan(shard, self.block(place.s), place.twin)]
+        for k in range(1, place.chips):
+            s = lax.rem(place.z + place.chips - k, place.chips) * 2 + place.core
+            view, passed = self.quarter(s, place.g), self.quarter(s, place.near)
+            self.second.append(
+                [
+                    net.plan(view, view, (place.near, place.s)),
+                    net.plan(view, view, (place.far, place.s)),
+                    net.plan(passed, passed, (place.far, place.s)),
+                ]
+            )
+            self.third.append(net.plan(self.block(s), self.block(s), place.twin))
+
+    def cut(self, ref, start, size):
+        at = pl.ds(pl.multiple_of(start, size), size)
+        return ref.at[at] if self.dim == 0 else ref.at[:, at]
+
+    def block(self, s):
+        return self.cut(self.whole, s * self.rows, self.rows)
+
+    def quarter(self, s, g):
+        part = self.rows // self.place.groups
+        return self.cut(self.whole, s * self.rows + g * part, part)
+
+    def line(self):
+        for copy in self.first:
+            copy.start()
+        self.own.start()
+        self.third[0].start()
+
+    def batch(self, *turns):
+        for k in turns or range(len(self.first)):
+            self.first[k].wait_recv()
+            for copy in self.second[k][:2]:
+                copy.start()
+
+    def forward(self, *turns):
+        for k in turns or range(len(self.first)):
+            self.second[k][0].wait_recv()
+            self.second[k][2].start()
+
+    def pair(self):
+        for k, copies in enumerate(self.second):
+            for copy in copies[1:]:
+                copy.wait_recv()
+            self.third[k + 1].start()
+
+    def sent(self):
+        return self.first + self.third + [c for copies in self.second for c in copies]
+
+    def ready(self):
+        self.own.wait()
+        for copy in self.third:
+            copy.wait_recv()
+
+
+def moments(total, width, total_count):
+    centre = gathered(total, 0, width // 4) / total_count
+    square = gathered(total, 1, width // 4) / total_count
+    return centre, lax.rsqrt(square - centre * centre + 1e-05)
+
+
+def sigma(value):
+    return 0.5 * jnp.tanh(0.5 * value) + 0.5
+
+
+def step_kernel(geometry, r):
+    cells, d_in, d_mid, columns, total_count, capacity, entries, samples, clips = geometry
+    place = Place()
+    net = Wires(r.send, r.recv)
+    ranks, groups = place.ranks, place.groups
+    half, size = d_in // 2, 2 * capacity
+    depth = d_in // ranks
+    entry = r.bank16.shape[0]
+    local = r.local
+    load_x = pltpu.make_async_copy(r.features, r.x, local.at[0])
+    load_x.start()
+    kv_weights = [rows_of(r.low_b, n, depth) for n in range(2)]
+    load_kv = [
+        pltpu.make_async_copy(source, target, local.at[9 + n])
+        for n, (source, target) in enumerate(zip((r.w_key, r.w_value), kv_weights))
+    ]
+    for copy in load_kv:
+        copy.start()
+    greet(place.row_peers + place.batch_peers)
+    a, b, c, q, o, h = (
+        Gather(net, place, shard, whole, local.at[n + 1], n // 5)
+        for n, (shard, whole) in enumerate(
+            (
+                (r.w_reduce, r.w_a),
+                (r.w_spatial, r.w_b),
+                (r.w_expand, r.w_c),
+                (r.w_query, r.w_q),
+                (r.w_out, r.w_o),
+                (r.w_head, r.w_h),
+            )
+        )
+    )
+    sums = [
+        Total(net, place, *refs)
+        for refs in (
+            (r.own1, r.rows1, r.mid1, r.batch1),
+            (r.own2, r.rows2, r.mid2, r.batch2),
+            (r.own3, r.rows3, r.mid3, r.batch3),
+            (r.own4, r.rows4, r.mid4, r.batch4),
+            (r.own5, r.rows5, r.mid5, r.batch5),
+            (r.own6, r.rows6, r.mid6, r.batch6),
+        )
+    ]
+    a.line()
+    b.line()
+
+    def at_block(s):
+        return pl.ds(pl.multiple_of(s * entry, entry), entry)
+
+    def at_depth(s):
+        return pl.ds(pl.multiple_of(s * depth, depth), depth)
+
+    r.bank16[...] = jnp.zeros_like(r.bank16)
+    r.bank16[0:entries, :] = r.bank[...]
+    for n in range(ranks):
+        r.box16[n, 0:1, 0:capacity] = r.piece_box[n : n + 1, :]
+    owner = lax.broadcasted_iota(jnp.int32, (ranks, 1), 0)
+    count = jnp.zeros((ranks, 1), jnp.int32)
+    for n in range(ranks):
+        count = jnp.where(owner == n, r.send_count[n], count)
+    for k in range(capacity):
+        on = slice(k * samples, (k + 1) * samples)
+        r.slot_cells[k] = r.sample_pos[:, on] + r.piece_clip[:, k : k + 1] * (cells // clips)
+        r.slot_weights[k] = jnp.where(k < count, r.sample_weight[:, on], 0.0)
+    asked = [
+        net.push(r.bank16.at[:, at_depth(peer[1])], rows_of(r.bank_cols, place.s, entry), peer)
+        for peer in place.row_peers
+    ]
+    named = [
+        net.push(r.box16.at[peer[1]], r.box_in.at[place.s], peer) for peer in place.row_peers
+    ]
+    r.bank_cols[at_block(place.s), :] = r.bank16[:, at_depth(place.s)]
+    mine = pl.ds(pl.multiple_of(place.s * size, size), size)
+    r.box_in[place.s] = r.box16[place.s]
+
+    by_rank = (capacity * ranks, ranks * size)
+    row, slot = (lax.broadcasted_iota(jnp.int32, by_rank, n) for n in range(2))
+    goal = lax.rem(row, ranks) * size + row // ranks
+    perms = [jnp.where(slot == goal + n * capacity, 1.0, 0.0).astype(LOW) for n in range(2)]
+
+    @pl.loop(0, capacity)
+    def _(k):
+        cell = lax.broadcasted_iota(jnp.int32, (ranks, cells), 1)
+        spots, weights = r.slot_cells[k], r.slot_weights[k]
+        total = jnp.zeros((ranks, cells), F32)
+        for j in range(samples):
+            total = total + jnp.where(cell == spots[:, j : j + 1], weights[:, j : j + 1], 0.0)
+        r.pieces[pl.ds(pl.multiple_of(k * ranks, ranks), ranks), 0:cells] = total
+
+    for n in range(2):
+        r.et[n] = tdot(r.pieces[0 : capacity * ranks, 0:cells].astype(LOW), perms[n]).astype(LOW)
+
+    a.batch()
+    a.forward()
+    b.batch(0)
+    a.pair()
+    load_x.wait()
+    a.ready()
+
+    acc = r.acc
+    acc[...] = jnp.zeros_like(acc)
+    big = 256
+    tiles = cells // big
+
+    @pl.loop(0, tiles)
+    def _(t):
+        at = pl.ds(pl.multiple_of(t * big, big), big)
+        value = jnp.dot(r.x[at, :], r.w_a[...], preferred_element_type=F32)
+        r.middle[at, :] = value
+        acc[0, :, 0:d_mid] += folded(value)
+        acc[1, :, 0:d_mid] += folded(value * value)
+
+    spread(r.own1, [jnp.sum(acc[n, :, 0:d_mid], axis=0, keepdims=True) for n in range(2)])
+    b.batch(1)
+    sums[0].start()
+    c.line()
+
+    def more_b():
+        b.batch(2)
+        b.forward(0, 1)
+
+    total = sums[0].finish(more_b)
+    centre, inverse = moments(total, d_mid, total_count)
+    gain, bias = r.gain_a[...], r.bias_a[...]
+    for n, value in enumerate((gain, bias, gain * inverse)):
+        r.norm_a[n : n + 1, :] = value
+
+    first, last = place.s == 0, place.s == ranks - 1
+    low_a, low_up, low_down = r.low_a, r.low_up, r.low_down
+
+    def halo(t, way):
+        at = pl.ds(pl.multiple_of(t * big, big), big)
+        return pltpu.make_async_remote_copy(
+            src_ref=low_a.at[at],
+            dst_ref=(low_up if way == 0 else low_down).at[at],
+            send_sem=r.halo_send.at[way, t],
+            recv_sem=r.halo_recv.at[way, t],
+            device_id=(place.g, place.s + 1 if way == 0 else place.s - 1),
+            device_id_type=MESH,
+        )
+
+    @pl.when(first)
+    def _():
+        low_up[...] = jnp.zeros_like(low_up)
+
+    @pl.when(last)
+    def _():
+        low_down[...] = jnp.zeros_like(low_down)
+
+    @pl.loop(0, tiles)
+    def _(t):
+        at = pl.ds(pl.multiple_of(t * big, big), big)
+        hat = (r.middle[at, :] - centre) * inverse
+        r.hat_a[at, :] = hat.astype(LOW)
+        act = gain * hat + bias
+        low_a[at, :] = (act * sigma(act)).astype(LOW)
+
+        @pl.when(jnp.logical_not(last))
+        def _():
+            halo(t, 0).start()
+
+        @pl.when(jnp.logical_not(first))
+        def _():
+            halo(t, 1).start()
+
+    keep_hat_a = pltpu.make_async_copy(r.hat_a, r.far_hat_a, local.at[8])
+    keep_hat_a.start()
+    c.batch()
+    b.forward(2)
+    for copy in asked:
+        copy.wait_recv()
+    for copy in load_kv:
+        copy.wait()
+    for n, weight in enumerate(kv_weights):
+        r.kv_part[n] = jnp.dot(
+            r.bank_cols[...], weight[...], preferred_element_type=F32
+        ).astype(LOW)
+
+    @pl.loop(0, tiles)
+    def _(t):
+        at = pl.ds(pl.multiple_of(t * big, big), big)
+        r.low_t[1, :, at] = jnp.transpose(low_a[at, :].astype(F32)).astype(LOW)
+
+    b.pair()
+    c.forward()
+    b.ready()
+    acc[...] = jnp.zeros_like(acc)
+
+    @pl.loop(0, tiles)
+    def _(t):
+        at = pl.ds(pl.multiple_of(t * big, big), big)
+
+        @pl.when(jnp.logical_not(first))
+        def _():
+            halo(t, 0).wait_recv()
+
+        @pl.when(jnp.logical_not(last))
+        def _():
+            halo(t, 1).wait_recv()
+
+        parts = []
+        for j in range(3):
+            taps = [r.w_b[(3 * i + j) * d_mid : (3 * i + j + 1) * d_mid, :] for i in range(3)]
+            parts.append(
+                jnp.dot(low_up[at, :], taps[0], preferred_element_type=F32)
+                + jnp.dot(low_a[at, :], taps[1], preferred_element_type=F32)
+                + jnp.dot(low_down[at, :], taps[2], preferred_element_type=F32)
+            )
+        value = from_left(parts[0], columns) + parts[1] + from_right(parts[2], columns)
+        r.middle[at, :] = value
+        acc[0, :, 0:d_mid] += folded(value)
+        acc[1, :, 0:d_mid] += folded(value * value)
+
+    spread(r.own2, [jnp.sum(acc[n, :, 0:d_mid], axis=0, keepdims=True) for n in range(2)])
+    sums[1].start()
+    q.line()
+    o.line()
+    h.line()
+
+    @pl.loop(0, tiles)
+    def _(t):
+        at = pl.ds(pl.multiple_of(t * big, big), big)
+        r.low_t[0, :, at] = jnp.transpose(low_up[at, :].astype(F32)).astype(LOW)
+        r.low_t[2, :, at] = jnp.transpose(low_down[at, :].astype(F32)).astype(LOW)
+
+    total = sums[1].finish()
+    centre, inverse = moments(total, d_mid, total_count)
+    gain, bias = r.gain_b[...], r.bias_b[...]
+    for n, value in enumerate((gain, bias, gain * inverse)):
+        r.norm_b[n : n + 1, :] = value
+    kv = [
+        net.plan(r.kv_part.at[:, at_block(peer[1])], r.kv_in.at[k], peer)
+        for k, peer in enumerate(place.row_peers)
+    ]
+    every = [
+        net.plan(r.kv_own, r.kv_all.at[:, at_block(place.s)], peer) for peer in place.row_peers
+    ]
+
+    def third_norm(pre_c):
+        c.pair()
+        c.ready()
+        acc[...] = jnp.zeros_like(acc)
+
+        @pl.loop(0, tiles)
+        def _(t):
+            at = pl.ds(pl.multiple_of(t * big, big), big)
+            hat = (r.middle[at, :] - centre) * inverse
+            r.hat_b[at, :] = hat.astype(LOW)
+            act = gain * hat + bias
+            low = (act * sigma(act)).astype(LOW)
+            r.low_b[at, :] = low
+            for k in range(4):
+                on = slice(k * (d_in // 4), (k + 1) * (d_in // 4))
+                value = jnp.dot(low, r.w_c[:, on], preferred_element_type=F32)
+                pre_c[at, on] = value
+                acc[0, :, on] += folded(value)
+                acc[1, :, on] += folded(value * value)
+
+        spread(r.own3, [jnp.sum(acc[n], axis=0, keepdims=True) for n in range(2)])
+        q.batch()
+        sums[2].start()
+        for copy in kv:
+            copy.start()
+
+        @pl.loop(0, tiles)
+        def _(t):
+            at = pl.ds(pl.multiple_of(t * big, big), big)
+            r.low_bt[:, at] = jnp.transpose(r.low_b[at, :].astype(F32)).astype(LOW)
+
+
+        def rest():
+            o.batch()
+            h.batch()
+            q.forward()
+
+        total = sums[2].finish(rest)
+        centre_wide, inverse_wide = moments(total, d_in, total_count)
+        r.scale_c[...] = r.gain_c[...] * inverse_wide
+        r.centre_c[0:1, :] = centre_wide
+        r.centre_c[1:2, :] = inverse_wide
+        for copy in kv:
+            copy.wait_recv()
+        for n in range(2):
+            total = r.kv_part[n, at_block(place.s), :].astype(F32)
+            for k in range(ranks - 1):
+                total = total + r.kv_in[k, n].astype(F32)
+            r.kv_own[n] = total.astype(LOW)
+            r.kv_all[n, at_block(place.s), :] = total.astype(LOW)
+        for copy in every:
+            copy.start()
+
+        q.pair()
+        o.forward()
+        h.forward()
+        r.pieces[...] = jnp.zeros_like(r.pieces)
+        tile = 128
+
+        @pl.loop(0, cells // tile)
+        def _(t):
+            at = pl.ds(pl.multiple_of(t * tile, tile), tile)
+            for k in range(4):
+                on = slice(k * (d_in // 4), (k + 1) * (d_in // 4))
+                into = slice((k % 2) * (d_in // 4), (k % 2 + 1) * (d_in // 4))
+                hat = (pre_c[at, on] - r.centre_c[0:1, on]) * r.centre_c[1:2, on]
+                r.hat_c[at, on] = hat.astype(LOW)
+                value = r.gain_c[:, on] * hat + r.bias_c[:, on] + r.x[at, on].astype(F32)
+                sig = sigma(value)
+                fmap = value * sig
+                r.x[at, on] = (sig + fmap * (1.0 - sig)).astype(LOW)
+                r.pieces[:, into] += tdot(r.et[k // 2, at, :], fmap.astype(LOW))
+
+
+    pl.run_scoped(third_norm, pltpu.VMEM((cells, d_in), F32))
+    r.blocks[...] = r.pieces[...].astype(LOW)
+    pushed = [
+        net.push(rows_of(r.blocks, peer[1], size), rows_of(r.arrived, place.s, size), peer)
+        for peer in place.row_peers
+    ]
+    r.arrived[mine, :] = r.blocks[mine, :]
+    o.pair()
+    h.pair()
+    for copy in named + every + pushed:
+        copy.wait_recv()
+
+    def block_rows(ref, count):
+        return lambda s: rows_of(ref, s, ref.shape[0] // count)
+
+    def by_columns(width):
+        return lambda view, g: view.at[:, pl.ds(pl.multiple_of(g * width, width), width)]
+
+    def by_rows(height):
+        return lambda view, g: view.at[pl.ds(pl.multiple_of(g * height, height), height)]
+
+    def scatter(key, shard, part, landing):
+        return Scatter(
+            net, place, shard, part, landing, *(getattr(r, n + key) for n in ("ba_", "pa_", "li_", "out_"))
+        )
+
+    per = cells // depth
+
+    def shard_a(s):
+        at = pl.ds(pl.multiple_of(lax.rem(s, per) * depth, depth), depth)
+        return r.low_t.at[s // per, :, at]
+
+    sc = {
+        "q": scatter("q", block_rows(r.w_q, ranks), by_columns(d_mid // groups), Corner(r.tw_q, depth, d_mid)),
+        "o": scatter("o", block_rows(r.w_o, ranks), by_columns(d_in // groups), r.tw_o.at),
+        "h": scatter("h", lambda s: r.g_h.at[s], by_rows(r.g_h.shape[1] // groups), r.tw_h.at),
+        "c": scatter("c", block_rows(r.w_c, ranks), by_columns(d_in // groups), r.tw_c.at),
+        "a": scatter("a", shard_a, by_rows(d_mid // groups), Corner(r.tw_q, r.tw_q.shape[0] // 2, depth)),
+    }
+    returned = [
+        net.plan(rows_of(r.blocks, peer[1], size), rows_of(r.back_in, place.s, size), peer)
+        for peer in place.row_peers
+    ]
+    asked_back = [
+        net.plan(r.kv_part.at[:, at_block(peer[1])], r.kv_in.at[k], peer)
+        for k, peer in enumerate(place.row_peers)
+    ]
+
+    def own_boxes(pooled, joined, d_branch, d_pooled):
+        boxes = r.cotangent.shape[1]
+        number = jnp.concatenate([r.box_in[n, 0:1, :] for n in range(ranks)], axis=0)
+        box = lax.broadcasted_iota(jnp.int32, (ranks, boxes), 1)
+        hits = jnp.concatenate(
+            [jnp.where(number[:, k : k + 1] == box, 1.0, 0.0) for k in range(capacity)], axis=0
+        ).astype(LOW)
+        picks = [tdot(perm, hits).astype(LOW) for perm in perms]
+        across = lax.broadcasted_iota(jnp.int32, (boxes, boxes), 0) == lax.broadcasted_iota(
+            jnp.int32, (boxes, boxes), 1
+        )
+
+        def upright(value):
+            wide = jnp.broadcast_to(value.astype(F32), (boxes, boxes))
+            return jnp.sum(jnp.where(across, wide, 0.0), axis=1, keepdims=True)
+
+        bank_row = lax.broadcasted_iota(jnp.int32, (boxes, ranks * entry), 1)
+        inner = lax.rem(bank_row, entry)
+        spot = (bank_row // entry * entries + inner).astype(F32)
+        start, length = upright(r.win_start[...]), upright(r.win_len[...])
+        window = (inner < entries) & (spot >= start) & (spot < start + length)
+        for k in range(2):
+            pooled[:, k * half : (k + 1) * half] = tdot(picks[k], r.arrived[...])
+        joined[:, 0:d_in] = pooled[...].astype(LOW)
+        pooled_low = joined.at[:, 0:d_in]
+        keys, vals = r.kv_all.at[0], r.kv_all.at[1]
+        scale = d_mid ** (-0.5)
+        q.ready()
+        queries = jnp.dot(pooled_low[...], r.w_q[...], preferred_element_type=F32).astype(LOW)
+        scores = jnp.where(window, ndot(queries, keys[...]) * scale, -1e30)
+        raised = jnp.exp(scores - jnp.max(scores, axis=1, keepdims=True))
+        attend = raised / jnp.sum(raised, axis=1, keepdims=True)
+        attend_low = attend.astype(LOW)
+        mixture = jnp.dot(attend_low, vals[...], preferred_element_type=F32)
+        centred = mixture - jnp.mean(mixture, axis=1, keepdims=True)
+        inverse_z = lax.rsqrt(jnp.mean(centred * centred, axis=1, keepdims=True) + 1e-05)
+        hat_z = centred * inverse_z
+        pre_ln = r.ln_gain[...] * hat_z + r.ln_bias[...]
+        sig_z = sigma(pre_ln)
+        low_r = (pre_ln * sig_z).astype(LOW)
+        slope_z = sig_z * (1.0 + pre_ln * (1.0 - sig_z))
+        o.ready()
+        for k in range(4):
+            on = slice(k * (d_in // 4), (k + 1) * (d_in // 4))
+            into = slice(d_in + k * (d_in // 4), d_in + (k + 1) * (d_in // 4))
+            joined[:, into] = (
+                pooled[:, on] + jnp.dot(low_r, r.w_o[:, on], preferred_element_type=F32)
+            ).astype(LOW)
+        h.ready()
+        logits = (
+            ndot(joined[...], r.w_h[...]) + r.head_bias[...]
+        )
+        likely = jax.nn.sigmoid(logits)
+        r.out_probs[...] = likely
+        d_logit = (jnp.transpose(r.cotangent[...]) * (likely * (1.0 - likely))).astype(LOW)
+        for k in range(4):
+            on = slice(k * (d_in // 4), (k + 1) * (d_in // 4))
+            below = slice(d_in + k * (d_in // 4), d_in + (k + 1) * (d_in // 4))
+            upper = jnp.dot(d_logit, r.w_h[:, below], preferred_element_type=F32)
+            d_branch[:, on] = upper.astype(LOW)
+            pooled[:, on] = (
+                jnp.dot(d_logit, r.w_h[:, on], preferred_element_type=F32) + upper
+            )
+        d_ln = ndot(d_branch[...], r.w_o[...]) * slope_z
+        d_hat = d_ln * r.ln_gain[...]
+        d_mixture = (
+            inverse_z
+            * (
+                d_hat
+                - jnp.mean(d_hat, axis=1, keepdims=True)
+                - hat_z * jnp.mean(d_hat * hat_z, axis=1, keepdims=True)
+            )
+        ).astype(LOW)
+        d_attend = ndot(d_mixture, vals[...])
+        d_scores = (attend * (d_attend - jnp.sum(d_attend * attend, axis=1, keepdims=True))).astype(LOW)
+        d_queries = (jnp.dot(d_scores, keys[...], preferred_element_type=F32) * scale).astype(LOW)
+        for k in range(4):
+            on = slice(k * (d_in // 4), (k + 1) * (d_in // 4))
+            d_pooled[:, on] = (pooled[:, on] + ndot(d_queries, r.w_q[on, :])).astype(LOW)
+        net.settle(pushed)
+        r.blocks[...] = (
+            jnp.dot(picks[0], d_pooled[:, 0:half], preferred_element_type=F32)
+            + jnp.dot(picks[1], d_pooled[:, half:d_in], preferred_element_type=F32)
+        ).astype(LOW)
+        for copy in returned:
+            copy.start()
+        r.back_in[mine, :] = r.blocks[mine, :]
+
+        net.settle(q.sent() + o.sent() + kv + every)
+        r.kv_part[0] = (tdot(d_scores, queries) * scale).astype(LOW)
+        r.kv_part[1] = tdot(attend_low, d_mixture).astype(LOW)
+        for k in range(4):
+            on = slice(k * (d_in // 4), (k + 1) * (d_in // 4))
+            r.w_q[on, :] = tdot(joined[:, on], d_queries).astype(LOW)
+            r.w_o[:, on] = tdot(low_r, d_branch[:, on]).astype(LOW)
+        width = 2 * depth
+        classes = d_logit.shape[1]
+        share = classes // groups
+        held, kind = (
+            lax.broadcasted_iota(jnp.int32, (classes, r.g_h.shape[1]), n) for n in range(2)
+        )
+        padded_class = held // share * (r.g_h.shape[1] // groups) + lax.rem(held, share)
+        spaced = jnp.where(kind == padded_class, 1.0, 0.0).astype(LOW)
+        d_spaced = jnp.dot(d_logit, spaced, preferred_element_type=F32).astype(LOW)
+        for s in range(ranks):
+            r.g_h[s] = tdot(d_spaced, joined[:, s * width : (s + 1) * width]).astype(LOW)
+        quarter = d_mid // 4
+        r.own4[...] = jnp.zeros_like(r.own4)
+        for n, value in enumerate(
+            (jnp.sum(d_ln * hat_z, axis=0, keepdims=True), jnp.sum(d_ln, axis=0, keepdims=True))
+        ):
+            for k in range(4):
+                r.own4[4 * n + k : 4 * n + k + 1, d_in // 4 : d_in // 4 + quarter] = value[
+                    :, k * quarter : (k + 1) * quarter
+                ]
+        r.own4[0:1, d_in // 4 + quarter : d_in // 4 + quarter + classes] = jnp.sum(
+            d_logit.astype(F32), axis=0, keepdims=True
+        )
+        sc["h"].pair()
+        sc["q"].pair()
+        sc["o"].pair()
+        for copy in asked_back:
+            copy.start()
+        sc["h"].batch()
+        sc["q"].batch()
+
+
+    boxes = r.cotangent.shape[1]
+    pl.run_scoped(
+        own_boxes,
+        pltpu.VMEM((boxes, d_in), F32),
+        pltpu.VMEM((boxes, 2 * d_in), LOW),
+        pltpu.VMEM((boxes, d_in), LOW),
+        pltpu.VMEM((boxes, d_in), LOW),
+    )
+    keep_hat_a.wait()
+    for copy in returned:
+        copy.wait_recv()
+
+    @pl.loop(0, tiles)
+    def _(t):
+        @pl.when(jnp.logical_not(last))
+        def _():
+            halo(t, 0).wait_send()
+
+        @pl.when(jnp.logical_not(first))
+        def _():
+            halo(t, 1).wait_send()
+
+    chips = place.chips
+    dkv, dkv_in, dkv_own, dkv_all = r.kv_part, r.kv_in, r.kv_own, r.kv_all
+
+    def backward(d_pre, g_b):
+        sc["b"] = scatter("b", block_rows(g_b, ranks), by_columns(d_mid // groups), r.tw_b.at)
+        hat_c, slope, d_c, back = r.hat_c, r.x, r.x, r.back_in
+        acc = r.acc
+        acc[...] = jnp.zeros_like(acc)
+        tile = 128
+
+        @pl.loop(0, cells // tile)
+        def _(t):
+            at = pl.ds(pl.multiple_of(t * tile, tile), tile)
+            for h in range(2):
+                on = slice(h * half, (h + 1) * half)
+                grad = jnp.dot(
+                    r.et[h, at, :], back[...], preferred_element_type=F32
+                ) * slope[at, on].astype(F32)
+                d_pre[at, on] = grad.astype(LOW)
+                acc[0, :, on] += folded(grad)
+                acc[1, :, on] += folded(grad * hat_c[at, on].astype(F32))
+
+        own4 = r.own4
+        spread(own4, [jnp.sum(acc[n], axis=0, keepdims=True) for n in range(2)])
+        sums[3].start()
+        sc["h"].forward()
+        sc["q"].forward()
+        for copy in asked_back:
+            copy.wait_recv()
+        own = pl.ds(pl.multiple_of(place.s * entry, entry), entry)
+        for n in range(2):
+            total = dkv[n, own, :].astype(F32)
+            for k in range(ranks - 1):
+                total = total + dkv_in[k, n].astype(F32)
+            dkv_own[n] = total.astype(LOW)
+            dkv_all[n, own, :] = total.astype(LOW)
+        shared = [
+            net.push(dkv_own, dkv_all.at[:, own], peer)
+            for peer in place.row_peers
+        ]
+
+        total = sums[3].finish(sc["o"].batch)
+        r.out_head[...] = total
+        shift_c = gathered(total, 0, d_in // 4) / total_count
+        gain_c = gathered(total, 1, d_in // 4) / total_count
+        scale_c = r.scale_c[...]
+
+        w_c, hat_b, d_act = r.w_c, r.hat_b, r.middle
+        acc[...] = jnp.zeros_like(acc)
+        norm_b, norm_a = r.norm_b, r.norm_a
+
+        @pl.loop(0, cells // tile)
+        def _(t):
+            at = pl.ds(pl.multiple_of(t * tile, tile), tile)
+            grad = scale_c * (
+                d_pre[at, :].astype(F32) - shift_c - hat_c[at, :].astype(F32) * gain_c
+            )
+            low = grad.astype(LOW)
+            d_c[at, :] = low
+            hat = hat_b[at, :].astype(F32)
+            back_b = ndot(low, w_c[...]) * slope_of(norm_b[0:1, :] * hat + norm_b[1:2, :])
+            d_act[at, :] = back_b
+            acc[0, :, 0:d_mid] += folded(back_b)
+            acc[1, :, 0:d_mid] += folded(back_b * hat)
+
+        reload = pltpu.make_async_copy(r.features, r.hat_c, local.at[20])
+        reload.start()
+        own5 = r.own5
+        spread(own5, [jnp.sum(acc[n, :, 0:d_mid], axis=0, keepdims=True) for n in range(2)])
+        sums[4].start()
+        net.settle(c.sent())
+        wide = 256
+
+        @pl.loop(0, d_in // wide)
+        def _(t):
+            at = pl.ds(pl.multiple_of(t * wide, wide), wide)
+            w_c[:, at] = jnp.dot(
+                r.low_bt[...], d_c[:, at], preferred_element_type=F32
+            ).astype(LOW)
+
+        sc["c"].pair()
+        sc["h"].line()
+        sc["q"].line()
+        for copy in shared:
+            copy.wait_recv()
+        kv_out, kv_in = r.kv_out, r.kv_back
+        for n in range(2):
+            kv_out[n] = tdot(r.bank_cols[...], dkv_all[n]).astype(LOW)
+        share = d_mid // groups
+        crossing = [
+            net.push(
+                kv_out.at[:, :, pl.ds(pl.multiple_of(peer[0] * share, share), share)], kv_in.at[k], peer
+            )
+            for k, peer in enumerate(place.batch_peers)
+        ]
+
+
+        def middle():
+            sc["o"].forward()
+            sc["c"].batch()
+
+        total = sums[4].finish(middle)
+        r.out_b_sums[...] = total
+        shift_b = gathered(total, 0, d_mid // 4) / total_count
+        gain_b = gathered(total, 1, d_mid // 4) / total_count
+
+        d_b, d_up, d_down = (r.low_up, r.low_a, r.low_down), r.low_b, r.hat_a
+
+        def halo_back(t, way):
+            at = pl.ds(pl.multiple_of(t * big, big), big)
+            return pltpu.make_async_remote_copy(
+                src_ref=d_b[1].at[at],
+                dst_ref=(d_up if way == 0 else d_down).at[at],
+                send_sem=r.back_send.at[way, t],
+                recv_sem=r.back_recv.at[way, t],
+                device_id=(place.g, place.s + 1 if way == 0 else place.s - 1),
+                device_id_type=MESH,
+            )
+
+        @pl.when(first)
+        def _():
+            d_up[...] = jnp.zeros_like(d_up)
+
+        @pl.when(last)
+        def _():
+            d_down[...] = jnp.zeros_like(d_down)
+
+        @pl.loop(0, tiles)
+        def _(t):
+            at = pl.ds(pl.multiple_of(t * big, big), big)
+            grad = norm_b[2:3, :] * (
+                d_act[at, :] - shift_b - hat_b[at, :].astype(F32) * gain_b
+            )
+            d_b[1][at, :] = grad.astype(LOW)
+
+            @pl.when(jnp.logical_not(last))
+            def _():
+                halo_back(t, 0).start()
+
+            @pl.when(jnp.logical_not(first))
+            def _():
+                halo_back(t, 1).start()
+
+            d_b[0][at, :] = from_right(grad, columns).astype(LOW)
+            d_b[2][at, :] = from_left(grad, columns).astype(LOW)
+
+        @pl.loop(0, 3)
+        def _(i):
+            for j in range(3):
+                at = pl.ds(pl.multiple_of((3 * i + j) * d_mid, d_mid), d_mid)
+                g_b[at, :] = jnp.dot(
+                    r.low_t[i], d_b[j][...], preferred_element_type=F32
+                ).astype(LOW)
+
+        more = pltpu.make_async_copy(r.far_hat_a, hat_b, local.at[18])
+        more.start()
+        sc["b"].pair()
+        sc["c"].forward()
+        sc["o"].line()
+        sc["b"].batch()
+
+        more.wait()
+        w_b, hat_a = r.w_b, hat_b
+        acc[...] = jnp.zeros_like(acc)
+
+        @pl.loop(0, tiles)
+        def _(t):
+            at = pl.ds(pl.multiple_of(t * big, big), big)
+
+            @pl.when(jnp.logical_not(first))
+            def _():
+                halo_back(t, 0).wait_recv()
+
+            @pl.when(jnp.logical_not(last))
+            def _():
+                halo_back(t, 1).wait_recv()
+
+            parts = []
+            for j in range(3):
+                taps = [w_b[(3 * i + j) * d_mid : (3 * i + j + 1) * d_mid, :] for i in range(3)]
+                parts.append(
+                    ndot(d_down[at, :], taps[0]) + ndot(d_b[1][at, :], taps[1]) + ndot(d_up[at, :], taps[2])
+                )
+            grad = from_right(parts[0], columns) + parts[1] + from_left(parts[2], columns)
+            hat = hat_a[at, :].astype(F32)
+            grad = grad * slope_of(norm_a[0:1, :] * hat + norm_a[1:2, :])
+            d_act[at, :] = grad
+            acc[0, :, 0:d_mid] += folded(grad)
+            acc[1, :, 0:d_mid] += folded(grad * hat)
+
+        own6 = r.own6
+        spread(own6, [jnp.sum(acc[n, :, 0:d_mid], axis=0, keepdims=True) for n in range(2)])
+        sums[5].start()
+        sc["c"].line()
+
+        def late():
+            sc["b"].forward()
+
+        total = sums[5].finish(late)
+        r.out_a_sums[...] = total
+        shift_a = gathered(total, 0, d_mid // 4) / total_count
+        gain_a = gathered(total, 1, d_mid // 4) / total_count
+        d_a, d_at = d_b[0], r.low_bt
+
+        @pl.loop(0, tiles)
+        def _(t):
+            at = pl.ds(pl.multiple_of(t * big, big), big)
+            grad = norm_a[2:3, :] * (
+                d_act[at, :] - shift_a - hat_a[at, :].astype(F32) * gain_a
+            )
+            d_a[at, :] = grad.astype(LOW)
+            d_at[:, at] = jnp.transpose(grad).astype(LOW)
+
+        reload.wait()
+        x = r.hat_c
+
+        @pl.loop(0, ranks)
+        def _(s):
+            shard_a(s)[...] = jnp.dot(
+                d_at[...],
+                x[:, pl.ds(pl.multiple_of(s * depth, depth), depth)],
+                preferred_element_type=F32,
+            ).astype(LOW)
+
+        sc["a"].pair()
+        sc["b"].line()
+        sc["a"].batch()
+        out_x = r.out_x
+
+        def leave(t):
+            at = pl.ds(pl.multiple_of(t * tile, tile), tile)
+            return pltpu.make_async_copy(d_pre.at[at], out_x.at[at], local.at[21 + t])
+
+        @pl.loop(0, cells // tile)
+        def _(t):
+            at = pl.ds(pl.multiple_of(t * tile, tile), tile)
+            d_pre[at, :] = (
+                ndot(d_a[at, :], r.w_a[...]) + d_pre[at, :].astype(F32)
+            ).astype(LOW)
+            leave(t).start()
+
+        sc["a"].forward()
+        for key in "qohcb":
+            sc[key].finish()
+        sc["a"].line()
+        for copy in crossing:
+            copy.wait_recv()
+        for n, key in enumerate((r.out_k, r.out_v)):
+            total = kv_out[n, :, pl.ds(pl.multiple_of(place.g * share, share), share)].astype(F32)
+            for k in range(groups - 1):
+                total = total + kv_in[k, n].astype(F32)
+            key[...] = total
+        sc["a"].finish()
+
+        @pl.loop(0, cells // tile)
+        def _(t):
+            leave(t).wait()
+
+        @pl.loop(0, tiles)
+        def _(t):
+            @pl.when(jnp.logical_not(last))
+            def _():
+                halo_back(t, 0).wait_send()
+
+            @pl.when(jnp.logical_not(first))
+            def _():
+                halo_back(t, 1).wait_send()
+
+        net.close()
+
+    pl.run_scoped(
+        backward,
+        pltpu.VMEM((cells, d_in), LOW),
+        pltpu.VMEM(r.w_b.shape, LOW),
+    )
+
+
+class Refs:
+    def __init__(self, names, refs, **more):
+        self.__dict__.update(zip(names, refs), **more)
+
+
+def run_kernel(body, geometry, channel, held, far, outs, far_outs, scratch):
+    anywhere = pl.BlockSpec(memory_space=pl.ANY)
+    inside = pl.BlockSpec(memory_space=pltpu.VMEM)
+    names = [*held, *far, *outs, *far_outs, *scratch]
+    scalars = pl.BlockSpec(memory_space=pltpu.SMEM)
+    results = pl.pallas_call(
+        lambda *refs: body(geometry, Refs(names, refs)),
+        out_shape=(*outs.values(), *far_outs.values()),
+        in_specs=[scalars if v.ndim == 1 else inside for v in held.values()] + [anywhere] * len(far),
+        out_specs=(inside,) * len(outs) + (anywhere,) * len(far_outs),
+        scratch_shapes=[*scratch.values()],
+        compiler_params=pltpu.CompilerParams(
+            collective_id=channel, has_side_effects=True, vmem_limit_bytes=64 << 20
+        ),
+    )(*held.values(), *far.values())
+    return Refs([*outs, *far_outs], results)
+
+
+def shape(kind, *sizes):
+    return jax.ShapeDtypeStruct(sizes, kind)
+
+
+def room(kind, *sizes):
+    return pltpu.VMEM(sizes, kind)
+
+
+def run_step(geometry, held, far):
+    cells, d_in, d_mid, columns, total_count, capacity, entries, samples, clips = geometry
+    groups, ranks = lax.axis_size("batch"), lax.axis_size("rows")
+    chips, dma = ranks // 2, pltpu.SemaphoreType.DMA
+    slots = ranks * 2 * capacity
+    entry = -(-entries // 16) * 16
+    bank = ranks * entry
+    classes, boxes = held["cotangent"].shape
+    spaced = groups * (-(-classes // groups // 16) * 16)
+    spatial = far["w_spatial"].shape[0] * ranks
+    half, depth = d_in // 2, d_in // ranks
+    head = d_in // 4 + d_mid // 4 + spaced
+    share = dict(
+        q=(d_in // ranks, d_mid // groups),
+        o=(d_mid // ranks, d_in // groups),
+        h=(spaced // groups, 2 * d_in // ranks),
+        c=(d_mid // ranks, d_in // groups),
+        b=(spatial // ranks, d_mid // groups),
+        a=(d_mid // groups, d_in // ranks),
+    )
+    block = dict(
+        q=(d_in // ranks, d_mid),
+        o=(d_mid // ranks, d_in),
+        h=(spaced, 2 * d_in // ranks),
+        c=(d_mid // ranks, d_in),
+        b=(spatial // ranks, d_mid),
+        a=(d_mid, d_in // ranks),
+    )
+    outs = dict(
+        out_probs=shape(F32, boxes, classes),
+        out_head=shape(F32, 8, head),
+        out_b_sums=shape(F32, 8, d_mid // 4),
+        out_a_sums=shape(F32, 8, d_mid // 4),
+        out_k=shape(F32, depth, d_mid // groups),
+        out_v=shape(F32, depth, d_mid // groups),
+    )
+    far_outs = dict(out_x=shape(LOW, cells, d_in), far_hat_a=shape(LOW, cells, d_mid))
+    scratch = dict(
+        x=room(LOW, cells, d_in),
+        hat_c=room(LOW, cells, d_in),
+        w_a=room(LOW, d_in, d_mid),
+        w_b=room(LOW, spatial, d_mid),
+        w_c=room(LOW, d_mid, d_in),
+        w_q=room(LOW, d_in, d_mid),
+        w_o=room(LOW, d_mid, d_in),
+        w_h=room(LOW, classes, 2 * d_in),
+        g_h=room(LOW, ranks, spaced, 2 * d_in // ranks),
+        middle=room(F32, cells, d_mid),
+        hat_a=room(LOW, cells, d_mid),
+        hat_b=room(LOW, cells, d_mid),
+        low_a=room(LOW, cells, d_mid),
+        low_up=room(LOW, cells, d_mid),
+        low_down=room(LOW, cells, d_mid),
+        low_b=room(LOW, cells, d_mid),
+        low_t=room(LOW, 3, d_mid, cells),
+        low_bt=room(LOW, d_mid, cells),
+        bank16=room(LOW, entry, d_in),
+        bank_cols=room(LOW, bank, depth),
+        box16=room(jnp.int32, ranks, 8, 128),
+        box_in=room(jnp.int32, ranks, 8, 128),
+        slot_cells=room(jnp.int32, capacity, ranks, samples),
+        slot_weights=room(F32, capacity, ranks, samples),
+        et=room(LOW, 2, cells, slots),
+        kv_part=room(LOW, 2, bank, d_mid),
+        kv_in=room(LOW, ranks - 1, 2, entry, d_mid),
+        kv_own=room(LOW, 2, entry, d_mid),
+        kv_all=room(LOW, 2, bank, d_mid),
+        kv_out=room(LOW, 2, depth, d_mid),
+        kv_back=room(LOW, groups - 1, 2, depth, d_mid // groups),
+        norm_a=room(F32, 8, d_mid),
+        norm_b=room(F32, 8, d_mid),
+        scale_c=room(F32, 1, d_in),
+        centre_c=room(F32, 8, d_in),
+        acc=room(F32, 2, 8, d_in),
+        pieces=room(F32, slots, half),
+        blocks=room(LOW, slots, half),
+        arrived=room(LOW, slots, half),
+        back_in=room(LOW, slots, half),
+        halo_send=dma((2, cells // 256)),
+        halo_recv=dma((2, cells // 256)),
+        back_send=dma((2, cells // 256)),
+        back_recv=dma((2, cells // 256)),
+        local=dma((32,)),
+        send=dma((400,)),
+        recv=dma((400,)),
+    )
+    scratch.update(tw_q=room(LOW, chips * depth, d_mid))
+    narrow = d_mid // 4
+    for n, width in enumerate((narrow, narrow, d_in // 4, head, narrow, narrow)):
+        scratch["own%d" % (n + 1)] = room(F32, 8, width)
+        scratch["mid%d" % (n + 1)] = room(F32, 8, width)
+        scratch["rows%d" % (n + 1)] = room(F32, ranks - 1, 8, width)
+        scratch["batch%d" % (n + 1)] = room(F32, groups - 1, 8, width)
+    for key in share:
+        outs["out_" + key] = shape(F32, *share[key])
+        if key not in "qa":
+            scratch["tw_" + key] = room(LOW, chips, *block[key])
+        scratch["ba_" + key] = room(LOW, groups - 1, chips, *share[key])
+        scratch["pa_" + key] = room(LOW, chips, *share[key])
+        scratch["li_" + key] = room(LOW, chips - 1, *share[key])
+    return run_kernel(step_kernel, geometry, 11, held, far, outs, far_outs, scratch)
+
+
+def finish_kernel(r):
+    chunk = r.in_x.shape[0] // 8
+
+    def across(n, leave):
+        at = pl.ds(n * chunk, chunk)
+        source, target = (r.stage, r.x) if leave else (r.in_x, r.stage)
+        return pltpu.make_async_copy(source.at[at], target.at[at], r.local.at[leave, n])
+
+    for n in range(8):
+        across(n, 0).start()
+    for n in range(8):
+        across(n, 0).wait()
+        across(n, 1).start()
+    r.probs[...] = jnp.transpose(r.in_probs[...])
+    r.a[...] = jnp.transpose(r.in_a[...])
+    r.b[...] = r.in_b[...]
+    r.c[...] = r.in_c[...]
+    r.q[...] = r.in_q[...]
+    r.k[...] = r.in_k[...]
+    r.v[...] = r.in_v[...]
+    r.o[...] = r.in_o[...]
+    r.h[...] = r.in_h[0 : r.h.shape[0], :]
+    r.bias_a[...], r.gain_a[...] = r.in_a_sums[0:4, :], r.in_a_sums[4:8, :]
+    r.bias_b[...], r.gain_b[...] = r.in_b_sums[0:4, :], r.in_b_sums[4:8, :]
+    lanes = r.ln_gain.shape[1]
+    per = r.gain_c.shape[0] // 4
+    for n in range(4):
+        for k in range(per):
+            on = slice(k * lanes, (k + 1) * lanes)
+            r.bias_c[per * n + k : per * n + k + 1, :] = r.in_head[n : n + 1, on]
+            r.gain_c[per * n + k : per * n + k + 1, :] = r.in_head[4 + n : 5 + n, on]
+    on = slice(per * lanes, (per + 1) * lanes)
+    r.ln_gain[...], r.ln_bias[...] = r.in_head[0:4, on], r.in_head[4:8, on]
+    at = (per + 1) * lanes
+    r.head_bias[...] = r.in_head[0:1, at : at + r.head_bias.shape[1]]
+    for n in range(8):
+        across(n, 1).wait()
+
+
+def run_finish(probs, two, groups, d_mid, classes):
+    held = dict(
+        in_probs=probs,
+        in_a=two.out_a,
+        in_b=two.out_b,
+        in_c=two.out_c,
+        in_q=two.out_q,
+        in_k=two.out_k,
+        in_v=two.out_v,
+        in_o=two.out_o,
+        in_h=two.out_h,
+        in_a_sums=two.out_a_sums,
+        in_b_sums=two.out_b_sums,
+        in_head=two.out_head,
+    )
+    like = lambda v: shape(F32, *v.shape)
+    lanes = two.out_a_sums.shape[1]
+    row = shape(F32, 4, lanes)
+    wide = shape(F32, 4 * (two.out_x.shape[1] // 4 // lanes), lanes)
+    outs = dict(
+        probs=shape(F32, *probs.shape[::-1]),
+        a=shape(F32, *two.out_a.shape[::-1]),
+        b=like(two.out_b),
+        c=like(two.out_c),
+        q=like(two.out_q),
+        k=like(two.out_k),
+        v=like(two.out_v),
+        o=like(two.out_o),
+        h=shape(F32, classes // groups, two.out_h.shape[1]),
+        gain_a=row,
+        bias_a=row,
+        gain_b=row,
+        bias_b=row,
+        gain_c=wide,
+        bias_c=wide,
+        ln_gain=row,
+        ln_bias=row,
+        head_bias=shape(F32, 1, classes),
+    )
+    far_outs = dict(x=shape(LOW, *two.out_x.shape))
+    anywhere = pl.BlockSpec(memory_space=pl.ANY)
+    inside = pl.BlockSpec(memory_space=pltpu.VMEM)
+    names = [*held, "in_x", *outs, *far_outs, "stage", "local"]
+    results = pl.pallas_call(
+        lambda *refs: finish_kernel(Refs(names, refs)),
+        out_shape=(*outs.values(), *far_outs.values()),
+        in_specs=[inside] * len(held) + [anywhere],
+        out_specs=(inside,) * len(outs) + (anywhere,),
+        scratch_shapes=[room(LOW, *two.out_x.shape), pltpu.SemaphoreType.DMA((2, 8))],
+        compiler_params=pltpu.CompilerParams(vmem_limit_bytes=64 << 20),
+    )(*held.values(), two.out_x)
+    return Refs([*outs, *far_outs], results)
+
+
+def fused_device(
+    features,
+    w_reduce,
+    w_spatial,
+    w_expand,
+    query_weight,
+    w_key,
+    w_value,
+    w_out,
+    w_head,
+    gain_a,
+    bias_a,
+    gain_b,
+    bias_b,
+    gain_c,
+    bias_c,
+    ln_gain,
+    ln_bias,
+    head_bias,
+    bank,
+    piece_box,
+    piece_clip,
+    send_count,
+    sample_pos,
+    sample_weight,
+    win_start,
+    win_len,
+    prob_cotangent,
+):
+    groups, ranks = lax.axis_size("batch"), lax.axis_size("rows")
+    clip_dev, row_dev, columns, d_in = features.shape
+    d_mid = w_reduce.shape[1]
+    cells = clip_dev * row_dev * columns
+    total_count = cells * ranks * groups
+    capacity = piece_box.shape[1]
+    samples = sample_pos.shape[1] // capacity
+    entries = bank.shape[0]
+    geometry = (cells, d_in, d_mid, columns, total_count, capacity, entries, samples, clip_dev)
+    line = lambda v: v.reshape(1, -1)
+    held = dict(
+        bank=bank,
+        piece_box=piece_box,
+        piece_clip=piece_clip,
+        send_count=send_count,
+        sample_pos=sample_pos,
+        sample_weight=sample_weight,
+        gain_a=line(gain_a),
+        bias_a=line(bias_a),
+        gain_b=line(gain_b),
+        bias_b=line(bias_b),
+        gain_c=line(gain_c),
+        bias_c=line(bias_c),
+        ln_gain=line(ln_gain),
+        ln_bias=line(ln_bias),
+        win_start=line(win_start),
+        win_len=line(win_len),
+        head_bias=line(head_bias),
+        cotangent=prob_cotangent.T,
+    )
+    far = dict(
+        features=features.reshape(cells, d_in),
+        w_reduce=w_reduce,
+        w_spatial=w_spatial,
+        w_expand=w_expand,
+        w_query=query_weight,
+        w_out=w_out,
+        w_head=w_head.T,
+        w_key=w_key,
+        w_value=w_value,
+    )
+    done = run_step(geometry, held, far)
+    last = run_finish(done.out_probs, done, groups, d_mid, prob_cotangent.shape[1])
+    flat = lambda v: v.reshape(-1)
+    return (
+        last.probs.T,
+        last.x.reshape(features.shape),
+        last.a,
+        last.b,
+        last.c,
+        last.q,
+        last.k,
+        last.v,
+        last.o,
+        last.h.T,
+        flat(last.gain_a),
+        flat(last.bias_a),
+        flat(last.gain_b),
+        flat(last.bias_b),
+        flat(last.gain_c),
+        flat(last.bias_c),
+        flat(last.ln_gain),
+        flat(last.ln_bias),
+        flat(last.head_bias),
+    )
+
+
+def plain_normalize(field, total_count):
     sums, squares = lax.psum((jnp.sum(field, 0), jnp.sum(field * field, 0)), ("batch", "rows"))
     centre_value = sums / total_count
     inverse = lax.rsqrt(squares / total_count - centre_value * centre_value + 1e-05)
     return ((field - centre_value) * inverse, inverse)
 
 
-def segment_totals(grad, normed):
+def plain_totals(grad, normed):
     return lax.psum((jnp.sum(grad, 0), jnp.sum(grad * normed, 0)), ("batch", "rows"))
 
 
-def norm_back(grad, normed, inverse, gain, shift_sum, gain_total_grad, total_count):
-    return (
-        gain * inverse * (grad - shift_sum / total_count - normed * gain_total_grad / total_count)
-    )
-
-
-def on_device(
+def plain_device(
     features,
     w_reduce,
     w_spatial,
@@ -122,7 +1550,7 @@
     d_mid = w_a.shape[1]
     flat_x = features.reshape(cell_count, d_in)
     pre_a = jnp.dot(flat_x, w_a, preferred_element_type=jnp.float32)
-    hat_a, inverse_a = normalize(pre_a, total_count)
+    hat_a, inverse_a = plain_normalize(pre_a, total_count)
     act_a = gain_a * hat_a + bias_a
     low_a = jax.nn.silu(act_a).astype(jnp.bfloat16)
     halo_a = padded(low_a.reshape(clip_dev, row_dev, col_count, d_mid), (("rows", 1),), 1)
@@ -136,11 +1564,11 @@
         axis=3,
     ).reshape(cell_count, 9 * d_mid)
     pre_b = jnp.dot(window_a, w_b, preferred_element_type=jnp.float32)
-    hat_b, inverse_b = normalize(pre_b, total_count)
+    hat_b, inverse_b = plain_normalize(pre_b, total_count)
     act_b = gain_b * hat_b + bias_b
     low_b = jax.nn.silu(act_b).astype(jnp.bfloat16)
     pre_c = jnp.dot(low_b, w_c, preferred_element_type=jnp.float32)
-    hat_c, inverse_c = normalize(pre_c, total_count)
+    hat_c, inverse_c = plain_normalize(pre_c, total_count)
     pre_out = gain_c * hat_c + bias_c + flat_x.astype(jnp.float32)
     fmap = jax.nn.silu(pre_out).astype(jnp.bfloat16)
     capacity = piece_box.shape[1]
@@ -251,7 +1679,7 @@
     ).astype(jnp.bfloat16)
     grad_wc = tdot(low_b, d_c)
     d_act_b = ndot(d_c, w_c) * silu_slope(act_b)
-    shift_b_sum, gain_b_sum = segment_totals(d_act_b, hat_b)
+    shift_b_sum, gain_b_sum = plain_totals(d_act_b, hat_b)
     d_b = norm_back(d_act_b, hat_b, inverse_b, gain_b, shift_b_sum, gain_b_sum, total_count).astype(
         jnp.bfloat16
     )
@@ -270,7 +1698,7 @@
     ).reshape(cell_count, 9 * d_mid)
     flipped = w_b.reshape(9, d_mid, d_mid).transpose(0, 2, 1).reshape(9 * d_mid, d_mid)
     d_act_a = jnp.dot(window_d, flipped, preferred_element_type=jnp.float32) * silu_slope(act_a)
-    shift_a_sum, gain_a_sum = segment_totals(d_act_a, hat_a)
+    shift_a_sum, gain_a_sum = plain_totals(d_act_a, hat_a)
     d_a = norm_back(d_act_a, hat_a, inverse_a, gain_a, shift_a_sum, gain_a_sum, total_count).astype(
         jnp.bfloat16
     )
@@ -333,6 +1761,11 @@
         head_sums[3],
         head_sums[4],
     )
+
+
+def on_device(*args):
+    fits = all(a.shape[0] % 64 == 0 for a in args[1:9]) and lax.axis_size("rows") % 2 == 0
+    return (fused_device if fits else plain_device)(*args)
 
 
 def solution(mesh):

time: 1020 us -> 217 us (0.21)
  waiting for transfers between devices: 395 us -> 0 us
  blocking collectives: 364 us -> 0 us
  Pallas kernels: 0 us -> 216 us
  matrix products: 128 us -> 0 us
  local copies, waits for them, and re-layouts: 45.6 us -> 0 us
  other arithmetic: 43.2 us -> 0 us
  starting transfers between devices: 18.9 us -> 0 us
  between operations: 17.1 us -> 0.84 us
    reduce_scatter x13 -> x0, waiting for transfers between devices: 285 us -> none  [the longest x1 98 us: on_device(): lax.psum_scatter(grad_wb, 'rows', scatter_dimension=0, tiled=True)]
    psum x6 -> x0, blocking collectives: 261 us -> none  [the longest x3 126 us: normalize(): lax.psum((jnp.sum(field, 0), jnp.sum(field * field, 0)), ('batch', 'rows'))]
    pallas_call x0 -> x2, Pallas kernels: none -> 216 us  [the longest x1 210 us: run_kernel(): pl.pallas_call(lambda *refs: body(geometry, Refs(names, refs)), out_shape...]
    dot_general x31 -> x0, matrix products: 128 us -> none  [the longest x11 49.2 us: tdot(): lax.dot_general(left, right, (((0,), (0,)), ((), ())), preferred_element_...]
    unnamed x26 -> x0, waiting for transfers between devices: 88.4 us -> none
    all_gather x3 -> x0, blocking collectives: 69.4 us -> none  [the longest x1 39.7 us: on_device(): lax.all_gather(w_head, 'rows', axis=0, tiled=True)]
    all_to_all x2 -> x0, blocking collectives: 33.3 us -> none  [the longest x1 17 us: on_device(): lax.all_to_all(back_pieces, 'rows', split_axis=0, concat_axis=0, tiled=True)]
    convert_element_type x20 -> x0, other arithmetic: 32.3 us -> none  [the longest x1 7.4 us: on_device(): d_c = norm_back(d_pre, hat_c, inverse_c, gain_c, head_sums[0], head_sums[...]
  transfers between devices with their start and end apart: 29 -> 0, of which waited for: 12 -> 0; matrix products, arithmetic and copies ran while one was open for 20% -> 0% of each run, Pallas kernels for 0% -> 0%
where the time goes in v4:
time: 217 us
  Pallas kernels  216 us (100%)
    pallas_call x1, Pallas kernels, run_kernel(): pl.pallas_call(lambda *refs: body(geometry, Refs(names, refs)), out_shape...  210 us
    pallas_call x1, Pallas kernels, run_finish(): pl.pallas_call(lambda *refs: finish_kernel(Refs(names, refs)), out_shape=...  5.96 us

profile of v4, /device:TPU:0, one launch (start us, length us, event | category | flops | bytes accessed | tf_op | source)
XLA Modules:
  0.0 217.1 jit_solution(5360344171632361921)
XLA Ops:
  0.7 210.3 %shard_map.402 = (f32[128,80]{1,0:T(8,128)}, f32[8,768]{1,0:T(8,128)}, f32[8,128]{1,0:T(8,128)}, f32[8,128]{1,0:T(8,128)}, f32[256,128]{1,0:T(8,128)}, /*index=5...) custom-call(bf16[10,2048]{1,0:T(8,128)(2,1)} %refs_0_.1, ...), custom_call_target="tpu_custom_call" | custom-call | tf_op jit(solution)/shard_map/pallas_call | solution.py:1183
  211.0 6.0 %shard_map.403 = (f32[80,128]{1,0:T(8,128)}, f32[256,128]{1,0:T(8,128)}, f32[576,128]{1,0:T(8,128)}, f32[64,512]{1,0:T(8,128)}, f32[256,128]{1,0:T(8,128)}, /*in...) custom-call(f32[128,80]{1,0:T(8,128)} %get-tuple-element.51.refs_0_,, ...), custom_call_target="tpu_custom_call" | custom-call | tf_op jit(solution)/shard_map/pallas_call | solution.py:1389

commit v5 on v4

--- a/solution.py
+++ b/solution.py
@@ -74,14 +74,14 @@
 
 class Wires:
     def __init__(self, send, recv):
-        self.send, self.recv, self.at, self.open = send, recv, 0, []
-
-    def plan(self, source, target, peer):
+        self.send, self.recv, self.at, self.open, self.some = send, recv, 0, [], []
+
+    def plan(self, source, target, peer, land=None):
         copy = pltpu.make_async_remote_copy(
             src_ref=source,
             dst_ref=target,
             send_sem=self.send.at[self.at],
-            recv_sem=self.recv.at[self.at],
+            recv_sem=self.recv.at[self.at if land is None else land],
             device_id=peer,
             device_id_type=MESH,
         )
@@ -89,6 +89,21 @@
         self.open.append(copy)
         return copy
 
+    def waiter(self, like, land, peer):
+        return pltpu.make_async_remote_copy(
+            src_ref=like,
+            dst_ref=like,
+            send_sem=self.send.at[0],
+            recv_sem=self.recv.at[land],
+            device_id=peer,
+            device_id_type=MESH,
+        )
+
+    def only_where(self, where, copy):
+        self.open.pop()
+        self.some.append((where, copy))
+        return where, copy
+
     def push(self, source, target, peer):
         return start(self.plan(source, target, peer))
 
@@ -98,9 +113,20 @@
         done = {id(copy) for copy in copies}
         self.open = [copy for copy in self.open if id(copy) not in done]
 
+    def settle_some(self, pairs):
+        for where, copy in pairs:
+
+            @pl.when(where)
+            def _():
+                copy.wait_send()
+
+        done = {id(copy) for where, copy in pairs}
+        self.some = [pair for pair in self.some if id(pair[1]) not in done]
+
     def close(self):
         for copy in self.open:
             copy.wait_send()
+        self.settle_some(self.some)
 
 
 def start(copy):
@@ -157,6 +183,9 @@
     def start(self):
         for copy in self.rows:
             copy.start()
+
+    def sent(self):
+        return self.rows + self.batch
 
     def finish(self, behind=None):
         for copy in self.rows:
@@ -225,6 +254,9 @@
             for k, peer in enumerate(place.line_peers)
         ]
 
+    def sent(self, steps):
+        return self.first + [copy for copies in self.second for copy in copies[:steps]]
+
     def pair(self):
         for copy in self.first:
             copy.start()
@@ -309,17 +341,21 @@
 
 
 class Gather:
-    def __init__(self, net, place, shard, whole, local, dim=0):
+    def __init__(self, net, place, shard, whole, local, dim=0, relayed=False):
         self.net, self.place, self.shard, self.whole = net, place, shard, whole
         self.dim, self.rows = dim, whole.shape[dim] // place.ranks
         self.own = pltpu.make_async_copy(shard, self.block(place.s), local)
         part = self.rows // place.groups
         source = self.cut(shard, place.g * part, part)
-        self.first = [
-            net.plan(source, self.quarter(place.s, place.g), peer) for peer in place.line_peers
-        ]
+        self.relayed, self.some = relayed and place.chips == 4, []
+        if self.relayed:
+            self.plan_relay(net, source)
+        else:
+            self.first = [
+                net.plan(source, self.quarter(place.s, place.g), peer) for peer in place.line_peers
+            ]
         self.second, self.third = [], [net.plan(shard, self.block(place.s), place.twin)]
-        for k in range(1, place.chips):
+        for k in self.order if self.relayed else range(1, place.chips):
             s = lax.rem(place.z + place.chips - k, place.chips) * 2 + place.core
             view, passed = self.quarter(s, place.g), self.quarter(s, place.near)
             self.second.append(
@@ -331,6 +367,55 @@
             )
             self.third.append(net.plan(self.block(s), self.block(s), place.twin))
 
+    def plan_relay(self, net, source):
+        place, z, base = self.place, self.place.z, net.at
+        right, left = (
+            (place.g, lax.rem(z + n, 4) * 2 + place.core) for n in (1, 3)
+        )
+        mine = self.quarter(place.s, place.g)
+        passed = [
+            self.quarter(lax.rem(z + 4 - k, 4) * 2 + place.core, place.g) for k in (1, 2, 3)
+        ]
+        self.inner = (z == 1) | (z == 2)
+        first = 1 + (3 - z) // 3 * 2
+        then = 2 + lax.rem((z + 1) // 2, 2)
+        self.order = (first, then, 6 - first - then)
+        self.arrivals = [net.waiter(passed[0], base + k - 1, place.twin) for k in self.order]
+        steps = (
+            (z < 3, source, mine, right, base),
+            (self.inner, passed[0], passed[0], right, base + 1),
+            (z > 0, source, mine, left, base + 2),
+            (self.inner, passed[2], passed[2], left, base + 1),
+            (z == 2, passed[1], passed[1], right, base + 2),
+            (z == 1, passed[1], passed[1], left, base),
+        )
+        for where, origin, goal, peer, land in steps:
+            self.some.append(net.only_where(where, net.plan(origin, goal, peer, land)))
+        self.first = [copy for where, copy in self.some[:3]]
+
+    def go(self, n):
+        where, copy = self.some[n]
+
+        @pl.when(where)
+        def _():
+            copy.start()
+
+    def relay(self):
+        @pl.when(self.inner)
+        def _():
+            self.first[0].wait_recv()
+            self.some[1][1].start()
+            self.first[2].wait_recv()
+            self.some[3][1].start()
+
+    def relay_last(self):
+        @pl.when(self.inner)
+        def _():
+            self.first[1].wait_recv()
+
+        self.go(4)
+        self.go(5)
+
     def cut(self, ref, start, size):
         at = pl.ds(pl.multiple_of(start, size), size)
         return ref.at[at] if self.dim == 0 else ref.at[:, at]
@@ -343,14 +428,25 @@
         return self.cut(self.whole, s * self.rows + g * part, part)
 
     def line(self):
-        for copy in self.first:
-            copy.start()
+        if self.relayed:
+            self.go(0)
+            self.go(2)
+        else:
+            for copy in self.first:
+                copy.start()
         self.own.start()
         self.third[0].start()
 
     def batch(self, *turns):
         for k in turns or range(len(self.first)):
-            self.first[k].wait_recv()
+            if self.relayed:
+
+                @pl.when(jnp.logical_not(self.inner))
+                def _():
+                    self.arrivals[k].wait_recv()
+
+            else:
+                self.first[k].wait_recv()
             for copy in self.second[k][:2]:
                 copy.start()
 
@@ -366,7 +462,7 @@
             self.third[k + 1].start()
 
     def sent(self):
-        return self.first + self.third + [c for copies in self.second for c in copies]
+        return ([] if self.relayed else self.first) + self.third + [c for copies in self.second for c in copies]
 
     def ready(self):
         self.own.wait()
@@ -404,7 +500,7 @@
         copy.start()
     greet(place.row_peers + place.batch_peers)
     a, b, c, q, o, h = (
-        Gather(net, place, shard, whole, local.at[n + 1], n // 5)
+        Gather(net, place, shard, whole, local.at[n + 1], n // 5, n in (1, 3, 4, 5))
         for n, (shard, whole) in enumerate(
             (
                 (r.w_reduce, r.w_a),
@@ -428,7 +524,6 @@
         )
     ]
     a.line()
-    b.line()
 
     def at_block(s):
         return pl.ds(pl.multiple_of(s * entry, entry), entry)
@@ -438,6 +533,11 @@
 
     r.bank16[...] = jnp.zeros_like(r.bank16)
     r.bank16[0:entries, :] = r.bank[...]
+    asked = [
+        net.push(r.bank16.at[:, at_depth(peer[1])], rows_of(r.bank_cols, place.s, entry), peer)
+        for peer in place.row_peers
+    ]
+    b.line()
     for n in range(ranks):
         r.box16[n, 0:1, 0:capacity] = r.piece_box[n : n + 1, :]
     owner = lax.broadcasted_iota(jnp.int32, (ranks, 1), 0)
@@ -448,10 +548,6 @@
         on = slice(k * samples, (k + 1) * samples)
         r.slot_cells[k] = r.sample_pos[:, on] + r.piece_clip[:, k : k + 1] * (cells // clips)
         r.slot_weights[k] = jnp.where(k < count, r.sample_weight[:, on], 0.0)
-    asked = [
-        net.push(r.bank16.at[:, at_depth(peer[1])], rows_of(r.bank_cols, place.s, entry), peer)
-        for peer in place.row_peers
-    ]
     named = [
         net.push(r.box16.at[peer[1]], r.box_in.at[place.s], peer) for peer in place.row_peers
     ]
@@ -477,82 +573,12 @@
         r.et[n] = tdot(r.pieces[0 : capacity * ranks, 0:cells].astype(LOW), perms[n]).astype(LOW)
 
     a.batch()
+    b.relay()
     a.forward()
     b.batch(0)
     a.pair()
-    load_x.wait()
-    a.ready()
-
-    acc = r.acc
-    acc[...] = jnp.zeros_like(acc)
-    big = 256
-    tiles = cells // big
-
-    @pl.loop(0, tiles)
-    def _(t):
-        at = pl.ds(pl.multiple_of(t * big, big), big)
-        value = jnp.dot(r.x[at, :], r.w_a[...], preferred_element_type=F32)
-        r.middle[at, :] = value
-        acc[0, :, 0:d_mid] += folded(value)
-        acc[1, :, 0:d_mid] += folded(value * value)
-
-    spread(r.own1, [jnp.sum(acc[n, :, 0:d_mid], axis=0, keepdims=True) for n in range(2)])
+    b.relay_last()
     b.batch(1)
-    sums[0].start()
-    c.line()
-
-    def more_b():
-        b.batch(2)
-        b.forward(0, 1)
-
-    total = sums[0].finish(more_b)
-    centre, inverse = moments(total, d_mid, total_count)
-    gain, bias = r.gain_a[...], r.bias_a[...]
-    for n, value in enumerate((gain, bias, gain * inverse)):
-        r.norm_a[n : n + 1, :] = value
-
-    first, last = place.s == 0, place.s == ranks - 1
-    low_a, low_up, low_down = r.low_a, r.low_up, r.low_down
-
-    def halo(t, way):
-        at = pl.ds(pl.multiple_of(t * big, big), big)
-        return pltpu.make_async_remote_copy(
-            src_ref=low_a.at[at],
-            dst_ref=(low_up if way == 0 else low_down).at[at],
-            send_sem=r.halo_send.at[way, t],
-            recv_sem=r.halo_recv.at[way, t],
-            device_id=(place.g, place.s + 1 if way == 0 else place.s - 1),
-            device_id_type=MESH,
-        )
-
-    @pl.when(first)
-    def _():
-        low_up[...] = jnp.zeros_like(low_up)
-
-    @pl.when(last)
-    def _():
-        low_down[...] = jnp.zeros_like(low_down)
-
-    @pl.loop(0, tiles)
-    def _(t):
-        at = pl.ds(pl.multiple_of(t * big, big), big)
-        hat = (r.middle[at, :] - centre) * inverse
-        r.hat_a[at, :] = hat.astype(LOW)
-        act = gain * hat + bias
-        low_a[at, :] = (act * sigma(act)).astype(LOW)
-
-        @pl.when(jnp.logical_not(last))
-        def _():
-            halo(t, 0).start()
-
-        @pl.when(jnp.logical_not(first))
-        def _():
-            halo(t, 1).start()
-
-    keep_hat_a = pltpu.make_async_copy(r.hat_a, r.far_hat_a, local.at[8])
-    keep_hat_a.start()
-    c.batch()
-    b.forward(2)
     for copy in asked:
         copy.wait_recv()
     for copy in load_kv:
@@ -561,7 +587,98 @@
         r.kv_part[n] = jnp.dot(
             r.bank_cols[...], weight[...], preferred_element_type=F32
         ).astype(LOW)
-
+    load_x.wait()
+    a.ready()
+
+    acc = r.acc
+    acc[...] = jnp.zeros_like(acc)
+    big = 256
+    tiles = cells // big
+
+    @pl.loop(0, tiles)
+    def _(t):
+        at = pl.ds(pl.multiple_of(t * big, big), big)
+        value = jnp.dot(r.x[at, :], r.w_a[...], preferred_element_type=F32)
+        r.middle[at, :] = value
+        acc[0, :, 0:d_mid] += folded(value)
+        acc[1, :, 0:d_mid] += folded(value * value)
+
+    spread(r.own1, [jnp.sum(acc[n, :, 0:d_mid], axis=0, keepdims=True) for n in range(2)])
+    own_mean = jnp.sum(acc[0, :, 0:d_mid], axis=0, keepdims=True) / cells
+
+    first, last = place.s == 0, place.s == ranks - 1
+    low_a, low_up, low_down = r.low_a, r.low_up, r.low_down
+
+    def halo(t, way):
+        at = pl.ds(pl.multiple_of(t * big, big), big)
+        return pltpu.make_async_remote_copy(
+            src_ref=r.low_b.at[at],
+            dst_ref=(low_up if way == 0 else low_down).at[at],
+            send_sem=r.halo_send.at[way, t],
+            recv_sem=r.halo_recv.at[way, t],
+            device_id=(place.g, place.s + 1 if way == 0 else place.s - 1),
+            device_id_type=MESH,
+        )
+
+    @pl.when(first)
+    def _():
+        low_up[...] = jnp.zeros_like(low_up)
+
+    @pl.when(last)
+    def _():
+        low_down[...] = jnp.zeros_like(low_down)
+
+    @pl.loop(0, tiles)
+    def _(t):
+        at = pl.ds(pl.multiple_of(t * big, big), big)
+        r.low_b[at, :] = (r.middle[at, :] - own_mean).astype(LOW)
+
+    b.forward(0)
+    b.batch(2)
+    sums[0].start()
+    c.line()
+
+    @pl.loop(0, tiles)
+    def _(t):
+        @pl.when(jnp.logical_not(last))
+        def _():
+            halo(t, 0).start()
+
+        @pl.when(jnp.logical_not(first))
+        def _():
+            halo(t, 1).start()
+
+
+    def more_b():
+        b.forward(1)
+
+    total = sums[0].finish(more_b)
+    centre, inverse = moments(total, d_mid, total_count)
+    gain, bias = r.gain_a[...], r.bias_a[...]
+    for n, value in enumerate((gain, bias, gain * inverse)):
+        r.norm_a[n : n + 1, :] = value
+
+    @pl.loop(0, tiles)
+    def _(t):
+        at = pl.ds(pl.multiple_of(t * big, big), big)
+        hat = (r.middle[at, :] - centre) * inverse
+        r.hat_a[at, :] = hat.astype(LOW)
+        act = gain * hat + bias
+        low_a[at, :] = (act * sigma(act)).astype(LOW)
+
+    beyond = [
+        (
+            low,
+            gathered(r.rows1[n], 0, d_mid // 4) / cells - centre,
+            jnp.where(edge, 0.0, 1.0),
+        )
+        for low, n, edge in ((low_up, 0, first), (low_down, ranks - 2, last))
+    ]
+
+    keep_hat_a = pltpu.make_async_copy(r.hat_a, r.far_hat_a, local.at[8])
+    keep_hat_a.start()
+    b.forward(2)
+    c.batch()
     @pl.loop(0, tiles)
     def _(t):
         at = pl.ds(pl.multiple_of(t * big, big), big)
@@ -584,6 +701,9 @@
         def _():
             halo(t, 1).wait_recv()
 
+        for low, offset, inside in beyond:
+            act = gain * ((low[at, :].astype(F32) + offset) * inverse) + bias
+            low[at, :] = (act * sigma(act) * inside).astype(LOW)
         parts = []
         for j in range(3):
             taps = [r.w_b[(3 * i + j) * d_mid : (3 * i + j + 1) * d_mid, :] for i in range(3)]
@@ -599,6 +719,7 @@
 
     spread(r.own2, [jnp.sum(acc[n, :, 0:d_mid], axis=0, keepdims=True) for n in range(2)])
     sums[1].start()
+    net.settle(sums[0].sent() + asked + named + a.sent())
     q.line()
     o.line()
     h.line()
@@ -610,6 +731,8 @@
         r.low_t[2, :, at] = jnp.transpose(low_down[at, :].astype(F32)).astype(LOW)
 
     total = sums[1].finish()
+    for gather in (q, o, h):
+        gather.relay()
     centre, inverse = moments(total, d_mid, total_count)
     gain, bias = r.gain_b[...], r.bias_b[...]
     for n, value in enumerate((gain, bias, gain * inverse)):
@@ -621,6 +744,16 @@
     every = [
         net.plan(r.kv_own, r.kv_all.at[:, at_block(place.s)], peer) for peer in place.row_peers
     ]
+
+    @pl.loop(0, tiles)
+    def _(t):
+        @pl.when(jnp.logical_not(last))
+        def _():
+            halo(t, 0).wait_send()
+
+        @pl.when(jnp.logical_not(first))
+        def _():
+            halo(t, 1).wait_send()
 
     def third_norm(pre_c):
         c.pair()
@@ -643,8 +776,11 @@
                 acc[1, :, on] += folded(value * value)
 
         spread(r.own3, [jnp.sum(acc[n], axis=0, keepdims=True) for n in range(2)])
-        q.batch()
+        for gather in (q, o, h):
+            gather.relay_last()
         sums[2].start()
+        net.settle(sums[1].sent() + b.sent())
+        net.settle_some(b.some)
         for copy in kv:
             copy.start()
 
@@ -655,9 +791,8 @@
 
 
         def rest():
-            o.batch()
-            h.batch()
-            q.forward()
+            for gather in (q, o, h):
+                gather.batch()
 
         total = sums[2].finish(rest)
         centre_wide, inverse_wide = moments(total, d_in, total_count)
@@ -675,15 +810,13 @@
         for copy in every:
             copy.start()
 
-        q.pair()
-        o.forward()
-        h.forward()
+        q.forward()
         r.pieces[...] = jnp.zeros_like(r.pieces)
         tile = 128
 
-        @pl.loop(0, cells // tile)
+        @pl.loop(0, cells // 256)
         def _(t):
-            at = pl.ds(pl.multiple_of(t * tile, tile), tile)
+            at = pl.ds(pl.multiple_of(t * 256, 256), 256)
             for k in range(4):
                 on = slice(k * (d_in // 4), (k + 1) * (d_in // 4))
                 into = slice((k % 2) * (d_in // 4), (k % 2 + 1) * (d_in // 4))
@@ -697,12 +830,15 @@
 
 
     pl.run_scoped(third_norm, pltpu.VMEM((cells, d_in), F32))
+    o.forward()
+    h.forward()
     r.blocks[...] = r.pieces[...].astype(LOW)
     pushed = [
         net.push(rows_of(r.blocks, peer[1], size), rows_of(r.arrived, place.s, size), peer)
         for peer in place.row_peers
     ]
     r.arrived[mine, :] = r.blocks[mine, :]
+    q.pair()
     o.pair()
     h.pair()
     for copy in named + every + pushed:
@@ -833,6 +969,7 @@
         r.back_in[mine, :] = r.blocks[mine, :]
 
         net.settle(q.sent() + o.sent() + kv + every)
+        net.settle_some(q.some + o.some)
         r.kv_part[0] = (tdot(d_scores, queries) * scale).astype(LOW)
         r.kv_part[1] = tdot(attend_low, d_mixture).astype(LOW)
         for k in range(4):
@@ -883,16 +1020,6 @@
     for copy in returned:
         copy.wait_recv()
 
-    @pl.loop(0, tiles)
-    def _(t):
-        @pl.when(jnp.logical_not(last))
-        def _():
-            halo(t, 0).wait_send()
-
-        @pl.when(jnp.logical_not(first))
-        def _():
-            halo(t, 1).wait_send()
-
     chips = place.chips
     dkv, dkv_in, dkv_own, dkv_all = r.kv_part, r.kv_in, r.kv_own, r.kv_all
 
@@ -918,6 +1045,8 @@
         own4 = r.own4
         spread(own4, [jnp.sum(acc[n], axis=0, keepdims=True) for n in range(2)])
         sums[3].start()
+        net.settle(sums[2].sent() + returned + h.sent())
+        net.settle_some(h.some)
         sc["h"].forward()
         sc["q"].forward()
         for copy in asked_back:
@@ -944,9 +1073,9 @@
         acc[...] = jnp.zeros_like(acc)
         norm_b, norm_a = r.norm_b, r.norm_a
 
-        @pl.loop(0, cells // tile)
+        @pl.loop(0, cells // 256)
         def _(t):
-            at = pl.ds(pl.multiple_of(t * tile, tile), tile)
+            at = pl.ds(pl.multiple_of(t * 256, 256), 256)
             grad = scale_c * (
                 d_pre[at, :].astype(F32) - shift_c - hat_c[at, :].astype(F32) * gain_c
             )
@@ -963,6 +1092,8 @@
         own5 = r.own5
         spread(own5, [jnp.sum(acc[n, :, 0:d_mid], axis=0, keepdims=True) for n in range(2)])
         sums[4].start()
+        net.settle(sums[3].sent() + asked_back)
+        net.settle([copy for key in "hqo" for copy in sc[key].sent(3 if key in "hq" else 2)])
         net.settle(c.sent())
         wide = 256
 
@@ -981,16 +1112,21 @@
         kv_out, kv_in = r.kv_out, r.kv_back
         for n in range(2):
             kv_out[n] = tdot(r.bank_cols[...], dkv_all[n]).astype(LOW)
+
+
         share = d_mid // groups
         crossing = [
-            net.push(
-                kv_out.at[:, :, pl.ds(pl.multiple_of(peer[0] * share, share), share)], kv_in.at[k], peer
+            net.plan(
+                kv_out.at[:, :, pl.ds(pl.multiple_of(peer[0] * share, share), share)],
+                kv_in.at[k],
+                peer,
             )
             for k, peer in enumerate(place.batch_peers)
         ]
 
-
         def middle():
+            for copy in crossing:
+                copy.start()
             sc["o"].forward()
             sc["c"].batch()
 
@@ -1086,6 +1222,9 @@
         own6 = r.own6
         spread(own6, [jnp.sum(acc[n, :, 0:d_mid], axis=0, keepdims=True) for n in range(2)])
         sums[5].start()
+        net.settle(sums[4].sent() + shared + crossing)
+        net.settle(sc["c"].sent(3) + sc["b"].sent(2) + sc["h"].third + sc["q"].third)
+        net.settle([copies[2] for copies in sc["o"].second])
         sc["c"].line()
 
         def late():
@@ -1135,9 +1274,10 @@
             leave(t).start()
 
         sc["a"].forward()
-        for key in "qohcb":
+        for key in "qohc":
             sc[key].finish()
         sc["a"].line()
+        sc["b"].finish()
         for copy in crossing:
             copy.wait_recv()
         for n, key in enumerate((r.out_k, r.out_v)):

time: 217 us -> 202 us (0.931)
  Pallas kernels: 216 us -> 201 us
    pallas_call x1, Pallas kernels: 210 us -> 195 us  [run_kernel(): pl.pallas_call(lambda *refs: body(geometry, Refs(names, refs)), out_shape...]
where the time goes in v5:
time: 202 us
  Pallas kernels  201 us (100%)
    pallas_call x1, Pallas kernels, run_kernel(): pl.pallas_call(lambda *refs: body(geometry, Refs(names, refs)), out_shape...  195 us
    pallas_call x1, Pallas kernels, run_finish(): pl.pallas_call(lambda *refs: finish_kernel(Refs(names, refs)), out_shape=...  5.96 us

profile of v5, /device:TPU:0, one launch (start us, length us, event | category | flops | bytes accessed | tf_op | source)
XLA Modules:
  0.0 201.7 jit_solution(13034107171576595885)
XLA Ops:
  0.7 194.9 %shard_map.402 = (f32[128,80]{1,0:T(8,128)}, f32[8,768]{1,0:T(8,128)}, f32[8,128]{1,0:T(8,128)}, f32[8,128]{1,0:T(8,128)}, f32[256,128]{1,0:T(8,128)}, /*index=5...) custom-call(bf16[10,2048]{1,0:T(8,128)(2,1)} %refs_0_.1, ...), custom_call_target="tpu_custom_call" | custom-call | tf_op jit(solution)/shard_map/pallas_call | solution.py:1323
  195.6 6.0 %shard_map.403 = (f32[80,128]{1,0:T(8,128)}, f32[256,128]{1,0:T(8,128)}, f32[576,128]{1,0:T(8,128)}, f32[64,512]{1,0:T(8,128)}, f32[256,128]{1,0:T(8,128)}, /*in...) custom-call(f32[128,80]{1,0:T(8,128)} %get-tuple-element.51.refs_0_,, ...), custom_call_target="tpu_custom_call" | custom-call | tf_op jit(solution)/shard_map/pallas_call | solution.py:1529

commit v6 on v5

--- a/solution.py
+++ b/solution.py
@@ -648,6 +648,8 @@
         def _():
             halo(t, 1).start()
 
+    for gather in (q, o, h):
+        gather.line()
 
     def more_b():
         b.forward(1)
@@ -720,9 +722,8 @@
     spread(r.own2, [jnp.sum(acc[n, :, 0:d_mid], axis=0, keepdims=True) for n in range(2)])
     sums[1].start()
     net.settle(sums[0].sent() + asked + named + a.sent())
-    q.line()
-    o.line()
-    h.line()
+    for gather in (q, o, h):
+        gather.relay()
 
     @pl.loop(0, tiles)
     def _(t):
@@ -730,9 +731,14 @@
         r.low_t[0, :, at] = jnp.transpose(low_up[at, :].astype(F32)).astype(LOW)
         r.low_t[2, :, at] = jnp.transpose(low_down[at, :].astype(F32)).astype(LOW)
 
-    total = sums[1].finish()
+
+    def begin():
+        for gather in (q, o, h):
+            gather.batch(0)
+
+    total = sums[1].finish(begin)
     for gather in (q, o, h):
-        gather.relay()
+        gather.relay_last()
     centre, inverse = moments(total, d_mid, total_count)
     gain, bias = r.gain_b[...], r.bias_b[...]
     for n, value in enumerate((gain, bias, gain * inverse)):
@@ -777,7 +783,7 @@
 
         spread(r.own3, [jnp.sum(acc[n], axis=0, keepdims=True) for n in range(2)])
         for gather in (q, o, h):
-            gather.relay_last()
+            gather.batch(1)
         sums[2].start()
         net.settle(sums[1].sent() + b.sent())
         net.settle_some(b.some)
@@ -792,7 +798,8 @@
 
         def rest():
             for gather in (q, o, h):
-                gather.batch()
+                gather.batch(2)
+                gather.forward(0)
 
         total = sums[2].finish(rest)
         centre_wide, inverse_wide = moments(total, d_in, total_count)
@@ -810,7 +817,8 @@
         for copy in every:
             copy.start()
 
-        q.forward()
+        for gather in (q, o, h):
+            gather.forward(1)
         r.pieces[...] = jnp.zeros_like(r.pieces)
         tile = 128
 
@@ -830,8 +838,8 @@
 
 
     pl.run_scoped(third_norm, pltpu.VMEM((cells, d_in), F32))
-    o.forward()
-    h.forward()
+    for gather in (q, o, h):
+        gather.forward(2)
     r.blocks[...] = r.pieces[...].astype(LOW)
     pushed = [
         net.push(rows_of(r.blocks, peer[1], size), rows_of(r.arrived, place.s, size), peer)
@@ -1248,15 +1256,21 @@
         reload.wait()
         x = r.hat_c
 
-        @pl.loop(0, ranks)
-        def _(s):
+        def block_a(s):
             shard_a(s)[...] = jnp.dot(
                 d_at[...],
                 x[:, pl.ds(pl.multiple_of(s * depth, depth), depth)],
                 preferred_element_type=F32,
             ).astype(LOW)
 
-        sc["a"].pair()
+        for z in range(chips):
+            block_a(2 * z + place.other)
+            sc["a"].first[z].start()
+
+        @pl.loop(0, chips)
+        def _(z):
+            block_a(2 * z + place.core)
+
         sc["b"].line()
         sc["a"].batch()
         out_x = r.out_x

time: 202 us -> 196 us (0.970)
  Pallas kernels: 201 us -> 195 us
    pallas_call x1, Pallas kernels: 195 us -> 189 us  [run_kernel(): pl.pallas_call(lambda *refs: body(geometry, Refs(names, refs)), out_shape...]
where the time goes in v6:
time: 196 us
  Pallas kernels  195 us (99%)
    pallas_call x1, Pallas kernels, run_kernel(): pl.pallas_call(lambda *refs: body(geometry, Refs(names, refs)), out_shape...  189 us
    pallas_call x1, Pallas kernels, run_finish(): pl.pallas_call(lambda *refs: finish_kernel(Refs(names, refs)), out_shape=...  5.96 us

profile of v6, /device:TPU:0, one launch (start us, length us, event | category | flops | bytes accessed | tf_op | source)
XLA Modules:
  0.0 195.5 jit_solution(1945019449801322073)
XLA Ops:
  0.7 188.7 %shard_map.402 = (f32[128,80]{1,0:T(8,128)}, f32[8,768]{1,0:T(8,128)}, f32[8,128]{1,0:T(8,128)}, f32[8,128]{1,0:T(8,128)}, f32[256,128]{1,0:T(8,128)}, /*index=5...) custom-call(bf16[10,2048]{1,0:T(8,128)(2,1)} %refs_0_.1, ...), custom_call_target="tpu_custom_call" | custom-call | tf_op jit(solution)/shard_map/pallas_call | solution.py:1337
  189.4 6.0 %shard_map.403 = (f32[80,128]{1,0:T(8,128)}, f32[256,128]{1,0:T(8,128)}, f32[576,128]{1,0:T(8,128)}, f32[64,512]{1,0:T(8,128)}, f32[256,128]{1,0:T(8,128)}, /*in...) custom-call(f32[128,80]{1,0:T(8,128)} %get-tuple-element.51.refs_0_,, ...), custom_call_target="tpu_custom_call" | custom-call | tf_op jit(solution)/shard_map/pallas_call | solution.py:1543
